TPU v7x, 32 devices: a whole 2x2x4 slice. The times are simulated.
32 devices in a mesh: section: 2 (over core), dp: 16 (over z, y, x).
Axes of the slice: x: 2, y: 2, z: 4, core: 2. Of those that a mesh axis runs over, the one named last changes fastest.
Arguments:
- text: bfloat16 [8192, 768], P('dp'), may hold values from -6 to 6
- image: bfloat16 [128, 576, 768], P('dp', 'section'), may hold values from -6 to 6
- image_counts: int32 [128], P('dp'), may hold values from 196 to 576, as said below
- cotangent: bfloat16 [8192, 768], P('dp'), may hold values from -6 to 6
- attn_norm_gain: float32 [2, 768], P('section'), may hold values from 0.5 to 1.5
- attn_norm_bias: float32 [2, 768], P('section'), may hold values from -1.75 to 1.75
- qkv_weight: bfloat16 [2, 768, 2304], P('section'), may hold values from -0.21875 to 0.21875
- attn_out_weight: bfloat16 [2, 768, 768], P('section'), may hold values from -0.625 to 0.625
- mlp_norm_gain: float32 [2, 768], P('section'), may hold values from 0.5 to 1.5
- mlp_norm_bias: float32 [2, 768], P('section'), may hold values from -1.75 to 1.75
- up_weight: bfloat16 [2, 768, 3072], P('section'), may hold values from -0.21875 to 0.21875
- up_bias: float32 [2, 3072], P('section'), may hold values from -1.75 to 1.75
- down_weight: bfloat16 [2, 3072, 768], P('section'), may hold values from -0.109375 to 0.109375
- down_bias: float32 [2, 768], P('section'), may hold values from -1.75 to 1.75
- cross_norm_gain: float32 [2, 768], replicated, may hold values from 0.5 to 1.5
- cross_norm_bias: float32 [2, 768], replicated, may hold values from -1.75 to 1.75
- cross_query: bfloat16 [768, 768], replicated, may hold values from -0.21875 to 0.21875
- cross_key_value: bfloat16 [768, 1536], replicated, may hold values from -0.21875 to 0.21875
- cross_out: bfloat16 [768, 768], replicated, may hold values from -0.875 to 0.875
Outputs:
- layer_outputs: bfloat16 [2, 8192, 768], P('section', 'dp')
- input_grads: float32 [2, 8192, 768], P('section', 'dp')
- image_grad: float32 [128, 576, 768], P('dp', 'section')
- grad_attn_norm_gain: float32 [2, 768], P('section', 'dp')
- grad_attn_norm_bias: float32 [2, 768], P('section', 'dp')
- grad_qkv_weight: float32 [2, 768, 2304], P('section', 'dp')
- grad_attn_out_weight: float32 [2, 768, 768], P('section', 'dp')
- grad_mlp_norm_gain: float32 [2, 768], P('section', 'dp')
- grad_mlp_norm_bias: float32 [2, 768], P('section', 'dp')
- grad_up_weight: float32 [2, 768, 3072], P('section', 'dp')
- grad_up_bias: float32 [2, 3072], P('section', 'dp')
- grad_down_weight: float32 [2, 3072, 768], P('section', 'dp')
- grad_down_bias: float32 [2, 768], P('section', 'dp')
- grad_cross_norm_gain: float32 [2, 768], P(None, ('section', 'dp'))
- grad_cross_norm_bias: float32 [2, 768], P(None, ('section', 'dp'))
- grad_cross_query: float32 [768, 768], P(('section', 'dp'))
- grad_cross_key_value: float32 [768, 1536], P(('section', 'dp'))
- grad_cross_out: float32 [768, 768], P(('section', 'dp'))
Inputs may be any that keep to these rules, and one draw needn't show every extreme that they name: `image_counts`: each caption has 196 or 576 valid image tokens, the first ones of its row; the rest is padding.
All inputs are finite; a program needn't handle non-finite values.
Results may differ from a plain program's by a relative error of at most 0.02.
Values may be sent and summed in bfloat16 or wider, within the bound.
No kernel may reach another device: no remote copies, remote signals or barrier semaphores. Data moves between devices by JAX's collectives and lax.ppermute only.
A program may use at most 384 MiB of HBM per device.

v0:
```python
import jax
import jax.numpy as jnp
from jax import lax
from jax.sharding import PartitionSpec as P

HEADS = 12
HEAD_DIM = 64
SEQ = 64
MICRO = 2


eps = 1e-05
neg_large = -1e30
row_contract = (((0,), (0,)), ((), ()))
col_contract = (((1,), (1,)), ((), ()))


def shifted(value, axis, steps):
    count = lax.axis_size(axis)
    initial, last = (max(0, -steps), min(count, count - steps))
    return lax.ppermute(value, axis, [(source, source + steps) for source in range(initial, last)])


def layer_norm(stream, gain, bias):
    centred = stream - jnp.mean(stream, -1, keepdims=True)
    spread = jnp.mean(centred * centred, -1, keepdims=True)
    return centred * lax.rsqrt(spread + eps) * gain + bias


def product(left, right):
    return jnp.dot(left, right, preferred_element_type=jnp.float32)


def times_transposed(grad_rows, weight):
    return lax.dot_general(grad_rows, weight, col_contract, preferred_element_type=jnp.float32)


def outer_sum(inputs, grad_rows):
    return lax.dot_general(inputs, grad_rows, row_contract, preferred_element_type=jnp.float32)


def add_trees(left, right):
    return jax.tree.map(jnp.add, left, right)


def attend_forward(query, keys, values, key_mask):
    scores = jnp.einsum(
        "cqhd,ckhd->chqk", query, keys, preferred_element_type=jnp.float32
    ) * HEAD_DIM ** (-0.5)
    scores = jnp.where(key_mask, scores, neg_large)
    row_max = jnp.max(scores, -1, keepdims=True)
    powers = jnp.exp(scores - row_max)
    summed = jnp.sum(powers, -1, keepdims=True)
    attn_prob = (powers / summed).astype(jnp.bfloat16)
    mixed = jnp.einsum("chqk,ckhd->cqhd", attn_prob, values, preferred_element_type=jnp.float32)
    return (mixed, row_max + jnp.log(summed))


def attend_backward(query, keys, values, key_mask, log_total, grad_out):
    score_scale = HEAD_DIM ** (-0.5)
    scores = (
        jnp.einsum("cqhd,ckhd->chqk", query, keys, preferred_element_type=jnp.float32) * score_scale
    )
    scores = jnp.where(key_mask, scores, neg_large)
    attn_prob = jnp.exp(scores - log_total)
    grad_prob = jnp.einsum("cqhd,ckhd->chqk", grad_out, values, preferred_element_type=jnp.float32)
    centre = jnp.sum(attn_prob * grad_prob, -1, keepdims=True)
    grad_scores = (attn_prob * (grad_prob - centre)).astype(jnp.bfloat16)
    grad_query = (
        jnp.einsum("chqk,ckhd->cqhd", grad_scores, keys, preferred_element_type=jnp.float32)
        * score_scale
    )
    grad_keys = (
        jnp.einsum("chqk,cqhd->ckhd", grad_scores, query, preferred_element_type=jnp.float32)
        * score_scale
    )
    grad_values = jnp.einsum(
        "chqk,cqhd->ckhd",
        attn_prob.astype(jnp.bfloat16),
        grad_out,
        preferred_element_type=jnp.float32,
    )
    return (grad_query, grad_keys, grad_values)


def norm_backward(stream, gain, bias, grad_normed):
    unused, pullback = jax.vjp(layer_norm, stream, gain, bias)
    return pullback(grad_normed)


def self_forward(stream, gain, bias, w_qkv, w_out):
    caption_count = stream.shape[0] // SEQ
    normed = layer_norm(stream, gain, bias).astype(jnp.bfloat16)
    joined = (
        product(normed, w_qkv).astype(jnp.bfloat16).reshape(caption_count, SEQ, 3, HEADS, HEAD_DIM)
    )
    positions = jnp.arange(SEQ, dtype=jnp.int32)
    causal = (positions[:, None] >= positions[None, :])[None, None]
    query, keys, values = (joined[:, :, 0], joined[:, :, 1], joined[:, :, 2])
    mixed, log_total = attend_forward(query, keys, values, causal)
    attended = mixed.astype(jnp.bfloat16).reshape(stream.shape)
    return (
        product(attended, w_out),
        (stream, normed, query, keys, values, causal, log_total, attended),
    )


def self_backward(saved, grad_in, gain, bias, w_qkv, w_out):
    stream, normed, query, keys, values, causal, log_total, attended = saved
    grad_branch = grad_in.astype(jnp.bfloat16)
    grad_wout = outer_sum(attended, grad_branch)
    grad_att = times_transposed(grad_branch, w_out).astype(jnp.bfloat16).reshape(query.shape)
    grad_query, grad_keys, grad_values = attend_backward(
        query, keys, values, causal, log_total, grad_att
    )
    grad_joined = (
        jnp.stack([grad_query, grad_keys, grad_values], 2)
        .astype(jnp.bfloat16)
        .reshape(stream.shape[0], -1)
    )
    grad_wqkv = outer_sum(normed, grad_joined)
    grad_stream, grad_gain, grad_bias = norm_backward(
        stream, gain, bias, times_transposed(grad_joined, w_qkv)
    )
    return (grad_in + grad_stream, (grad_gain, grad_bias, grad_wqkv, grad_wout))


def mlp_forward(stream, gain, bias, w_up, b_up, w_down, b_down):
    normed = layer_norm(stream, gain, bias).astype(jnp.bfloat16)
    hidden = product(normed, w_up) + b_up
    activated = jax.nn.gelu(hidden).astype(jnp.bfloat16)
    return (product(activated, w_down) + b_down, (stream, normed, hidden, activated))


def mlp_backward(saved, grad_in, gain, bias, w_up, w_down):
    stream, normed, hidden, activated = saved
    grad_branch = grad_in.astype(jnp.bfloat16)
    grad_wdown = outer_sum(activated, grad_branch)
    grad_bdown = jnp.sum(grad_branch.astype(jnp.float32), 0)
    grad_act = times_transposed(grad_branch, w_down)
    unused, pullback = jax.vjp(jax.nn.gelu, hidden)
    grad_hidden = pullback(grad_act)[0].astype(jnp.bfloat16)
    grad_wup = outer_sum(normed, grad_hidden)
    grad_bup = jnp.sum(grad_hidden.astype(jnp.float32), 0)
    grad_stream, grad_gain, grad_bias = norm_backward(
        stream, gain, bias, times_transposed(grad_hidden, w_up)
    )
    return (
        grad_in + grad_stream,
        (grad_gain, grad_bias, grad_wup, grad_bup, grad_wdown, grad_bdown),
    )


def image_keys(image_rows, gain, bias, w_key_value):
    flat_rows = image_rows.reshape(-1, image_rows.shape[-1]).astype(jnp.float32)
    normed = layer_norm(flat_rows, gain, bias).astype(jnp.bfloat16)
    joined = product(normed, w_key_value).astype(jnp.bfloat16)
    return joined.reshape(image_rows.shape[0], image_rows.shape[1], 2, HEADS, HEAD_DIM)


def image_backward(image_rows, gain, bias, w_key_value, grad_kv):
    flat_rows = image_rows.reshape(-1, image_rows.shape[-1]).astype(jnp.float32)
    normed = layer_norm(flat_rows, gain, bias).astype(jnp.bfloat16)
    grad_rows = grad_kv.reshape(flat_rows.shape[0], -1)
    grad_wkv = outer_sum(normed, grad_rows)
    grad_image, grad_gain, grad_bias = norm_backward(
        flat_rows, gain, bias, times_transposed(grad_rows, w_key_value)
    )
    return (grad_image.reshape(image_rows.shape), grad_gain, grad_bias, grad_wkv)


def cross_forward(stream, keys_values, key_mask, gain, bias, w_query, w_out):
    normed = layer_norm(stream, gain, bias).astype(jnp.bfloat16)
    query = (
        product(normed, w_query)
        .astype(jnp.bfloat16)
        .reshape(keys_values.shape[0], -1, HEADS, HEAD_DIM)
    )
    mixed, log_total = attend_forward(query, keys_values[:, :, 0], keys_values[:, :, 1], key_mask)
    attended = mixed.astype(jnp.bfloat16).reshape(stream.shape)
    return (product(attended, w_out), (stream, normed, query, log_total, attended))


def cross_backward(saved, keys_values, key_mask, grad_in, gain, bias, w_query, w_out):
    stream, normed, query, log_total, attended = saved
    grad_branch = grad_in.astype(jnp.bfloat16)
    grad_wout = outer_sum(attended, grad_branch)
    grad_att = times_transposed(grad_branch, w_out).astype(jnp.bfloat16).reshape(query.shape)
    grad_query, grad_keys, grad_values = attend_backward(
        query, keys_values[:, :, 0], keys_values[:, :, 1], key_mask, log_total, grad_att
    )
    grad_kv = jnp.stack([grad_keys, grad_values], 2).astype(jnp.bfloat16)
    grad_q = grad_query.astype(jnp.bfloat16).reshape(stream.shape[0], -1)
    grad_wq = outer_sum(normed, grad_q)
    grad_stream, grad_gain, grad_bias = norm_backward(
        stream, gain, bias, times_transposed(grad_q, w_query)
    )
    return (grad_in + grad_stream, (grad_gain, grad_bias, grad_wq, grad_wout), grad_kv)


def first_forward(stream, layer_weights):
    g_one, b_one, w_qkv, w_out, g_two, b_two, w_up, b_up, w_down, b_down = layer_weights
    delta, unused = self_forward(stream, g_one, b_one, w_qkv, w_out)
    middle = stream + delta
    delta, unused = mlp_forward(middle, g_two, b_two, w_up, b_up, w_down, b_down)
    return middle + delta


def first_backward(stream, grad_in, layer_weights):
    g_one, b_one, w_qkv, w_out, g_two, b_two, w_up, b_up, w_down, b_down = layer_weights
    delta, self_saved = self_forward(stream, g_one, b_one, w_qkv, w_out)
    middle = stream + delta
    delta, mlp_saved = mlp_forward(middle, g_two, b_two, w_up, b_up, w_down, b_down)
    grad_in, mlp_grads = mlp_backward(mlp_saved, grad_in, g_two, b_two, w_up, w_down)
    grad_in, self_grads = self_backward(self_saved, grad_in, g_one, b_one, w_qkv, w_out)
    return (grad_in, self_grads + mlp_grads)


def second_pass(stream, keys_values, key_mask, grad_in, layer_weights, crossing):
    g_one, b_one, w_qkv, w_out, g_two, b_two, w_up, b_up, w_down, b_down = layer_weights
    gains, biases, w_query, w_key_value, w_cross = crossing
    delta, self_saved = self_forward(stream, g_one, b_one, w_qkv, w_out)
    second = stream + delta
    delta, cross_saved = cross_forward(
        second, keys_values, key_mask, gains[1], biases[1], w_query, w_cross
    )
    third = second + delta
    delta, mlp_saved = mlp_forward(third, g_two, b_two, w_up, b_up, w_down, b_down)
    final_out = third + delta
    grad_in, mlp_grads = mlp_backward(mlp_saved, grad_in, g_two, b_two, w_up, w_down)
    grad_in, cross_grads, grad_kv = cross_backward(
        cross_saved, keys_values, key_mask, grad_in, gains[1], biases[1], w_query, w_cross
    )
    grad_in, self_grads = self_backward(self_saved, grad_in, g_one, b_one, w_qkv, w_out)
    return (final_out, grad_in, self_grads + mlp_grads, cross_grads, grad_kv)


def on_device(
    text,
    image,
    image_counts,
    cotangent,
    attn_norm_gain,
    attn_norm_bias,
    qkv_weight,
    attn_out_weight,
    mlp_norm_gain,
    mlp_norm_bias,
    up_weight,
    up_bias,
    down_weight,
    down_bias,
    cross_norm_gain,
    cross_norm_bias,
    cross_query,
    cross_key_value,
    cross_out,
):
    section_index = lax.axis_index("section")
    layer_weights = (
        attn_norm_gain[0],
        attn_norm_bias[0],
        qkv_weight[0],
        attn_out_weight[0],
        mlp_norm_gain[0],
        mlp_norm_bias[0],
        up_weight[0],
        up_bias[0],
        down_weight[0],
        down_bias[0],
    )
    crossing = (cross_norm_gain, cross_norm_bias, cross_query, cross_key_value, cross_out)
    rows_all, model_width = text.shape
    captions_dev, half_patches = (image.shape[0], image.shape[1])
    per_micro = captions_dev // MICRO
    rows_micro = rows_all // MICRO
    patch_positions = jnp.arange(lax.axis_size("section") * half_patches, dtype=jnp.int32)
    layer_zero = tuple((jnp.zeros(weight.shape, jnp.float32) for weight in layer_weights))
    cross_zero = tuple((jnp.zeros(weight.shape, jnp.float32) for weight in crossing))
    act_zero = jnp.zeros((rows_micro, model_width), jnp.bfloat16)
    extra_zero = jnp.zeros((per_micro, half_patches, model_width), jnp.bfloat16)
    back_zero = jnp.zeros((per_micro, half_patches, model_width), jnp.float32)
    layer_acc, cross_acc = (layer_zero, cross_zero)
    buffers = {
        "outputs": jnp.zeros((rows_all, model_width), jnp.bfloat16),
        "in_grads": jnp.zeros((rows_all, model_width), jnp.float32),
        "image_grads": jnp.zeros(image.shape, jnp.float32),
    }
    incoming = (act_zero, extra_zero, act_zero, back_zero)
    for tick_now in range(MICRO + 2):

        def first_section(operand, tick_now=tick_now):
            buffers, incoming = operand
            buffers = dict(buffers)
            send_act, send_extra = (act_zero, extra_zero)
            layer_tick, cross_tick = (layer_zero, cross_zero)
            if tick_now < MICRO:
                row_span = slice(tick_now * rows_micro, (tick_now + 1) * rows_micro)
                cap_span = slice(tick_now * per_micro, (tick_now + 1) * per_micro)
                send_act = first_forward(text[row_span].astype(jnp.float32), layer_weights).astype(
                    jnp.bfloat16
                )
                buffers["outputs"] = buffers["outputs"].at[row_span].set(send_act)
            if tick_now >= 2:
                micro_index = tick_now - 2
                row_span = slice(micro_index * rows_micro, (micro_index + 1) * rows_micro)
                cap_span = slice(micro_index * per_micro, (micro_index + 1) * per_micro)
                grad_text, layer_tick = first_backward(
                    text[row_span].astype(jnp.float32),
                    incoming[2].astype(jnp.float32),
                    layer_weights,
                )
                buffers["in_grads"] = buffers["in_grads"].at[row_span].set(grad_text)
                buffers["image_grads"] = buffers["image_grads"].at[cap_span].set(incoming[3])
            return (buffers, (send_act, send_extra, act_zero, back_zero), layer_tick, cross_tick)

        def second_section(operand, tick_now=tick_now):
            buffers, incoming = operand
            buffers = dict(buffers)
            send_grad, send_back = (act_zero, back_zero)
            layer_tick, cross_tick = (layer_zero, cross_zero)
            if 1 <= tick_now <= MICRO:
                micro_index = tick_now - 1
                row_span = slice(micro_index * rows_micro, (micro_index + 1) * rows_micro)
                cap_span = slice(micro_index * per_micro, (micro_index + 1) * per_micro)
                own_image = image[cap_span]
                counts = image_counts[cap_span]
                key_mask = (patch_positions[None, :] < counts[:, None])[:, None, None, :]
                full_image = jnp.concatenate([incoming[1], own_image], 1)
                keys_values = image_keys(
                    full_image, cross_norm_gain[0], cross_norm_bias[0], cross_key_value
                )
                final_out, grad_in, layer_tick, text_cross, grad_kv = second_pass(
                    incoming[0].astype(jnp.float32),
                    keys_values,
                    key_mask,
                    cotangent[row_span].astype(jnp.float32),
                    layer_weights,
                    crossing,
                )
                buffers["outputs"] = (
                    buffers["outputs"].at[row_span].set(final_out.astype(jnp.bfloat16))
                )
                send_grad = grad_in.astype(jnp.bfloat16)
                buffers["in_grads"] = (
                    buffers["in_grads"].at[row_span].set(send_grad.astype(jnp.float32))
                )
                grad_image, grad_gain, grad_bias, grad_wkv = image_backward(
                    full_image, cross_norm_gain[0], cross_norm_bias[0], cross_key_value, grad_kv
                )
                send_back = grad_image[:, :half_patches]
                buffers["image_grads"] = (
                    buffers["image_grads"].at[cap_span].set(grad_image[:, half_patches:])
                )
                cross_tick = (
                    jnp.stack([grad_gain, text_cross[0]]),
                    jnp.stack([grad_bias, text_cross[1]]),
                    text_cross[2],
                    grad_wkv,
                    text_cross[3],
                )
            return (buffers, (act_zero, extra_zero, send_grad, send_back), layer_tick, cross_tick)

        buffers, outgoing, layer_tick, cross_tick = lax.cond(
            section_index == 0, first_section, second_section, (buffers, incoming)
        )
        arrived_act, arrived_extra, arrived_grad, arrived_back = incoming
        if tick_now < MICRO:
            image_part = image[tick_now * per_micro : (tick_now + 1) * per_micro]
            arrived_act, arrived_extra = shifted((outgoing[0], image_part), "section", 1)
        if 1 <= tick_now <= MICRO:
            arrived_grad = shifted(outgoing[2], "section", -1)
            arrived_back = shifted(outgoing[3].astype(jnp.bfloat16), "section", -1).astype(
                jnp.float32
            )
        incoming = (arrived_act, arrived_extra, arrived_grad, arrived_back)
        if tick_now >= 1:
            layer_acc = add_trees(layer_acc, layer_tick)
            cross_acc = add_trees(cross_acc, cross_tick)
    layer_acc = lax.psum_scatter(layer_acc, "dp", scatter_dimension=0, tiled=True)
    cross_acc = (
        lax.psum_scatter(cross_acc[0], ("section", "dp"), scatter_dimension=1, tiled=True),
        lax.psum_scatter(cross_acc[1], ("section", "dp"), scatter_dimension=1, tiled=True),
        lax.psum_scatter(cross_acc[2], ("section", "dp"), scatter_dimension=0, tiled=True),
        lax.psum_scatter(cross_acc[3], ("section", "dp"), scatter_dimension=0, tiled=True),
        lax.psum_scatter(cross_acc[4], ("section", "dp"), scatter_dimension=0, tiled=True),
    )
    return (
        (buffers["outputs"][None], buffers["in_grads"][None], buffers["image_grads"])
        + tuple((part[None] for part in layer_acc))
        + tuple(cross_acc)
    )


def solution(mesh):
    placed = (
        P("dp", None),
        P("dp", "section", None),
        P("dp"),
        P("dp", None),
        P("section", None),
        P("section", None),
        P("section", None, None),
        P("section", None, None),
        P("section", None),
        P("section", None),
        P("section", None, None),
        P("section", None),
        P("section", None, None),
        P("section", None),
        P(),
        P(),
        P(),
        P(),
        P(),
    )
    return jax.shard_map(
        on_device,
        mesh=mesh,
        in_specs=placed,
        out_specs=(
            P("section", "dp", None),
            P("section", "dp", None),
            P("dp", "section", None),
            P("section", "dp"),
            P("section", "dp"),
            P("section", "dp", None),
            P("section", "dp", None),
            P("section", "dp"),
            P("section", "dp"),
            P("section", "dp", None),
            P("section", "dp"),
            P("section", "dp", None),
            P("section", "dp"),
            P(None, ("section", "dp")),
            P(None, ("section", "dp")),
            P(("section", "dp"), None),
            P(("section", "dp"), None),
            P(("section", "dp"), None),
        ),
        check_vma=False,
    )
```

profile of v0, /device:TPU:0, one launch (start us, length us, event | category | flops | bytes accessed | tf_op | source)
XLA Modules:
  0.0 1580.8 jit_solution(14367425968442987112)
XLA Ops:
  7.3 4.1 fusion.360
  11.4 3.6 collective-permute-start.1
  15.1 34.7 %conditional.5 = (bf16[512,768]{1,0:T(8,128)(2,1)}, bf16[256,768]{1,0:T(8,128)(2,1)}) conditional(s32[]{:T(128)} %convert_element_type.564, () %tuple.104, (bf16[512,768]{1,0:T(8,128)(2,1)S(1)}, f32[1,768]{1,0:T(1,128)S(1)}, f32[1,768]{1,0:T(1,128)S(1)}, bf16[768,2304]{1,0:T(8,128)(2,1)}, bf16[768,768]{1,0:T(8,128)(2,1)S(1)}, ...), branch_computations={%region_0.0_spmd, %region_1.8_spmd} | conditional | flops 3689356800 | bytes 40305872 | solution.py:364
  18.0 4.2 convolution_convert_fusion
  26.2 3.7 fusion.338
  35.6 2.6 fusion.11
  40.3 7.6 fusion.13
  51.1 2.5 collective-permute-start.3
  53.6 62.6 %conditional.6 = (f32[8,288,768]{2,1,0:T(8,128)}, f32[512,768]{1,0:T(8,128)}, bf16[512,768]{1,0:T(8,128)(2,1)}, bf16[256,768]{1,0:T(8,128)(2,1)S(1)}, bf16[256,7...) conditional(s32[]{:T(128)} %convert_element_type.564, ...), branch_computations={%region_8.41_spmd, %region_41.48_spmd} | conditional | flops 30736519168 | bytes 754910208 | solution.py:364
  66.3 4.2 convolution_convert_fusion.9
  74.5 3.7 fusion.341
  84.0 2.6 fusion.130
  88.6 7.7 constant_dynamic-update-slice_fusion
  100.2 3.3 broadcast_in_dim.370
  103.5 3.6 broadcast_in_dim.364
  107.1 4.8 broadcast_in_dim.371
  111.9 4.1 broadcast_in_dim.373
  117.8 198.0 %collective-permute-start.2 = (bf16[256,768]{1,0:T(8,128)(2,1)S(1)}, bf16[256,768]{1,0:T(8,128)(2,1)S(1)}, u32[]{:S(2)}, u32[]{:S(2)}) collective-permute-start(bf16[256,768]{1,0:T(8,128)(2,1)S(1)} %get-tuple-element.764), channel_id=1, source_target_pairs={{0,16},{1,17},{2,18},{3,19},{4,20},{5,21},{6,22},{7,23},{8,24},{9,... | collective-permute-start | bytes 1179656 | tf_op jit(solution)/shard_map/ppermute | solution.py:21
  319.7 119.6 %conditional.7 = (bf16[256,768]{1,0:T(8,128)(2,1)}, bf16[4,288,768]{2,1,0:T(8,128)(2,1)}, f32[768,2304]{1,0:T(8,128)}, f32[768,768]{1,0:T(8,128)}, f32[768,3072]...) conditional(s32[]{:T(128)} %convert_element_type.564, ...), branch_computations={%region_48.75_spmd, %region_75.87_spmd} | conditional | flops 30732787712 | bytes 757900544
  338.9 3.1 convolution_convert_fusion.18
  343.4 3.6 reshape.1358
  350.8 2.5 copy.412
  358.1 2.5 reshape.1359
  368.0 4.4 fusion.361
  372.3 2.8 broadcast_in_dim.395
  375.1 6.5 fusion.326
  389.6 2.7 reshape.1418
  401.2 5.4 copy.327
  406.6 3.7 convert_element_type.539
  410.3 4.1 fusion.250
  416.1 2.6 add_add_fusion.13
  420.7 4.1 fusion.261
  424.7 7.1 fusion.234
  431.8 6.4 fusion.262
  439.4 3.4 add.885
  442.8 4.1 add.887
  446.9 6.9 add.886
  456.5 3.1 scatter.44
  459.6 4.0 constant_dynamic-update-slice_fusion.2
  463.7 164.4 %collective-permute-done.6 = bf16[4,288,768]{2,1,0:T(8,128)(2,1)} collective-permute-done((bf16[4,288,768]{2,1,0:T(8,128)(2,1)}, bf16[4,288,768]{2,1,0:T(8,128)(2,1)}, u32[]{:S(2)}, u32[]{:S(2)}) %collective-permute-start.6) | collective-permute-done | bytes 1769504 | tf_op jit(solution)/shard_map/ppermute | solution.py:21
  629.9 86.7 %conditional.8 = (f32[8,288,768]{2,1,0:T(8,128)}, f32[512,768]{1,0:T(8,128)}, f32[768]{0:T(1024)}, f32[768]{0:T(1024)}, f32[768,2304]{1,0:T(8,128)}, /*index=5*/...) conditional(s32[]{:T(128)} %convert_element_type.564, ...), branch_computations={%region_87.88_spmd, %region_88.106_spmd} | conditional | flops 9862638592 | bytes 197889120 | solution.py:364
  633.6 4.2 convolution_convert_fusion.22
  639.6 2.5 reshape.1361
  642.1 3.7 fusion.357
  653.4 2.5 reshape.1362
  657.9 4.2 fusion.368
  662.1 5.9 convert_reduce_fusion.9
  684.6 5.4 copy.346
  690.0 3.8 convert_element_type.555
  693.8 3.9 fusion.323
  701.1 4.2 fusion.315
  705.3 5.8 fusion.277
  711.2 5.2 fusion.319
  716.6 4.2 add_add_fusion.20
  720.9 11.4 add_add_fusion.19
  732.4 15.1 add_add_fusion.18
  747.6 14.2 add_add_fusion.17
  766.5 42.0 %all-reduce.11 = (f32[2,768]{1,0:T(2,128)S(1)}, f32[2,768]{1,0:T(2,128)S(1)}) all-reduce(f32[2,768]{1,0:T(2,128)S(1)} %add.883, f32[2,768]{1,0:T(2,128)S(1)} %add.884), channel_id=12, replica_groups=mesh['section'=2,'dp'=16] {'section','dp'}, use_global_device_ids=true, to_apply=%region_122.123.clone | all-reduce | flops 3072 | bytes 24576
  815.8 76.2 %all-reduce.12 = (f32[768]{0:T(1024)S(1)}, f32[768]{0:T(1024)S(1)}, f32[768]{0:T(1024)S(1)}, f32[768]{0:T(1024)S(1)}, f32[3072]{0:T(1024)S(1)}, /*index=5*/f32[768]{0:T(1024)S(1)}) all-reduce(f32[768]{0:T(1024)S(1)} %add_add_fusion.26, f32[768]{0:T(1024)S(1)} %get-tuple-element.992, ...), channel_id=2, replica_groups=mesh['section'=2,'dp'=16] {'dp'}, use_global_device_ids=true, to_apply=%region_107.108.clone | all-reduce | flops 6912 | bytes 55296
  895.5 35.5 %reduce-scatter.20.cloned.1.call-done = f32[24,1536]{1,0:T(8,128)} async-done(((f32[768,1536]{1,0:T(8,128)}), f32[24,1536]{1,0:T(8,128)}) %reduce-scatter.20.cloned.1.call-update) | async-done | bytes 147472 | tf_op jit(solution)/shard_map/reduce_scatter | solution.py:385
  931.0 133.4 %reduce-scatter.12.cloned.1.call-done = f32[48,768]{1,0:T(8,128)} async-done(((f32[768,768]{1,0:T(8,128)}), f32[48,768]{1,0:T(8,128)}) %reduce-scatter.12.cloned.1.call-update) | async-done | bytes 147472 | tf_op jit(solution)/shard_map/reduce_scatter | solution.py:380
  1064.4 156.2 %reduce-scatter.10.cloned.1.call-done = f32[48,2304]{1,0:T(8,128)} async-done(((f32[768,2304]{1,0:T(8,128)}), f32[48,2304]{1,0:T(8,128)}) %reduce-scatter.10.cloned.1.call-update) | async-done | bytes 442384 | tf_op jit(solution)/shard_map/reduce_scatter | solution.py:380
  1220.6 176.1 %reduce-scatter.14.cloned.1.call-done = f32[48,3072]{1,0:T(8,128)} async-done(((f32[768,3072]{1,0:T(8,128)}), f32[48,3072]{1,0:T(8,128)}) %reduce-scatter.14.cloned.1.call-update) | async-done | bytes 589840 | tf_op jit(solution)/shard_map/reduce_scatter | solution.py:380
  1396.7 176.8 %reduce-scatter.16.cloned.1.call-done = f32[192,768]{1,0:T(8,128)} async-done(((f32[3072,768]{1,0:T(8,128)}), f32[192,768]{1,0:T(8,128)}) %reduce-scatter.16.cloned.1.call-update) | async-done | bytes 589840 | tf_op jit(solution)/shard_map/reduce_scatter | solution.py:380
  (438 shorter events, 143.4 us)
Async XLA Ops:
  7.2 7.9 copy-start.137
  7.2 7.9 copy-start.135
  7.2 7.9 copy-start.132
  7.2 7.8 copy-start.129
  7.2 7.8 copy-start.147
  7.2 7.8 copy-start.3
  7.3 7.8 copy-start.2
  7.3 888.2 %reduce-scatter.18.cloned.1.call-start = ((), (), s32[]{:S(2)}) async-start(), calls=%async_computation.11 | async-start | bytes 2433024 | tf_op jit(solution)/shard_map/reduce_scatter | solution.py:384
  11.4 42.2 %collective-permute-start.1 = (bf16[4,288,768]{2,1,0:T(8,128)(2,1)}, bf16[4,288,768]{2,1,0:T(8,128)(2,1)}, u32[]{:S(2)}, u32[]{:S(2)}) collective-permute-start(bf16[4,288,768]{2,1,0:T(8,128)(2,1)} %get-tuple-element.988), channel_id=1, source_target_pairs={{0,16},{1,17},{2,18},{3,19},{4,20},{5,21},{6,22},{7,23},{8,24},{9,... | collective-permute-start | bytes 5308424 | tf_op jit(solution)/shard_map/ppermute | solution.py:21
  49.8 3.8 collective-permute-start
  51.1 266.0 %collective-permute-start.3 = (bf16[4,288,768]{2,1,0:T(8,128)(2,1)}, bf16[4,288,768]{2,1,0:T(8,128)(2,1)}, u32[]{:S(2)}, u32[]{:S(2)}) collective-permute-start(bf16[4,288,768]{2,1,0:T(8,128)(2,1)} %get-tuple-element.987), channel_id=1, source_target_pairs={{0,16},{1,17},{2,18},{3,19},{4,20},{5,21},{6,22},{7,23},{8,24},{9,... | collective-permute-start | bytes 5308424 | tf_op jit(solution)/shard_map/ppermute | solution.py:21
  116.2 203.4 %copy-start.43 = (f32[768,768]{1,0:T(8,128)}, f32[768,768]{1,0:T(8,128)S(1)}, u32[]{:S(2)}) copy-start(f32[768,768]{1,0:T(8,128)S(1)} %get-tuple-element.816) | copy-start | bytes 7077892
  116.2 203.4 %copy-start.45 = (f32[768,768]{1,0:T(8,128)}, f32[768,768]{1,0:T(8,128)S(1)}, u32[]{:S(2)}) copy-start(f32[768,768]{1,0:T(8,128)S(1)} %get-tuple-element.791) | copy-start | bytes 7077892
  116.2 203.4 %copy-start.85 = (f32[768,1536]{1,0:T(8,128)}, f32[768,1536]{1,0:T(8,128)S(1)}, u32[]{:S(2)}) copy-start(f32[768,1536]{1,0:T(8,128)S(1)} %get-tuple-element.818) | copy-start | bytes 14155780
  116.3 203.4 %copy-start.167 = (f32[768]{0:T(1024)}, f32[768]{0:T(1024)S(1)}, u32[]{:S(2)}) copy-start(f32[768]{0:T(1024)S(1)} %get-tuple-element.809) | copy-start | bytes 9220
  116.3 203.4 %copy-start.157 = (f32[2,768]{1,0:T(2,128)}, f32[2,768]{1,0:T(2,128)S(1)}, u32[]{:S(2)}) copy-start(f32[2,768]{1,0:T(2,128)S(1)} %get-tuple-element.814) | copy-start | bytes 18436
  116.3 203.4 %copy-start.160 = (f32[2,768]{1,0:T(2,128)}, f32[2,768]{1,0:T(2,128)S(1)}, u32[]{:S(2)}) copy-start(f32[2,768]{1,0:T(2,128)S(1)} %get-tuple-element.812) | copy-start | bytes 18436
  116.3 203.4 %copy-start.165 = (f32[768]{0:T(1024)}, f32[768]{0:T(1024)S(1)}, u32[]{:S(2)}) copy-start(f32[768]{0:T(1024)S(1)} %get-tuple-element.781) | copy-start | bytes 9220
  116.3 203.4 %copy-start.171 = (f32[3072]{0:T(1024)}, f32[3072]{0:T(1024)S(1)}, u32[]{:S(2)}) copy-start(f32[3072]{0:T(1024)S(1)} %get-tuple-element.803) | copy-start | bytes 36868
  116.3 203.4 %copy-start.185 = (f32[768]{0:T(1024)}, f32[768]{0:T(1024)S(1)}, u32[]{:S(2)}) copy-start(f32[768]{0:T(1024)S(1)} %get-tuple-element.794) | copy-start | bytes 9220
  116.3 203.4 %copy-start.187 = (f32[768]{0:T(1024)}, f32[768]{0:T(1024)S(1)}, u32[]{:S(2)}) copy-start(f32[768]{0:T(1024)S(1)} %get-tuple-element.798) | copy-start | bytes 9220
  116.3 203.4 %copy-start.189 = (f32[768]{0:T(1024)}, f32[768]{0:T(1024)S(1)}, u32[]{:S(2)}) copy-start(f32[768]{0:T(1024)S(1)} %get-tuple-element.786) | copy-start | bytes 9220
  116.3 203.2 %copy-start.148 = (f32[1,768]{1,0:T(1,128)S(1)}, f32[1,768]{1,0:T(1,128)}, u32[]{:S(2)}) copy-start(f32[1,768]{1,0:T(1,128)} %param.64) | copy-start | bytes 9220
  116.4 203.2 %copy-start.155 = (f32[2,768]{1,0:T(2,128)S(1)}, f32[2,768]{1,0:T(2,128)}, u32[]{:S(2)}) copy-start(f32[2,768]{1,0:T(2,128)} %param.65) | copy-start | bytes 18436
  116.4 203.2 %copy-start.156 = (f32[2,768]{1,0:T(2,128)S(1)}, f32[2,768]{1,0:T(2,128)}, u32[]{:S(2)}) copy-start(f32[2,768]{1,0:T(2,128)} %param.66) | copy-start | bytes 18436
  116.4 203.2 %copy-start.191 = (s32[8]{0:T(128)S(1)}, s32[8]{0:T(128)}, u32[]{:S(2)}) copy-start(s32[8]{0:T(128)} %param.53) | copy-start | bytes 100
  116.4 203.2 %copy-start.195 = (f32[1,3072]{1,0:T(1,128)S(1)}, f32[1,3072]{1,0:T(1,128)}, u32[]{:S(2)}) copy-start(f32[1,3072]{1,0:T(1,128)} %param.62) | copy-start | bytes 36868
  116.4 200.8 %collective-permute-start.5 = (bf16[4,288,768]{2,1,0:T(8,128)(2,1)S(1)}, bf16[4,288,768]{2,1,0:T(8,128)(2,1)S(1)}, u32[]{:S(2)}, u32[]{:S(2)}) collective-permute-start(bf16[4,288,768]{2,1,0:T(8,128)(2,1)S(1)} %get-tuple-element.769), channel_id=1, source_target_pairs={{16,0},{17,1},{18,2},{19,3},{20,4},{21,5},{22,6},{23,7},{24,8},{25... | collective-permute-start | bytes 5308424 | tf_op jit(solution)/shard_map/ppermute | solution.py:21
  117.8 199.3 %collective-permute-start.2 = (bf16[256,768]{1,0:T(8,128)(2,1)S(1)}, bf16[256,768]{1,0:T(8,128)(2,1)S(1)}, u32[]{:S(2)}, u32[]{:S(2)}) collective-permute-start(bf16[256,768]{1,0:T(8,128)(2,1)S(1)} %get-tuple-element.764), channel_id=1, source_target_pairs={{0,16},{1,17},{2,18},{3,19},{4,20},{5,21},{6,22},{7,23},{8,24},{9,... | collective-permute-start | bytes 1179656 | tf_op jit(solution)/shard_map/ppermute | solution.py:21
  315.8 3.7 collective-permute-start.4
  329.3 12.7 copy-start.199
  330.5 11.5 copy-start.153
  331.7 10.3 copy-start.173
  331.8 10.3 copy-start.163
  333.2 8.8 copy-start.143
  366.3 8.8 slice-start.16
  368.0 7.2 slice-start.17
  401.2 9.1 copy-start.154
  424.7 7.1 copy-start.121
  431.8 7.2 copy-start.44
  442.8 452.8 %reduce-scatter.22.cloned.1.call-start = ((), (), s32[]{:S(2)}) async-start(), calls=%async_computation.13 | async-start | bytes 2433024 | tf_op jit(solution)/shard_map/reduce_scatter | solution.py:386
  446.9 484.1 %reduce-scatter.20.cloned.1.call-start = ((), (), s32[]{:S(2)}) async-start(), calls=%async_computation.12 | async-start | bytes 4866048 | tf_op jit(solution)/shard_map/reduce_scatter | solution.py:385
  453.8 610.6 %reduce-scatter.12.cloned.1.call-start = ((), (), s32[]{:S(2)}) async-start(), calls=%async_computation.8 | async-start | bytes 2506752 | tf_op jit(solution)/shard_map/reduce_scatter | solution.py:380
  453.9 174.2 %collective-permute-start.6 = (bf16[4,288,768]{2,1,0:T(8,128)(2,1)}, bf16[4,288,768]{2,1,0:T(8,128)(2,1)}, u32[]{:S(2)}, u32[]{:S(2)}) collective-permute-start(bf16[4,288,768]{2,1,0:T(8,128)(2,1)} %get-tuple-element.777), channel_id=1, source_target_pairs={{16,0},{17,1},{18,2},{19,3},{20,4},{21,5},{22,6},{23,7},{24,8},{25... | collective-permute-start | bytes 5308424 | tf_op jit(solution)/shard_map/ppermute | solution.py:21
  455.2 174.7 %collective-permute-start.7 = (bf16[256,768]{1,0:T(8,128)(2,1)}, bf16[256,768]{1,0:T(8,128)(2,1)S(1)}, u32[]{:S(2)}, u32[]{:S(2)}) collective-permute-start(bf16[256,768]{1,0:T(8,128)(2,1)} %get-tuple-element.778), channel_id=1, source_target_pairs={{16,0},{17,1},{18,2},{19,3},{20,4},{21,5},{22,6},{23,7},{24,8},{25... | collective-permute-start | bytes 1179656 | tf_op jit(solution)/shard_map/ppermute | solution.py:21
  463.6 166.2 %copy-start.4 = (bf16[512,768]{1,0:T(8,128)(2,1)S(1)}, bf16[512,768]{1,0:T(8,128)(2,1)}, u32[]{:S(2)}) copy-start(bf16[512,768]{1,0:T(8,128)(2,1)} %param.51) | copy-start | bytes 2359300
  463.6 166.3 %copy-start.130 = (f32[1,768]{1,0:T(1,128)S(1)}, f32[1,768]{1,0:T(1,128)}, u32[]{:S(2)}) copy-start(f32[1,768]{1,0:T(1,128)} %param.55) | copy-start | bytes 9220
  463.6 166.3 %copy-start.133 = (f32[1,768]{1,0:T(1,128)S(1)}, f32[1,768]{1,0:T(1,128)}, u32[]{:S(2)}) copy-start(f32[1,768]{1,0:T(1,128)} %param.56) | copy-start | bytes 9220
  463.6 166.3 %copy-start.136 = (f32[1,768]{1,0:T(1,128)S(1)}, f32[1,768]{1,0:T(1,128)}, u32[]{:S(2)}) copy-start(f32[1,768]{1,0:T(1,128)} %param.59) | copy-start | bytes 9220
  463.7 166.3 %copy-start.138 = (f32[1,768]{1,0:T(1,128)S(1)}, f32[1,768]{1,0:T(1,128)}, u32[]{:S(2)}) copy-start(f32[1,768]{1,0:T(1,128)} %param.60) | copy-start | bytes 9220
  657.6 12.6 copy-start.37
  657.8 12.3 copy-start.169
  674.1 5.8 copy-start.125
  684.6 9.1 copy-start.150
  720.8 499.8 %reduce-scatter.10.cloned.1.call-start = ((), (), s32[]{:S(2)}) async-start(), calls=%async_computation.7 | async-start | bytes 7520256 | tf_op jit(solution)/shard_map/reduce_scatter | solution.py:380
  732.3 664.4 %reduce-scatter.14.cloned.1.call-start = ((), (), s32[]{:S(2)}) async-start(), calls=%async_computation.9 | async-start | bytes 10027008 | tf_op jit(solution)/shard_map/reduce_scatter | solution.py:380
  747.5 826.0 %reduce-scatter.16.cloned.1.call-start = ((), (), s32[]{:S(2)}) async-start(), calls=%async_computation.10 | async-start | bytes 10027008 | tf_op jit(solution)/shard_map/reduce_scatter | solution.py:380
  761.8 48.4 %copy-start.26 = (f32[256,768]{1,0:T(8,128)S(1)}, f32[256,768]{1,0:T(8,128)}, u32[]{:S(2)}) copy-start(f32[256,768]{1,0:T(8,128)} %get-tuple-element.782) | copy-start | bytes 2359300
  764.4 48.5 %copy-start.166 = (f32[768]{0:T(1024)S(1)}, f32[768]{0:T(1024)}, u32[]{:S(2)}) copy-start(f32[768]{0:T(1024)} %copy-done.165) | copy-start | bytes 9220
  764.4 49.2 %copy-start.168 = (f32[768]{0:T(1024)S(1)}, f32[768]{0:T(1024)}, u32[]{:S(2)}) copy-start(f32[768]{0:T(1024)} %copy-done.167) | copy-start | bytes 9220
  764.4 49.2 %copy-start.188 = (f32[768]{0:T(1024)S(1)}, f32[768]{0:T(1024)}, u32[]{:S(2)}) copy-start(f32[768]{0:T(1024)} %copy-done.187) | copy-start | bytes 9220
  764.4 49.9 %copy-start.186 = (f32[768]{0:T(1024)S(1)}, f32[768]{0:T(1024)}, u32[]{:S(2)}) copy-start(f32[768]{0:T(1024)} %copy-done.185) | copy-start | bytes 9220
  764.4 49.9 %copy-start.190 = (f32[768]{0:T(1024)S(1)}, f32[768]{0:T(1024)}, u32[]{:S(2)}) copy-start(f32[768]{0:T(1024)} %copy-done.189) | copy-start | bytes 9220
  764.4 50.6 %copy-start.172 = (f32[3072]{0:T(1024)S(1)}, f32[3072]{0:T(1024)}, u32[]{:S(2)}) copy-start(f32[3072]{0:T(1024)} %copy-done.171) | copy-start | bytes 36868
  (70 other events, 189.6 us)
Sparse Core Ops, SparseCore 0:
  442.9 270.5 reduce-scatter.17
  719.3 98.7 reduce-scatter.21
  824.1 106.8 reduce-scatter.19
  936.3 128.0 reduce-scatter.11
  1070.1 150.3 reduce-scatter.9
  1226.7 169.9 reduce-scatter.13
  1403.0 170.5 reduce-scatter.15
where the time goes:
time: 1590 us; the launch traced here: 1580 us
  waiting for transfers between devices  843 us (53%)
  starting transfers between devices  211 us (13%)
  local copies, waits for them, and re-layouts  139 us (9%)
  matrix products  126 us (8%)
  blocking collectives  118 us (7%)
  other arithmetic  106 us (7%)
  loops' own time  20.9 us (1%)
  between operations  16.5 us (1%)
    reduce_scatter x4, waiting for transfers between devices, on_device(): lax.psum_scatter(layer_acc, 'dp', scatter_dimension=0, tiled=True)  643 us
    ppermute x8, starting transfers between devices, shifted(): lax.ppermute(value, axis, [(source, source + steps) for source in range(i...  211 us
    ppermute x8, waiting for transfers between devices, shifted(): lax.ppermute(value, axis, [(source, source + steps) for source in range(i...  165 us
    unnamed x2, blocking collectives  118 us
    add x13, other arithmetic, add_trees(): return jax.tree.map(jnp.add, left, right)  62.1 us
    dot_general x12, matrix products, product(): return jnp.dot(left, right, preferred_element_type=jnp.float32)  47.8 us
    reduce_scatter x1, waiting for transfers between devices, on_device(): lax.psum_scatter(cross_acc[3], ('section', 'dp'), scatter_dimension=0, ti...  35.5 us
    dot_general x8, matrix products, outer_sum(): lax.dot_general(inputs, grad_rows, row_contract, preferred_element_type=j...  35.1 us
  transfers between devices with their start and end apart: 15, of which 7 were waited for; matrix products, arithmetic and copies ran while one was open for 16% of the time, Pallas kernels for 0%

commit v1 on v0

v1 whole, which is shorter than its diff:
```python
import jax
import jax.numpy as jnp
from jax import lax
from jax.experimental import pallas as pl
from jax.experimental.pallas import tpu as pltpu
from jax.sharding import PartitionSpec as P

HEAD_DIM = 64
SEQ = 64
LANES = 128
PAIR_ROWS = 2 * SEQ
CHUNK = 64
EPS = 1e-05
NEG = -1e30
SCALE = HEAD_DIM**-0.5
BF = jnp.bfloat16
F32 = jnp.float32


def nn(a, b):
    return lax.dot_general(a, b, (((1,), (0,)), ((), ())), preferred_element_type=F32)


def nt(a, b):
    return lax.dot_general(a, b, (((1,), (1,)), ((), ())), preferred_element_type=F32)


def tn(a, b):
    return lax.dot_general(a, b, (((0,), (0,)), ((), ())), preferred_element_type=F32)


def normalized(v):
    c = v - jnp.mean(v, -1, keepdims=True)
    inv = lax.rsqrt(jnp.mean(c * c, -1, keepdims=True) + EPS)
    return c * inv, inv


def norm(v, g, b):
    return normalized(v)[0] * g + b


def norm_grad(v, g, dh):
    nh, inv = normalized(v)
    e = dh * g
    dv = (e - jnp.mean(e, -1, keepdims=True) - nh * jnp.mean(e * nh, -1, keepdims=True)) * inv
    return dv, dh * nh


def fold(v):
    return jnp.sum(v.reshape(v.shape[0] // 8, 8, v.shape[1]), 0)


def gelu_pair(u):
    k = 0.7978845608028654
    t = jnp.tanh(k * (u + 0.044715 * u * u * u))
    g = 0.5 * u * (1.0 + t)
    dg = 0.5 * (1.0 + t) + 0.5 * u * (1.0 - t * t) * (k * (1.0 + 3 * 0.044715 * u * u))
    return g, dg


def gelu(u):
    k = 0.7978845608028654
    return 0.5 * u * (1.0 + jnp.tanh(k * (u + 0.044715 * u * u * u)))


def two_heads(v):
    low = lax.broadcasted_iota(jnp.int32, v.shape, 1) < HEAD_DIM
    zero = jnp.zeros_like(v)
    return jnp.concatenate([jnp.where(low, v, zero), jnp.where(low, zero, v)], 0)


def join_heads(v):
    half = v.shape[0] // 2
    low = lax.broadcasted_iota(jnp.int32, (half, LANES), 1) < HEAD_DIM
    return jnp.where(low, v[:half], v[half:])


def softmax(s):
    e = jnp.exp(s - jnp.max(s, -1, keepdims=True))
    return e / jnp.sum(e, -1, keepdims=True)


def self_probs(q2, k):
    s = nt(q2, k) * SCALE
    row = lax.broadcasted_iota(jnp.int32, s.shape, 0) % PAIR_ROWS
    col = lax.broadcasted_iota(jnp.int32, s.shape, 1)
    ok = (row // SEQ == col // SEQ) & (col <= row)
    return softmax(jnp.where(ok, s, NEG))


def cross_probs(q2, k, limits):
    s = nt(q2, k) * SCALE
    half = k.shape[0] // 2
    col = lax.broadcasted_iota(jnp.int32, s.shape, 1)
    bound = jnp.where(col < half, limits[0], limits[1] + half)
    return softmax(jnp.where(col < bound, s, NEG))


def attend_grad(q2, k, v, p, go):
    go2 = two_heads(go)
    dp = nt(go2, v)
    ds = (p * (dp - jnp.sum(p * dp, -1, keepdims=True))).astype(BF)
    dq = join_heads(nn(ds, k)) * SCALE
    dk = tn(ds, q2) * SCALE
    dv = tn(p.astype(BF), go2)
    return dq, dk, dv


def loop(count, body):
    def step(i, carry):
        body(i)
        return carry

    lax.fori_loop(0, count, step, 0)


def rows(i, size):
    return pl.ds(pl.multiple_of(i * size, size), size)


def lane(start, size):
    return pl.ds(pl.multiple_of(start, LANES), size)


def call(name, body, grid, scalars, ins, outs, scratch=(), flops=0):
    def spec(shape, item):
        block, index = item
        if block is None:
            block = shape
        if index is None:
            index = lambda *_, n=len(shape): (0,) * n
        return pl.BlockSpec(block, index)

    shapes = [jax.ShapeDtypeStruct(o[0], o[1]) for o in outs]
    moved = sum(a[0].size * a[0].dtype.itemsize for a in ins)
    moved += sum(s.size * s.dtype.itemsize for s in shapes)
    return pl.pallas_call(
        body,
        name=name,
        out_shape=shapes,
        grid_spec=pltpu.PrefetchScalarGridSpec(
            num_scalar_prefetch=len(scalars),
            grid=grid,
            in_specs=[spec(a[0].shape, a[1:]) for a in ins],
            out_specs=[spec(o[0], o[2:]) for o in outs],
            scratch_shapes=list(scratch),
        ),
        compiler_params=pltpu.CompilerParams(vmem_limit_bytes=56 << 20),
        cost_estimate=pl.CostEstimate(flops=int(flops), bytes_accessed=int(moved), transcendentals=0),
    )(*scalars, *[a[0] for a in ins])


def whole(a):
    return (a, None, None)


def out_whole(shape, dtype):
    return (shape, dtype, None, None)


class Half:
    def __init__(self, layer, own, got, width):
        self.layer, self.own, self.got, self.width = layer, own, got, width

    def cols(self, per, steps):
        layer, width = self.layer, self.width
        d = self.own.shape[0]

        def own_map(j, ids, *_):
            return (0, jnp.where(ids[0] == layer, per(j, ids[0]), 0))

        def got_map(j, ids, *_):
            return (0, jnp.where(ids[0] == layer, 0, j))

        return [(self.own, (d, width), own_map), (self.got, (d, width), got_map)]

    def rowblocks(self, per):
        layer, width = self.layer, self.width
        d = self.own.shape[1]

        def own_map(j, ids, *_):
            return (jnp.where(ids[0] == layer, per(j, ids[0]), 0), 0)

        def got_map(j, ids, *_):
            return (jnp.where(ids[0] == layer, 0, j), 0)

        return [(self.own, (width, d), own_map), (self.got, (width, d), got_map)]


def pick(ids, layer, own_ref, got_ref):
    return jnp.where(ids[0] == layer, own_ref[...], got_ref[...])


def self_fwd(layer, ids, stream, gain, bias, wqkv, wout):
    first = len(stream) == 1
    t, d = stream[0].shape
    h2 = d // 2
    n_in = len(stream)

    def body(ids_ref, *refs):
        xs, refs = refs[:n_in], refs[n_in:]
        g_ref, b_ref, own, got, o_own, o_got = refs[:6]
        outs = refs[6:]
        h_ref, qkv_ref, att_ref, part_ref, send_ref = outs[:5]
        j = pl.program_id(0)

        @pl.when(j == 0)
        def _():
            def chunk(i):
                sl = rows(i, CHUNK)
                if first:
                    x = xs[0][sl, :].astype(F32)
                else:
                    z = (xs[0][sl, :] + xs[1][sl, :] + xs[2][sl, :].astype(F32)).astype(BF)
                    outs[5][sl, :] = z
                    x = z.astype(F32)
                h_ref[sl, :] = norm(x, g_ref[...], b_ref[...]).astype(BF)

            loop(t // CHUNK, chunk)

        w = pick(ids_ref, layer, own, got)

        def project(i):
            sl = rows(i, 256)
            qkv_ref[j, sl, :] = nn(h_ref[sl, :], w).astype(BF)

        loop(t // 256, project)

        @pl.when(j == 2)
        def _():
            def block(i):
                sl = rows(i, PAIR_ROWS)
                for p in range(h2 // LANES):
                    ln = slice(p * LANES, (p + 1) * LANES)
                    k = qkv_ref[1, sl, ln]
                    probs = self_probs(two_heads(qkv_ref[0, sl, ln]), k).astype(BF)
                    att_ref[sl, ln] = join_heads(nn(probs, qkv_ref[2, sl, ln])).astype(BF)

            loop(t // PAIR_ROWS, block)
            wo = pick(ids_ref, layer, o_own, o_got)

            def finish(i):
                sl = rows(i, 256)
                part = nn(att_ref[sl, :], wo)
                part_ref[sl, :] = part
                send_ref[sl, :] = part.astype(BF)

            loop(t // 256, finish)

    outs = [
        out_whole((t, d), BF),
        out_whole((3, t, h2), BF),
        out_whole((t, h2), BF),
        out_whole((t, d), F32),
        out_whole((t, d), BF),
    ]
    if not first:
        outs.append(out_whole((t, d), BF))
    ins = [whole(x) for x in stream] + [whole(gain), whole(bias)]
    ins += wqkv.cols(lambda j, s: 2 * j + s, 3) + wout.rowblocks(lambda j, s: s)[:1]
    ins += [whole(wout.got)]
    return call(
        f"self_fwd_{layer}", body, (3,), [ids], ins, outs, flops=2 * t * d * 4 * h2 + 2e8
    )


def mlp_fwd(layer, ids, x, a_own, a_got, gain, bias, wup, b_up, wdown, b_down):
    t, d = x.shape
    fh = b_up.shape[1]
    width = wup.width

    def body(ids_ref, x_ref, p_ref, q_ref, g_ref, b_ref, u_own, u_got, bu_ref, d_own, d_got, bd_ref,
             x1_ref, n_ref, part_ref, send_ref):
        j = pl.program_id(0)

        @pl.when(j == 0)
        def _():
            def chunk(i):
                sl = rows(i, CHUNK)
                x1 = x_ref[sl, :].astype(F32) + p_ref[sl, :] + q_ref[sl, :].astype(F32)
                x1_ref[sl, :] = x1
                n_ref[sl, :] = norm(x1, g_ref[...], b_ref[...]).astype(BF)
                part_ref[sl, :] = jnp.broadcast_to(
                    jnp.where(ids_ref[0] == 0, bd_ref[...], 0.0), (CHUNK, d)
                )

            loop(t // CHUNK, chunk)

        up = pick(ids_ref, layer, u_own, u_got)
        down = pick(ids_ref, layer, d_own, d_got)

        def tile(i):
            sl = rows(i, 128)
            u = nn(n_ref[sl, :], up) + bu_ref[...]
            part_ref[sl, :] += nn(gelu(u).astype(BF), down)

        loop(t // 128, tile)

        @pl.when(j == pl.num_programs(0) - 1)
        def _():
            def chunk(i):
                sl = rows(i, CHUNK)
                send_ref[sl, :] = part_ref[sl, :].astype(BF)

            loop(t // CHUNK, chunk)

    per = fh // width
    ins = [whole(x), whole(a_own), whole(a_got), whole(gain), whole(bias)]
    ins += wup.cols(lambda j, s: s * per + j, per)
    ins += [(b_up, (1, width), lambda j, *_: (0, j))]
    ins += wdown.rowblocks(lambda j, s: s * per + j)
    ins += [whole(b_down)]
    outs = [
        out_whole((t, d), F32),
        out_whole((t, d), BF),
        out_whole((t, d), F32),
        out_whole((t, d), BF),
    ]
    return call(f"mlp_fwd_{layer}", body, (per,), [ids], ins, outs, flops=4 * t * d * fh)


def mlp_grad(layer, ids, lead, gain, bias, wup, b_up, wdown, b_down):
    second = layer == 1
    t, d = lead[0].shape
    fh = b_up.shape[1]
    width = wup.width
    n_in = len(lead)

    def body(ids_ref, *refs):
        lead_refs, refs = refs[:n_in], refs[n_in:]
        g_ref, b_ref, u_own, u_got, bu_ref, d_own, d_got, bd_ref = refs[:8]
        outs = refs[8:]
        act_ref, du_ref, dn_ref, dsend_ref, sums_ref, bup_ref = outs[:6]
        extra = outs[6:]
        j = pl.program_id(0)

        @pl.when(j == 0)
        def _():
            sums_ref[...] = jnp.zeros_like(sums_ref)

            def chunk(i):
                sl = rows(i, CHUNK)
                if second:
                    x_ref, p_ref, q_ref, cot_ref = lead_refs
                    x = x_ref[sl, :] + p_ref[sl, :] + q_ref[sl, :].astype(F32)
                    extra[0][sl, :] = x
                    extra[1][sl, :] = norm(x, g_ref[...], b_ref[...]).astype(BF)
                    extra[2][sl, :] = jnp.broadcast_to(
                        jnp.where(ids_ref[0] == 0, bd_ref[...], 0.0), (CHUNK, d)
                    )
                    sums_ref[2] += fold(cot_ref[sl, :].astype(F32))
                else:
                    grad_ref, p_ref, q_ref, z_ref, zg_ref, n_ref = lead_refs
                    dh = p_ref[sl, :] + q_ref[sl, :].astype(F32)
                    dv, dhn = norm_grad(z_ref[sl, :].astype(F32), zg_ref[...], dh)
                    dz = (grad_ref[sl, :] + dv).astype(BF)
                    extra[0][sl, :] = dz
                    sums_ref[0] += fold(dhn)
                    sums_ref[1] += fold(dh)
                    sums_ref[2] += fold(dz.astype(F32))
                dn_ref[sl, :] = jnp.zeros((CHUNK, d), F32)

            loop(t // CHUNK, chunk)

        up = pick(ids_ref, layer, u_own, u_got)
        down = pick(ids_ref, layer, d_own, d_got)
        bup_ref[...] = jnp.zeros_like(bup_ref)
        n_src = extra[1] if second else lead_refs[5]
        dm_src = lead_refs[3] if second else extra[0]

        def tile(i):
            sl = rows(i, 128)
            u = nn(n_src[sl, :], up) + bu_ref[...]
            g, dg = gelu_pair(u)
            g = g.astype(BF)
            act_ref[sl, :] = g
            du = (nt(dm_src[sl, :], down) * dg).astype(BF)
            du_ref[sl, :] = du
            bup_ref[...] += fold(du.astype(F32))
            dn_ref[sl, :] += nt(du, up)
            if second:
                extra[2][sl, :] += nn(g, down)

        loop(t // 128, tile)

        @pl.when(j == pl.num_programs(0) - 1)
        def _():
            def chunk(i):
                sl = rows(i, CHUNK)
                dsend_ref[sl, :] = dn_ref[sl, :].astype(BF)
                if second:
                    extra[3][sl, :] = extra[2][sl, :].astype(BF)

            loop(t // CHUNK, chunk)

    per = fh // width
    ins = [whole(a) for a in lead] + [whole(gain), whole(bias)]
    ins += wup.cols(lambda j, s: s * per + j, per)
    ins += [(b_up, (1, width), lambda j, *_: (0, j))]
    ins += wdown.rowblocks(lambda j, s: s * per + j)
    ins += [whole(b_down)]
    outs = [
        ((t, fh), BF, (t, width), lambda j, *_: (0, j)),
        ((t, fh), BF, (t, width), lambda j, *_: (0, j)),
        out_whole((t, d), F32),
        out_whole((t, d), BF),
        out_whole((3, 8, d), F32),
        ((8, fh), F32, (8, width), lambda j, *_: (0, j)),
    ]
    if second:
        outs += [
            out_whole((t, d), F32),
            out_whole((t, d), BF),
            out_whole((t, d), F32),
            out_whole((t, d), BF),
        ]
    else:
        outs += [out_whole((t, d), BF)]
    return call(
        f"mlp_grad_{layer}", body, (per,), [ids], ins, outs,
        flops=(8 if second else 6) * t * d * fh,
    )


def key_value(ids, image, gain, bias, w):
    caps, half, d = image.shape
    h2 = d // 2

    def body(ids_ref, im_ref, g_ref, b_ref, k_own, v_own, k_oth, v_oth, r_ref, own_ref, oth_ref):
        def chunk(i):
            sl = rows(i, 96)
            r_ref[0, sl, :] = norm(im_ref[0, sl, :].astype(F32), g_ref[...], b_ref[...]).astype(BF)

        loop(half // 96, chunk)
        r = r_ref[0]
        own_ref[0, :, :h2] = nn(r, k_own[...]).astype(BF)
        own_ref[0, :, h2:] = nn(r, v_own[...]).astype(BF)
        oth_ref[0, :, :h2] = nn(r, k_oth[...]).astype(BF)
        oth_ref[0, :, h2:] = nn(r, v_oth[...]).astype(BF)

    part = lambda off: (w, (d, h2), lambda c, ids: (0, off(ids[0])))
    blk = ((1, half, d), lambda c, *_: (c, 0, 0))
    ins = [(image,) + blk, whole(gain), whole(bias)]
    ins += [
        part(lambda s: s), part(lambda s: 2 + s), part(lambda s: 1 - s), part(lambda s: 3 - s)
    ]
    outs = [((caps, half, d), BF) + blk] * 3
    return call("key_value", body, (caps,), [ids], ins, outs, flops=4 * caps * half * d * d)


def key_value_grad(ids, image, gain, g_own, g_oth, w):
    caps, half, d = image.shape
    h2 = d // 2

    def body(ids_ref, im_ref, g_ref, own_ref, oth_ref, k_own, v_own, k_oth, v_oth, dx_ref, sums_ref):
        @pl.when(pl.program_id(0) == 0)
        def _():
            sums_ref[...] = jnp.zeros_like(sums_ref)

        def chunk(i):
            sl = rows(i, 96)
            dr = nt(own_ref[0, sl, :h2], k_own[...]) + nt(own_ref[0, sl, h2:], v_own[...])
            dr += nt(oth_ref[0, sl, :h2], k_oth[...]) + nt(oth_ref[0, sl, h2:], v_oth[...])
            dv, dhn = norm_grad(im_ref[0, sl, :].astype(F32), g_ref[...], dr)
            dx_ref[0, sl, :] = dv
            sums_ref[0] += fold(dhn)
            sums_ref[1] += fold(dr)

        loop(half // 96, chunk)

    part = lambda off: (w, (d, h2), lambda c, ids: (0, off(ids[0])))
    blk = ((1, half, d), lambda c, *_: (c, 0, 0))
    ins = [(image,) + blk, whole(gain), (g_own,) + blk, (g_oth,) + blk]
    ins += [
        part(lambda s: s), part(lambda s: 2 + s), part(lambda s: 1 - s), part(lambda s: 3 - s)
    ]
    outs = [((caps, half, d), F32) + blk, out_whole((2, 8, d), F32)]
    return call("key_value_grad", body, (caps,), [ids], ins, outs, flops=4 * caps * half * d * d)


def patch_limits(ids_ref, counts_ref, c, half):
    s = ids_ref[0]
    return counts_ref[c] - s * half, counts_ref[c] - (1 - s) * half


def cross_fwd(ids, counts, z, a_own, a_got, gain, bias, wq, wco, kv_own, kv_got):
    caps, half, d = kv_own.shape
    h2 = d // 2
    t = z.shape[0]

    def body(ids_ref, cnt_ref, z_ref, p_ref, q_ref, g_ref, b_ref, wq_ref, wo_ref, own_ref, got_ref,
             z2_ref, h_ref, cq_ref, att_ref, part_ref, send_ref):
        c = pl.program_id(0)

        @pl.when(c == 0)
        def _():
            def chunk(i):
                sl = rows(i, CHUNK)
                x = z_ref[sl, :].astype(F32) + p_ref[sl, :] + q_ref[sl, :].astype(F32)
                z2_ref[sl, :] = x
                h_ref[sl, :] = norm(x, g_ref[...], b_ref[...]).astype(BF)

            loop(t // CHUNK, chunk)

            def project(i):
                sl = rows(i, 256)
                cq_ref[sl, :] = nn(h_ref[sl, :], wq_ref[...]).astype(BF)

            loop(t // 256, project)

        limits = patch_limits(ids_ref, cnt_ref, c, half)
        sl = rows(c, SEQ)
        for p in range(h2 // LANES):
            ln = slice(p * LANES, (p + 1) * LANES)
            lv = slice(h2 + p * LANES, h2 + (p + 1) * LANES)
            k = jnp.concatenate([own_ref[0, :, ln], got_ref[0, :, ln]], 0)
            v = jnp.concatenate([own_ref[0, :, lv], got_ref[0, :, lv]], 0)
            probs = cross_probs(two_heads(cq_ref[sl, ln]), k, limits).astype(BF)
            att_ref[sl, ln] = join_heads(nn(probs, v)).astype(BF)

        @pl.when(c == pl.num_programs(0) - 1)
        def _():
            def finish(i):
                sl = rows(i, 256)
                part = nn(att_ref[sl, :], wo_ref[...])
                part_ref[sl, :] = part
                send_ref[sl, :] = part.astype(BF)

            loop(t // 256, finish)

    blk = ((1, half, d), lambda c, *_: (c, 0, 0))
    ins = [whole(z), whole(a_own), whole(a_got), whole(gain), whole(bias)]
    ins += [(wq, (d, h2), lambda c, ids, *_: (0, ids[0])), (wco, (h2, d), lambda c, ids, *_: (ids[0], 0))]
    ins += [(kv_own,) + blk, (kv_got,) + blk]
    outs = [
        out_whole((t, d), F32),
        out_whole((t, d), BF),
        out_whole((t, h2), BF),
        out_whole((t, h2), BF),
        out_whole((t, d), F32),
        out_whole((t, d), BF),
    ]
    return call(
        "cross_fwd", body, (caps,), [ids, counts], ins, outs, flops=4 * t * d * h2 + 16e8
    )


def cross_grad(ids, counts, grad, n_own, n_got, x3, gain3, cq, wq, wco, kv_own, kv_got):
    caps, half, d = kv_own.shape
    h2 = d // 2
    t = x3.shape[0]

    def body(ids_ref, cnt_ref, gr_ref, p_ref, q_ref, x_ref, g_ref, cq_ref, wq_ref, wo_ref, own_ref, got_ref,
             dz_ref, dc_ref, dcq_ref, down_ref, dgot_ref, dh_ref, dsend_ref, sums_ref, da_ref):
        c = pl.program_id(0)

        @pl.when(c == 0)
        def _():
            sums_ref[...] = jnp.zeros_like(sums_ref)

            def chunk(i):
                sl = rows(i, CHUNK)
                dh = p_ref[sl, :] + q_ref[sl, :].astype(F32)
                dv, dhn = norm_grad(x_ref[sl, :], g_ref[...], dh)
                dz = gr_ref[sl, :].astype(F32) + dv
                dz_ref[sl, :] = dz
                dc_ref[sl, :] = dz.astype(BF)
                sums_ref[0] += fold(dhn)
                sums_ref[1] += fold(dh)

            loop(t // CHUNK, chunk)

            def project(i):
                sl = rows(i, 256)
                da_ref[sl, :] = nt(dc_ref[sl, :], wo_ref[...]).astype(BF)

            loop(t // 256, project)

        limits = patch_limits(ids_ref, cnt_ref, c, half)
        sl = rows(c, SEQ)
        for p in range(h2 // LANES):
            ln = slice(p * LANES, (p + 1) * LANES)
            lv = slice(h2 + p * LANES, h2 + (p + 1) * LANES)
            k = jnp.concatenate([own_ref[0, :, ln], got_ref[0, :, ln]], 0)
            v = jnp.concatenate([own_ref[0, :, lv], got_ref[0, :, lv]], 0)
            q2 = two_heads(cq_ref[sl, ln])
            probs = cross_probs(q2, k, limits)
            dq, dk, dv = attend_grad(q2, k, v, probs, da_ref[sl, ln])
            dcq_ref[sl, ln] = dq.astype(BF)
            dk, dv = dk.astype(BF), dv.astype(BF)
            down_ref[0, :, ln] = dk[:half]
            dgot_ref[0, :, ln] = dk[half:]
            down_ref[0, :, lv] = dv[:half]
            dgot_ref[0, :, lv] = dv[half:]

        @pl.when(c == pl.num_programs(0) - 1)
        def _():
            def finish(i):
                sl = rows(i, 256)
                part = nt(dcq_ref[sl, :], wq_ref[...])
                dh_ref[sl, :] = part
                dsend_ref[sl, :] = part.astype(BF)

            loop(t // 256, finish)

    blk = ((1, half, d), lambda c, *_: (c, 0, 0))
    ins = [whole(grad), whole(n_own), whole(n_got), whole(x3), whole(gain3), whole(cq)]
    ins += [(wq, (d, h2), lambda c, ids, *_: (0, ids[0])), (wco, (h2, d), lambda c, ids, *_: (ids[0], 0))]
    ins += [(kv_own,) + blk, (kv_got,) + blk]
    outs = [
        out_whole((t, d), F32),
        out_whole((t, d), BF),
        out_whole((t, h2), BF),
        ((caps, half, d), BF) + blk,
        ((caps, half, d), BF) + blk,
        out_whole((t, d), F32),
        out_whole((t, d), BF),
        out_whole((2, 8, d), F32),
    ]
    return call(
        "cross_grad", body, (caps,), [ids, counts], ins, outs,
        scratch=[pltpu.VMEM((t, h2), BF)], flops=4 * t * d * h2 + 5e9,
    )


def self_grad(layer, ids, grad, h_own, h_got, x, gain_x, qkv, wqkv, wout):
    t, d = x.shape
    h2 = d // 2

    def body(ids_ref, gr_ref, p_ref, q_ref, x_ref, g_ref, qkv_ref, own, got, o_own, o_got,
             dz_ref, da_ref, dqkv_ref, dh_ref, dsend_ref, sums_ref, datt_ref):
        j = pl.program_id(0)

        @pl.when(j == 0)
        def _():
            sums_ref[...] = jnp.zeros_like(sums_ref)

            def chunk(i):
                sl = rows(i, CHUNK)
                dh = p_ref[sl, :] + q_ref[sl, :].astype(F32)
                dv, dhn = norm_grad(x_ref[sl, :].astype(F32), g_ref[...], dh)
                dz = gr_ref[sl, :].astype(F32) + dv
                dz_ref[sl, :] = dz
                da_ref[sl, :] = dz.astype(BF)
                sums_ref[0] += fold(dhn)
                sums_ref[1] += fold(dh)

            loop(t // CHUNK, chunk)
            wo = pick(ids_ref, layer, o_own, o_got)

            def project(i):
                sl = rows(i, 256)
                datt_ref[sl, :] = nt(da_ref[sl, :], wo).astype(BF)

            loop(t // 256, project)

            def block(i):
                sl = rows(i, PAIR_ROWS)
                for p in range(h2 // LANES):
                    ln = slice(p * LANES, (p + 1) * LANES)
                    k, v = qkv_ref[1, sl, ln], qkv_ref[2, sl, ln]
                    q2 = two_heads(qkv_ref[0, sl, ln])
                    dq, dk, dv = attend_grad(q2, k, v, self_probs(q2, k), datt_ref[sl, ln])
                    dqkv_ref[0, sl, ln] = dq.astype(BF)
                    dqkv_ref[1, sl, ln] = dk.astype(BF)
                    dqkv_ref[2, sl, ln] = dv.astype(BF)

            loop(t // PAIR_ROWS, block)

        w = pick(ids_ref, layer, own, got)

        def back(i):
            sl = rows(i, 256)
            part = nt(dqkv_ref[j, sl, :], w)

            @pl.when(j == 0)
            def _():
                dh_ref[sl, :] = part

            @pl.when(j > 0)
            def _():
                total = dh_ref[sl, :] + part
                dh_ref[sl, :] = total
                dsend_ref[sl, :] = total.astype(BF)

        loop(t // 256, back)

    ins = [whole(grad), whole(h_own), whole(h_got), whole(x), whole(gain_x), whole(qkv)]
    ins += wqkv.cols(lambda j, s: 2 * j + s, 3) + wout.rowblocks(lambda j, s: s)[:1]
    ins += [whole(wout.got)]
    outs = [
        out_whole((t, d), F32),
        out_whole((t, d), BF),
        out_whole((3, t, h2), BF),
        out_whole((t, d), F32),
        out_whole((t, d), BF),
        out_whole((2, 8, d), F32),
    ]
    return call(
        f"self_grad_{layer}", body, (3,), [ids], ins, outs,
        scratch=[pltpu.VMEM((t, h2), BF)], flops=2 * t * d * 4 * h2 + 5e8,
    )


def text_grad(grad, h_own, h_got, x, gain):
    t, d = x.shape

    def body(gr_ref, p_ref, q_ref, x_ref, g_ref, dx_ref, sums_ref):
        sums_ref[...] = jnp.zeros_like(sums_ref)

        def chunk(i):
            sl = rows(i, CHUNK)
            dh = p_ref[sl, :] + q_ref[sl, :].astype(F32)
            dv, dhn = norm_grad(x_ref[sl, :].astype(F32), g_ref[...], dh)
            dx_ref[sl, :] = gr_ref[sl, :] + dv
            sums_ref[0] += fold(dhn)
            sums_ref[1] += fold(dh)

        loop(t // CHUNK, chunk)

    ins = [whole(a) for a in (grad, h_own, h_got, x, gain)]
    outs = [out_whole((t, d), F32), out_whole((2, 8, d), F32)]
    return call("text_grad", body, (1,), [], ins, outs)


def orders(count):
    bits = [1 << i for i in range(count.bit_length() - 1)]
    third = [bits[2], bits[0], bits[1]] + bits[3:]
    return [bits, [bits[1], bits[0]] + bits[2:], third]


def pieces(order, count):
    result, left = [], list(range(count))
    rank = lambda r: [0 if r & b else 1 for b in order]
    for bit in order:
        result.append(sorted([r for r in left if r & bit], key=rank))
        left = [r for r in left if not r & bit]
    return result + [left]


def halving(parts, order, sent=BF):
    count = lax.axis_size("dp")
    for step, bit in enumerate(order):
        arrived = lax.ppermute(parts[step].astype(sent), "dp", [(i, i ^ bit) for i in range(count)])
        at = 0
        for later in range(step + 1, len(parts)):
            size = parts[later].shape[0]
            parts[later] = parts[later].astype(F32) + arrived[at : at + size].astype(F32)
            at += size
    return parts[-1][0].astype(F32)


def weight_kernel(name, ids, ins, row_count, count, fill, flops):
    cols = 3 * LANES
    plan = [pieces(o, count) for o in orders(count)]
    flat = [(k, piece) for k in range(3) for piece in plan[k]]

    def body(ids_ref, *refs):
        scr = refs[-1]
        me = ids_ref[1]

        def put(dest, first, block):
            scr[dest ^ me, pl.ds(first, block.shape[0]), :] = block

        fill(ids_ref, refs[: len(ins)], put)
        for out, (k, piece) in zip(refs[len(ins) : -1], flat):
            for at, rel in enumerate(piece):
                out[at] = scr[rel, :, k * LANES : (k + 1) * LANES].astype(BF)

    outs = [out_whole((len(piece), row_count, LANES), BF) for _, piece in flat]
    got = call(
        name, body, (1,), [ids], [whole(a) for a in ins], outs,
        scratch=[pltpu.VMEM((count, row_count, cols), F32)], flops=flops,
    )
    step = len(plan[0])
    return [got[i * step : (i + 1) * step] for i in range(3)]


def reduced(parts, count):
    sums = [halving(list(p), o) for p, o in zip(parts, orders(count))]
    return jnp.concatenate(sums, -1)


def up_down_weights(layer, ids, normed, du, act_own, act_got, dm, count):
    t, d = normed.shape
    fh = du.shape[1]
    h2 = d // 2
    up_rows, down_rows = d // count, 2 * fh // count
    units = fh // h2
    half_dest = count // 2

    def fill(ids_ref, refs, put):
        n_ref, du_ref, own_ref, got_ref, dm_ref = refs

        def up(j):
            w = tn(n_ref[...], du_ref[:, lane(j * h2, h2)])
            for dest in range(count):
                put(dest, pl.multiple_of(j * up_rows, up_rows), w[dest * up_rows : (dest + 1) * up_rows])

        loop(units, up)
        base = units * up_rows
        s = ids_ref[0]
        dm_half = dm_ref[:, lane(s * h2, h2)]
        per = h2 // down_rows

        def down(j):
            for ref, side in ((own_ref, s), (got_ref, 1 - s)):
                w = tn(ref[:, lane(j * h2, h2)], dm_half)
                for i in range(per):
                    put(side * half_dest + j * per + i, base, w[i * down_rows : (i + 1) * down_rows])

        loop(fh // h2, down)

    return weight_kernel(
        f"mlp_weights_{layer}", ids, [normed, du, act_own, act_got, dm],
        units * up_rows + down_rows, count, fill, 4 * t * d * fh,
    )


def self_weights(layer, ids, h, dqkv, att_own, att_got, da, count):
    t, d = h.shape
    h2 = d // 2
    each = d // count
    half_dest = count // 2

    def fill(ids_ref, refs, put):
        h_ref, dqkv_ref, own_ref, got_ref, da_ref = refs

        def one(j):
            w = tn(h_ref[...], dqkv_ref[j])
            for dest in range(count):
                put(dest, pl.multiple_of(j * each, each), w[dest * each : (dest + 1) * each])

        loop(3, one)
        s = ids_ref[0]
        da_half = da_ref[:, lane(s * h2, h2)]
        for ref, side in ((own_ref, s), (got_ref, 1 - s)):
            w = tn(ref[...], da_half)
            for i in range(half_dest):
                put(side * half_dest + i, 3 * each, w[i * each : (i + 1) * each])

    return weight_kernel(
        f"self_weights_{layer}", ids, [h, dqkv, att_own, att_got, da], 4 * each, count, fill,
        8 * t * d * h2,
    )


def cross_weights(ids, h, dcq, att_own, att_got, dc, count):
    t, d = h.shape
    h2 = d // 2
    each = h2 // count

    def fill(ids_ref, refs, put):
        h_ref, dcq_ref, own_ref, got_ref, dc_ref = refs
        w = tn(h_ref[...], dcq_ref[...])
        for half in range(2):
            for dest in range(count):
                at = half * h2 + dest * each
                put(dest, half * each, w[at : at + each])
        s = ids_ref[0]
        dc_half = dc_ref[:, lane(s * h2, h2)]
        for ref, side in ((own_ref, s), (got_ref, 1 - s)):
            w = tn(ref[...], dc_half)
            for dest in range(count):
                put(dest, pl.multiple_of((2 + side) * each, each), w[dest * each : (dest + 1) * each])

    return weight_kernel(
        "cross_weights", ids, [h, dcq, att_own, att_got, dc], 4 * each, count, fill, 4 * t * d * h2
    )


def key_value_weights(ids, r_own, r_got, g_own, g_got, count):
    caps, half, d = r_own.shape
    h2 = d // 2
    each = h2 // count
    cols = 3 * LANES
    plan = [pieces(o, count) for o in orders(count)]
    flat = [(k, piece) for k in range(3) for piece in plan[k]]

    def body(ids_ref, ro, rg, go, gg, *refs):
        outs, scr, acc = refs[:-2], refs[-2], refs[-1]
        c = pl.program_id(0)
        me = ids_ref[1]

        @pl.when(c == 0)
        def _():
            acc[...] = jnp.zeros_like(acc)

        def add(i):
            sl = rows(i, 256)
            acc[sl, :] += tn(ro[0, :, lane(i * 256, 256)], go[0]) + tn(rg[0, :, lane(i * 256, 256)], gg[0])

        loop(d // 256, add)

        @pl.when(c == pl.num_programs(0) - 1)
        def _():
            for kind in range(2):
                for part in range(2):
                    for dest in range(count):
                        at = part * h2 + dest * each
                        first = (2 * kind + part) * each
                        scr[dest ^ me, first : first + each, :] = acc[
                            at : at + each, kind * h2 : (kind + 1) * h2
                        ]
            for out, (k, piece) in zip(outs, flat):
                for at, rel in enumerate(piece):
                    out[at] = scr[rel, :, k * LANES : (k + 1) * LANES].astype(BF)

    blk = ((1, half, d), lambda c, *_: (c, 0, 0))
    ins = [(a,) + blk for a in (r_own, r_got, g_own, g_got)]
    outs = [out_whole((len(piece), 4 * each, LANES), BF) for _, piece in flat]
    got = call(
        "key_value_weights", body, (caps,), [ids], ins, outs,
        scratch=[pltpu.VMEM((count, 4 * each, cols), F32), pltpu.VMEM((d, d), F32)],
        flops=4 * caps * half * d * d,
    )
    step = len(plan[0])
    return [got[i * step : (i + 1) * step] for i in range(3)]


def plain_sums(s, count, mlp2, cross, attn2, mlp1, image, attn1):
    scatter = lambda g: lax.psum_scatter(g, "dp", scatter_dimension=0, tiled=True)

    def full(act):
        come = swap(act)
        return jnp.concatenate([jnp.where(s == 0, act, come), jnp.where(s == 0, come, act)], 1)

    def side(grad):
        h2 = grad.shape[1] // 2
        return lax.dynamic_slice(grad, (0, s * h2), (grad.shape[0], h2))

    def stacked(w, h2):
        return jnp.concatenate([w[:, i : i + h2] for i in range(0, w.shape[1], h2)], 0)

    def by_section(w):
        parts = w.reshape(2, count, -1, w.shape[1]).swapaxes(0, 1)
        return scatter(parts.reshape(w.shape))

    def mlp(n, du, act, dm):
        return jnp.concatenate(
            [stacked(scatter(tn(n, du)), n.shape[1] // 2), scatter(tn(full(act), side(dm)))], 0
        )

    def attn(h, dqkv, att, da):
        return jnp.concatenate(
            [scatter(tn(h, dqkv[j])) for j in range(3)] + [scatter(tn(full(att), side(da)))], 0
        )

    h, dcq, att, dc = cross
    r_own, r_got, g_own, g_got = [x.reshape(-1, x.shape[-1]) for x in image]
    w_kv = tn(r_own, g_own) + tn(r_got, g_got)
    h2 = dcq.shape[1]
    c = jnp.concatenate([by_section(tn(h, dcq)), by_section(tn(full(att), side(dc)))], 0)
    kv = jnp.concatenate([by_section(w_kv[:, :h2]), by_section(w_kv[:, h2:])], 0)
    return mlp(*mlp2), c, attn(*attn2), mlp(*mlp1), kv, attn(*attn1)


def swap(value):
    return lax.ppermute(value, "section", [(0, 1), (1, 0)])


def on_device(
    text, image, image_counts, cotangent,
    attn_norm_gain, attn_norm_bias, qkv_weight, attn_out_weight, mlp_norm_gain, mlp_norm_bias,
    up_weight, up_bias, down_weight, down_bias,
    cross_norm_gain, cross_norm_bias, cross_query, cross_key_value, cross_out,
):
    s = lax.axis_index("section")
    me = lax.axis_index("dp")
    count = lax.axis_size("dp")
    ids = jnp.stack([s, me]).astype(jnp.int32)
    t, d = text.shape
    h2 = d // 2
    caps, half = image.shape[:2]
    ff = up_bias.shape[1]
    fh = ff // 2
    other = 1 - s

    w_qkv, w_out, w_up, w_down = qkv_weight[0], attn_out_weight[0], up_weight[0], down_weight[0]
    vec_own = jnp.concatenate(
        [attn_norm_gain, attn_norm_bias, mlp_norm_gain, mlp_norm_bias, down_bias, up_bias], 1
    )
    vec_got = swap(vec_own)
    got_qkv = swap(
        jnp.concatenate(
            [lax.dynamic_slice(w_qkv, (0, (2 * j + other) * h2), (d, h2)) for j in range(3)], 1
        )
    )
    got_out = swap(lax.dynamic_slice(w_out, (other * h2, 0), (h2, d)))
    got_up = swap(lax.dynamic_slice(w_up, (0, other * fh), (d, fh)))
    got_down = swap(lax.dynamic_slice(w_down, (other * fh, 0), (fh, d)))

    vectors = []
    for layer in range(2):
        v = jnp.where(s == layer, vec_own, vec_got)
        parts = [v[:, i * d : (i + 1) * d] for i in range(5)]
        parts.append(lax.dynamic_slice(v, (0, 5 * d + s * fh), (1, fh)))
        vectors.append(parts)
    halves = []
    for layer in range(2):
        halves.append(
            (
                Half(layer, w_qkv, got_qkv, h2),
                Half(layer, w_out, got_out, h2),
                Half(layer, w_up, got_up, h2),
                Half(layer, w_down, got_down, h2),
            )
        )
    gain_i, gain_t = cross_norm_gain[0:1], cross_norm_gain[1:2]
    bias_i, bias_t = cross_norm_bias[0:1], cross_norm_bias[1:2]

    r_own, kv_own, kv_send = key_value(ids, image, gain_i, bias_i, cross_key_value)
    kv_got = swap(kv_send)
    r_got = swap(r_own)

    ag1, ab1, mg1, mb1, bd1, bu1 = vectors[0]
    qw1, ow1, uw1, dw1 = halves[0]
    ag2, ab2, mg2, mb2, bd2, bu2 = vectors[1]
    qw2, ow2, uw2, dw2 = halves[1]

    h1, qkv1, att1, part, send = self_fwd(0, ids, [text], ag1, ab1, qw1, ow1)
    x1, n1, part, send = mlp_fwd(0, ids, text, part, swap(send), mg1, mb1, uw1, bu1, dw1, bd1)
    h2n, qkv2, att2, part, send, z = self_fwd(1, ids, [x1, part, swap(send)], ag2, ab2, qw2, ow2)
    z2, ch, cq, catt, part, send = cross_fwd(
        ids, image_counts, z, part, swap(send), gain_t, bias_t, cross_query, cross_out, kv_own, kv_got
    )
    (act2, du2, dpart, dsend, sums_m2, bup2, z3, n2, mpart, msend) = mlp_grad(
        1, ids, [z2, part, swap(send), cotangent], mg2, mb2, uw2, bu2, dw2, bd2
    )
    y = z3 + mpart + swap(msend).astype(F32)
    layer_out = jnp.where(s == 0, z, y.astype(BF))

    (dz3, dc, dcq, dkv_own, dkv_send, cpart, csend, sums_n2) = cross_grad(
        ids, image_counts, cotangent, dpart, swap(dsend), z3, mg2, cq, cross_query, cross_out, kv_own, kv_got
    )
    dz2, da2, dqkv2, hpart, hsend, sums_c = self_grad(
        1, ids, dz3, cpart, swap(csend), z2, gain_t, qkv2, qw2, ow2
    )
    act1, du1, npart, nsend, sums_a2, bup1, dz = mlp_grad(
        0, ids, [dz2, hpart, swap(hsend), z, ag2, n1], mg1, mb1, uw1, bu1, dw1, bd1
    )
    dx1, da1, dqkv1, hpart, hsend, sums_n1 = self_grad(
        0, ids, dz, npart, swap(nsend), x1, mg1, qkv1, qw1, ow1
    )
    dtext, sums_a1 = text_grad(dx1, hpart, swap(hsend), text, ag1)

    dkv_mine = swap(dkv_send)
    image_grad, sums_i = key_value_grad(ids, image, gain_i, dkv_own, dkv_mine, cross_key_value)
    input_grad = jnp.where(s == 0, dtext, dz.astype(F32))

    if d // count == 48:
        m2 = reduced(up_down_weights(1, ids, n2, du2, act2, swap(act2), cotangent, count), count)
        c2 = reduced(cross_weights(ids, ch, dcq, catt, swap(catt), dc, count), count)
        a2 = reduced(self_weights(1, ids, h2n, dqkv2, att2, swap(att2), da2, count), count)
        m1 = reduced(up_down_weights(0, ids, n1, du1, act1, swap(act1), dz, count), count)
        kv = reduced(key_value_weights(ids, r_own, r_got, dkv_own, dkv_send, count), count)
        a1 = reduced(self_weights(0, ids, h1, dqkv1, att1, swap(att1), da1, count), count)
    else:
        m2, c2, a2, m1, kv, a1 = plain_sums(
            s, count, (n2, du2, act2, cotangent), (ch, dcq, catt, dc), (h2n, dqkv2, att2, da2),
            (n1, du1, act1, dz), (r_own, r_got, dkv_own, dkv_send), (h1, dqkv1, att1, da1),
        )

    each = d // count
    small = each // 2
    first = jnp.concatenate([m1, a1], 0)
    second = jnp.concatenate([m2, a2], 0)
    mine = jnp.where(s == 0, first, second)
    theirs = swap(jnp.where(s == 0, second, first))
    left = jnp.where(s == 0, mine, theirs)
    right = jnp.where(s == 0, theirs, mine)
    units = fh // h2
    both = lambda a, b: jnp.concatenate([left[a:b], right[a:b]], 1)

    def columns(start, number):
        return [x[start + i * each : start + (i + 1) * each] for x in (left, right) for i in range(number)]

    g_up = jnp.concatenate(columns(0, units), 1)
    at = units * each
    wide = ff // count
    g_down = both(at, at + wide)
    at += wide
    g_qkv = jnp.concatenate(
        [x[at + i * each : at + (i + 1) * each] for i in range(3) for x in (left, right)], 1
    )
    g_out = both(at + 3 * each, at + 4 * each)

    cross = jnp.concatenate([c2, kv], 0).reshape(4, 2, small, h2)
    keep = lax.dynamic_index_in_dim(cross, s, 1, False)
    come = swap(lax.dynamic_index_in_dim(cross, other, 1, False))
    cross = jnp.concatenate(
        [jnp.where(s == 0, keep, come), jnp.where(s == 0, come, keep)], 2
    )
    g_cq, g_co = cross[0], cross[1]
    g_kv = jnp.concatenate([cross[2], cross[3]], 1)

    bup = [jnp.sum(b, 0) for b in (bup1, bup2)]
    bup_mine = jnp.where(s == 0, bup[0], bup[1])
    bup_come = swap(jnp.where(s == 0, bup[1], bup[0]))
    bup = jnp.concatenate(
        [jnp.where(s == 0, bup_mine, bup_come), jnp.where(s == 0, bup_come, bup_mine)]
    )
    sums_i = sums_i + swap(sums_i)
    pair = lambda a, b: jnp.sum(jnp.where(s == 0, a, b), 0).reshape(count, -1)
    split = lambda v: jnp.sum(v, 0).reshape(2, count, -1).swapaxes(0, 1).reshape(count, -1)
    packed = [
        pair(sums_a1[0], sums_a2[0]), pair(sums_a1[1], sums_a2[1]),
        pair(sums_n1[0], sums_n2[0]), pair(sums_n1[1], sums_n2[1]),
        pair(sums_a2[2], sums_m2[2]), bup.reshape(count, -1),
        split(sums_i[0]), split(sums_c[0]), split(sums_i[1]), split(sums_c[1]),
    ]
    widths = [v.shape[1] for v in packed]
    packed = jnp.take(jnp.concatenate(packed, 1), jnp.arange(count, dtype=jnp.int32) ^ me, axis=0)
    order = orders(count)[0]
    vec = halving([packed[jnp.array(p)] for p in pieces(order, count)], order, F32)
    cut, at = [], 0
    for w in widths:
        cut.append(vec[at : at + w])
        at += w
    own = lambda v: lax.dynamic_slice(v, (s * small,), (small,))
    return (
        layer_out[None], input_grad[None], image_grad,
        cut[0][None], cut[1][None], g_qkv[None], g_out[None], cut[2][None], cut[3][None],
        g_up[None], cut[5][None], g_down[None], cut[4][None],
        jnp.stack([own(cut[6]), own(cut[7])]), jnp.stack([own(cut[8]), own(cut[9])]),
        g_cq, g_kv, g_co,
    )


def solution(mesh):
    placed = (
        P("dp", None), P("dp", "section", None), P("dp"), P("dp", None),
        P("section", None), P("section", None), P("section", None, None), P("section", None, None),
        P("section", None), P("section", None), P("section", None, None), P("section", None),
        P("section", None, None), P("section", None), P(), P(), P(), P(), P(),
    )
    two, three = P("section", "dp"), P("section", "dp", None)
    last = P(("section", "dp"), None)
    return jax.shard_map(
        on_device,
        mesh=mesh,
        in_specs=placed,
        out_specs=(
            three, three, P("dp", "section", None), two, two, three, three, two, two, three, two,
            three, two, P(None, ("section", "dp")), P(None, ("section", "dp")), last, last, last,
        ),
        check_vma=False,
    )
```

time: 1590 us -> 700 us (0.44)
  waiting for transfers between devices: 843 us -> 215 us
  Pallas kernels: 0 us -> 285 us
  matrix products: 126 us -> 0 us
  blocking collectives: 118 us -> 0 us
  local copies, waits for them, and re-layouts: 139 us -> 31.9 us
  starting transfers between devices: 211 us -> 108 us
  other arithmetic: 106 us -> 46.7 us
  loops' own time: 20.9 us -> 0 us
    reduce_scatter x7 -> x0, waiting for transfers between devices: 678 us -> none  [the longest x4 643 us: on_device(): lax.psum_scatter(layer_acc, 'dp', scatter_dimension=0, tiled=True)]
    pallas_call x0 -> x18, Pallas kernels: none -> 285 us  [call(): pl.pallas_call(body, name=name, out_shape=shapes, grid_spec=pltpu.Prefetc...]
    dot_general x44 -> x0, matrix products: 126 us -> none  [the longest x12 47.8 us: product(): return jnp.dot(left, right, preferred_element_type=jnp.float32)]
    unnamed x2 -> x0, blocking collectives: 118 us -> none
    ppermute x8 -> x103, starting transfers between devices: 211 us -> 108 us  [the longest x76 101 us: halving(): lax.ppermute(parts[step].astype(sent), 'dp', [(i, i ^ bit) for i in range...]
    add x16 -> x5, other arithmetic: 66 us -> 3.63 us  [the longest x4 2.83 us: halving(): parts[later] = parts[later].astype(F32) + arrived[at:at + size].astype(F32)]
    ppermute x8 -> x103, waiting for transfers between devices: 165 us -> 215 us  [the longest x76 205 us: halving(): lax.ppermute(parts[step].astype(sent), 'dp', [(i, i ^ bit) for i in range...]
    another operation x85 -> x0, local copies, waits for them, and re-layouts: 26.1 us -> none
  transfers between devices with their start and end apart: 15 -> 103, of which waited for: 7 -> 66; matrix products, arithmetic and copies ran while one was open for 16% -> 9% of each run, Pallas kernels for 0% -> 41%
where the time goes in v1:
time: 700 us; the launch traced here: 689 us
  Pallas kernels  285 us (41%)
  waiting for transfers between devices  215 us (31%)
  starting transfers between devices  108 us (15%)
  other arithmetic  46.7 us (7%)
  local copies, waits for them, and re-layouts  31.9 us (5%)
    pallas_call x18, Pallas kernels, call(): pl.pallas_call(body, name=name, out_shape=shapes, grid_spec=pltpu.Prefetc...  285 us
    ppermute x76, waiting for transfers between devices, halving(): lax.ppermute(parts[step].astype(sent), 'dp', [(i, i ^ bit) for i in range...  205 us
    ppermute x76, starting transfers between devices, halving(): lax.ppermute(parts[step].astype(sent), 'dp', [(i, i ^ bit) for i in range...  101 us
    convert_element_type x54, other arithmetic, halving(): parts[step].astype(sent)  23.5 us
    unnamed x230, local copies, waits for them, and re-layouts  15.5 us
  transfers between devices with their start and end apart: 103, of which 66 were waited for; matrix products, arithmetic and copies ran while one was open for 9% of the time, Pallas kernels for 41%

profile of v1, /device:TPU:0, one launch (start us, length us, event | category | flops | bytes accessed | tf_op | source)
XLA Modules:
  0.0 688.9 jit_solution(13871231739472685501)
XLA Ops:
  12.4 3.4 dynamic-slice_bitcast_fusion.1
  19.1 17.6 %key_value.1 = (bf16[8,288,768]{2,1,0:T(8,128)(2,1)}, bf16[8,288,768]{2,1,0:T(8,128)(2,1)}, bf16[8,288,768]{2,1,0:T(8,128)(2,1)}) custom-call(s32[2]{0:T(128)} %pad_add_fusion.ids_ref, bf16[8,288,768]{2,1,0:T(8,128)(2,1)} %im_ref.3, f32[1,768]{1,0:T(1,128)} %get-tuple-element.406.g_ref, f32[1,768]{1,0:T(1,128)} %get-tuple-element.392.b_ref, ...), custom_call_target="tpu_custom_call" | custom-call | flops 5435817984 | bytes 23599104 | tf_op jit(solution)/shard_map/key_value/pallas_call | solution.py:137
  40.0 13.2 %self_fwd_0.1 = (bf16[512,768]{1,0:T(8,128)(2,1)}, bf16[3,512,384]{2,1,0:T(8,128)(2,1)}, bf16[512,384]{1,0:T(8,128)(2,1)}, f32[512,768]{1,0:T(8,128)}, bf16[512,768]{1,0:T(8,128)(2,1)}) custom-call(s32[2]{0:T(128)} %pad_add_fusion.ids_ref, bf16[512,768]{1,0:T(8,128)(2,1)} %x_ref.3, f32[1,768]{1,0:T(1,128)} %get-tuple-element.389.refs_1_.g_ref, ...), custom_call_target="tpu_custom_call" | custom-call | flops 1407959552 | bytes 12589056 | tf_op jit(solution)/shard_map/self_fwd_0/pallas_call | solution.py:137
  56.5 16.3 %mlp_fwd_0.1 = (f32[512,768]{1,0:T(8,128)}, bf16[512,768]{1,0:T(8,128)(2,1)}, f32[512,768]{1,0:T(8,128)}, bf16[512,768]{1,0:T(8,128)(2,1)}) custom-call(s32[2]{0:T(128)} %pad_add_fusion.ids_ref, bf16[512,768]{1,0:T(8,128)(2,1)} %x_ref.3, f32[512,768]{1,0:T(8,128)} %get-tuple-element.173.p_ref, bf16[512,768]{1,0:T(8,128)(2,1)} %copy-done.10, ...), custom_call_target="tpu_custom_call" | custom-call | flops 2415919104 | bytes 22035456 | tf_op jit(solution)/shard_map/mlp_fwd_0/pallas_call | solution.py:137
  76.2 14.9 %self_fwd_1.1 = (bf16[512,768]{1,0:T(8,128)(2,1)}, bf16[3,512,384]{2,1,0:T(8,128)(2,1)}, bf16[512,384]{1,0:T(8,128)(2,1)}, f32[512,768]{1,0:T(8,128)}, bf16[512,...) custom-call(s32[2]{0:T(128)} %pad_add_fusion.ids_ref, f32[512,768]{1,0:T(8,128)} %get-tuple-element.175.refs_0_.x_ref, ...), custom_call_target="tpu_custom_call" | custom-call | flops 1407959552 | bytes 16521216 | tf_op jit(solution)/shard_map/self_fwd_1/pallas_call | solution.py:137
  94.5 20.0 %cross_fwd.1 = (f32[512,768]{1,0:T(8,128)}, bf16[512,768]{1,0:T(8,128)(2,1)}, bf16[512,384]{1,0:T(8,128)(2,1)}, bf16[512,384]{1,0:T(8,128)(2,1)}, f32[512,768]{1,0:T(8,128)}, /*index=5*/bf16[512,768]{1,0:T(8,128)(2,1)}) custom-call(s32[2]{0:T(128)} %pad_add_fusion.ids_ref, s32[8]{0:T(128)} %cnt_ref.3, bf16[512,768]{1,0:T(8,128)(2,1)} %get-tuple-element.178.z_ref.refs_3_, ...), custom_call_target="tpu_custom_call" | custom-call | flops 2203979776 | bytes 18094080 | tf_op jit(solution)/shard_map/cross_fwd/pallas_call | solution.py:137
  117.9 23.8 %mlp_grad_1.1 = (bf16[512,1536]{1,0:T(8,128)(2,1)}, bf16[512,1536]{1,0:T(8,128)(2,1)}, f32[512,768]{1,0:T(8,128)}, bf16[512,768]{1,0:T(8,128)(2,1)}, f32[3,8,768...) custom-call(s32[2]{0:T(128)} %pad_add_fusion.ids_ref, ...), custom_call_target="tpu_custom_call" | custom-call | flops 4831838208 | bytes 29236224 | tf_op jit(solution)/shard_map/mlp_grad_1/pallas_call | solution.py:137
  145.2 26.9 %cross_grad.1 = (f32[512,768]{1,0:T(8,128)}, bf16[512,768]{1,0:T(8,128)(2,1)}, bf16[512,384]{1,0:T(8,128)(2,1)}, bf16[8,288,768]{2,1,0:T(8,128)(2,1)}, bf16[8,28...) custom-call(s32[2]{0:T(128)} %pad_add_fusion.ids_ref, s32[8]{0:T(128)} %cnt_ref.3, ...), custom_call_target="tpu_custom_call" | custom-call | flops 5603979776 | bytes 26790912 | tf_op jit(solution)/shard_map/cross_grad/pallas_call | solution.py:137
  172.2 18.9 %key_value_weights.1 = (bf16[8,96,128]{2,1,0:T(8,128)(2,1)}, bf16[4,96,128]{2,1,0:T(8,128)(2,1)}, bf16[2,96,128]{2,1,0:T(8,128)(2,1)}, bf16[1,96,128]{2,1,0:T(8,...) custom-call(s32[2]{0:T(128)} %pad_add_fusion.ids_ref, ...), custom_call_target="tpu_custom_call" | custom-call | flops 5435817984 | bytes 15335424 | tf_op jit(solution)/shard_map/key_value_weights/pallas_call | solution.py:137
  191.1 2.8 collective-permute-start.98
  196.4 4.5 cross_weights.1
  202.7 5.7 collective-permute-done.94
  210.0 4.9 collective-permute-done.90
  215.1 5.6 collective-permute-done.85
  223.2 3.4 collective-permute-done.81
  229.1 4.5 collective-permute-done.77
  239.7 3.7 collective-permute-done.95
  245.0 3.1 collective-permute-done.91
  249.5 3.1 collective-permute-done.86
  254.2 3.1 collective-permute-done.82
  258.8 3.1 collective-permute-done.78
  263.4 2.5 collective-permute-done.100
  266.0 4.1 collective-permute-done.96
  270.1 4.1 collective-permute-done.92
  275.7 2.5 collective-permute-done.87
  278.5 3.9 collective-permute-done.83
  282.6 3.9 collective-permute-done.79
  286.4 2.8 collective-permute-start.101
  291.6 2.4 collective-permute-start.97
  305.8 2.4 collective-permute-start.84
  310.5 2.4 collective-permute-start.80
  319.4 19.7 %self_grad_1.1 = (f32[512,768]{1,0:T(8,128)}, bf16[512,768]{1,0:T(8,128)(2,1)}, bf16[3,512,384]{2,1,0:T(8,128)(2,1)}, f32[512,768]{1,0:T(8,128)}, bf16[512,768]{1,0:T(8,128)(2,1)}, /*index=5*/f32[2,8,768]{2,1,0:T(8,128)}) custom-call(s32[2]{0:T(128)} %pad_add_fusion.ids_ref, f32[512,768]{1,0:T(8,128)} %get-tuple-element.192.gr_ref, ...), custom_call_target="tpu_custom_call" | custom-call | flops 1707959552 | bytes 19713024 | tf_op jit(solution)/shard_map/self_grad_1/pallas_call | solution.py:137
  339.9 6.5 self_weights_1.1
  349.5 10.7 %mlp_weights_1.1 = (bf16[8,384,128]{2,1,0:T(8,128)(2,1)}, bf16[4,384,128]{2,1,0:T(8,128)(2,1)}, bf16[2,384,128]{2,1,0:T(8,128)(2,1)}, bf16[1,384,128]{2,1,0:T(8,...) custom-call(s32[2]{0:T(128)} %pad_add_fusion.ids_ref, ...), custom_call_target="tpu_custom_call" | custom-call | flops 2415919104 | bytes 11010048 | tf_op jit(solution)/shard_map/mlp_weights_1/pallas_call | solution.py:137
  363.8 7.7 %collective-permute-done.63 = bf16[8,192,128]{2,1,0:T(8,128)(2,1)S(1)} collective-permute-done((bf16[8,192,128]{2,1,0:T(8,128)(2,1)S(1)}, bf16[8,192,128]{2,1,0:T(8,128)(2,1)S(1)}, u32[]{:S(2)}, u32[]{:S(2)}) %collective-permute-start.63) | collective-permute-done | bytes 393248 | tf_op jit(solution)/shard_map/ppermute | solution.py:744
  373.0 4.5 collective-permute-done.72
  379.1 4.1 collective-permute-done.68
  383.5 6.4 collective-permute-done.64
  390.2 4.3 collective-permute-done.73
  396.3 2.9 collective-permute-done.69
  400.9 2.9 collective-permute-done.65
  406.0 3.0 collective-permute-done.74
  411.3 2.7 collective-permute-done.70
  416.3 2.7 collective-permute-done.66
  421.4 21.8 %mlp_grad_0.1 = (bf16[512,1536]{1,0:T(8,128)(2,1)}, bf16[512,1536]{1,0:T(8,128)(2,1)}, f32[512,768]{1,0:T(8,128)}, bf16[512,768]{1,0:T(8,128)(2,1)}, f32[3,8,768...) custom-call(s32[2]{0:T(128)} %pad_add_fusion.ids_ref, f32[512,768]{1,0:T(8,128)} %get-tuple-element.196.refs_0_, ...), custom_call_target="tpu_custom_call" | custom-call | flops 3623878656 | bytes 26093568 | tf_op jit(solution)/shard_map/mlp_grad_0/pallas_call | solution.py:137
  452.5 8.3 %collective-permute-done.59 = bf16[4,384,128]{2,1,0:T(8,128)(2,1)} collective-permute-done((bf16[4,384,128]{2,1,0:T(8,128)(2,1)}, bf16[4,384,128]{2,1,0:T(8,128)(2,1)}, u32[]{:S(2)}, u32[]{:S(2)}) %collective-permute-start.59) | collective-permute-done | bytes 393248 | tf_op jit(solution)/shard_map/ppermute | solution.py:744
  463.3 4.8 collective-permute-done.55
  472.6 3.2 collective-permute-done.60
  478.6 4.0 collective-permute-done.56
  485.3 4.0 collective-permute-done.52
  489.3 2.7 collective-permute-start.61
  492.9 6.0 collective-permute-done.61
  499.9 3.0 collective-permute-start.53
  502.9 19.5 %self_grad_0.1 = (f32[512,768]{1,0:T(8,128)}, bf16[512,768]{1,0:T(8,128)(2,1)}, bf16[3,512,384]{2,1,0:T(8,128)(2,1)}, f32[512,768]{1,0:T(8,128)}, bf16[512,768]{1,0:T(8,128)(2,1)}, /*index=5*/f32[2,8,768]{2,1,0:T(8,128)}) custom-call(s32[2]{0:T(128)} %pad_add_fusion.ids_ref, bf16[512,768]{1,0:T(8,128)(2,1)} %get-tuple-element.200.gr_ref.refs_4_, ...), custom_call_target="tpu_custom_call" | custom-call | flops 1707959552 | bytes 18926592 | tf_op jit(solution)/shard_map/self_grad_0/pallas_call | solution.py:137
  522.4 6.6 self_weights_0.1
  533.7 3.4 collective-permute-done.45
  541.2 8.1 %collective-permute-done.37 = bf16[8,192,128]{2,1,0:T(8,128)(2,1)S(1)} collective-permute-done((bf16[8,192,128]{2,1,0:T(8,128)(2,1)}, bf16[8,192,128]{2,1,0:T(8,128)(2,1)S(1)}, u32[]{:S(2)}, u32[]{:S(2)}) %collective-permute-start.37) | collective-permute-done | bytes 393248 | tf_op jit(solution)/shard_map/ppermute | solution.py:744
  570.2 5.8 text_grad.1
  576.1 27.3 %key_value_grad.1 = (f32[8,288,768]{2,1,0:T(8,128)}, f32[2,8,768]{2,1,0:T(8,128)}) custom-call(s32[2]{0:T(128)} %pad_add_fusion.ids_ref, bf16[8,288,768]{2,1,0:T(8,128)(2,1)} %im_ref.3, f32[1,768]{1,0:T(1,128)} %get-tuple-element.406.g_ref, bf16[8,288,768]{2,1,0:T(8,128)(2,1)} %get-tuple-element.208.own_ref.go, ...), custom_call_target="tpu_custom_call" | custom-call | flops 5435817984 | bytes 27184128 | tf_op jit(solution)/shard_map/key_value_grad/pallas_call | solution.py:137
  612.9 10.9 %mlp_weights_0.1 = (bf16[8,384,128]{2,1,0:T(8,128)(2,1)}, bf16[4,384,128]{2,1,0:T(8,128)(2,1)}, bf16[2,384,128]{2,1,0:T(8,128)(2,1)}, bf16[1,384,128]{2,1,0:T(8,...) custom-call(s32[2]{0:T(128)} %pad_add_fusion.ids_ref, ...), custom_call_target="tpu_custom_call" | custom-call | flops 2415919104 | bytes 11010048 | tf_op jit(solution)/shard_map/mlp_weights_0/pallas_call | solution.py:137
  630.1 12.2 %collective-permute-done.21 = f32[2,624]{1,0:T(2,128)S(1)} collective-permute-done((f32[2,624]{1,0:T(2,128)S(1)}, f32[2,624]{1,0:T(2,128)S(1)}, u32[]{:S(2)}, u32[]{:S(2)}) %collective-permute-start.21) | collective-permute-done | bytes 5024 | tf_op jit(solution)/shard_map/ppermute | solution.py:744
  653.7 8.5 %collective-permute-done.33 = bf16[4,384,128]{2,1,0:T(8,128)(2,1)S(1)} collective-permute-done((bf16[4,384,128]{2,1,0:T(8,128)(2,1)S(1)}, bf16[4,384,128]{2,1,0:T(8,128)(2,1)S(1)}, u32[]{:S(2)}, u32[]{:S(2)}) %collective-permute-start.33) | collective-permute-done | bytes 393248 | tf_op jit(solution)/shard_map/ppermute | solution.py:744
  670.8 2.7 collective-permute-done.30
  680.6 2.8 collective-permute-done.27
  (543 shorter events, 209.1 us)
Async XLA Ops:
  8.3 28.5 %collective-permute-start = (f32[1,6912]{1,0:T(1,128)}, f32[1,6912]{1,0:T(1,128)}, u32[]{:S(2)}, u32[]{:S(2)}) collective-permute-start(f32[1,6912]{1,0:T(1,128)} %constant_dynamic-update-slice_fusion), channel_id=1, source_target_pairs={{0,16},{16,0},{1,17},{17,1},{2,18},{18,2},{3,19},{19,3},{4,20},{20... | collective-permute-start | bytes 82952 | tf_op jit(solution)/shard_map/ppermute | solution.py:959
  11.8 26.7 %collective-permute-start.1 = (bf16[768,1152]{1,0:T(8,128)(2,1)}, bf16[768,1152]{1,0:T(8,128)(2,1)S(1)}, u32[]{:S(2)}, u32[]{:S(2)}) collective-permute-start(bf16[768,1152]{1,0:T(8,128)(2,1)} %pad_maximum_fusion), channel_id=1, source_target_pairs={{0,16},{16,0},{1,17},{17,1},{2,18},{18,2},{3,19},{19,3},{4,20},{20... | collective-permute-start | bytes 5308424 | tf_op jit(solution)/shard_map/ppermute | solution.py:959
  12.1 26.4 %collective-permute-start.2 = (bf16[384,768]{1,0:T(8,128)(2,1)S(1)}, bf16[384,768]{1,0:T(8,128)(2,1)S(1)}, u32[]{:S(2)}, u32[]{:S(2)}) collective-permute-start(bf16[384,768]{1,0:T(8,128)(2,1)S(1)} %dynamic-slice_bitcast_fusion.2), channel_id=1, source_target_pairs={{0,16},{16,0},{1,17},{17,1},{2,18},{18,2},{3,19},{19,3},{4,20},{20... | collective-permute-start | bytes 1769480 | tf_op jit(solution)/shard_map/ppermute | solution.py:959
  15.8 38.1 %collective-permute-start.4 = (bf16[768,1536]{1,0:T(8,128)(2,1)}, bf16[768,1536]{1,0:T(8,128)(2,1)}, u32[]{:S(2)}, u32[]{:S(2)}) collective-permute-start(bf16[768,1536]{1,0:T(8,128)(2,1)} %dynamic-slice_bitcast_fusion.1), channel_id=1, source_target_pairs={{0,16},{16,0},{1,17},{17,1},{2,18},{18,2},{3,19},{19,3},{4,20},{20... | collective-permute-start | bytes 7077896 | tf_op jit(solution)/shard_map/ppermute | solution.py:959
  17.7 36.3 %collective-permute-start.5 = (bf16[1536,768]{1,0:T(8,128)(2,1)}, bf16[1536,768]{1,0:T(8,128)(2,1)}, u32[]{:S(2)}, u32[]{:S(2)}) collective-permute-start(bf16[1536,768]{1,0:T(8,128)(2,1)} %dynamic-slice_bitcast_fusion), channel_id=1, source_target_pairs={{0,16},{16,0},{1,17},{17,1},{2,18},{18,2},{3,19},{19,3},{4,20},{20... | collective-permute-start | bytes 7077896 | tf_op jit(solution)/shard_map/ppermute | solution.py:959
  36.7 54.9 %collective-permute-start.8 = (bf16[8,288,768]{2,1,0:T(8,128)(2,1)}, bf16[8,288,768]{2,1,0:T(8,128)(2,1)}, u32[]{:S(2)}, u32[]{:S(2)}) collective-permute-start(bf16[8,288,768]{2,1,0:T(8,128)(2,1)} %get-tuple-element.182), channel_id=1, source_target_pairs={{0,16},{16,0},{1,17},{17,1},{2,18},{18,2},{3,19},{19,3},{4,20},{20... | collective-permute-start | bytes 10616840 | tf_op jit(solution)/shard_map/ppermute | solution.py:959
  91.3 80.8 %collective-permute-start.89 = (bf16[8,288,768]{2,1,0:T(8,128)(2,1)S(1)}, bf16[8,288,768]{2,1,0:T(8,128)(2,1)}, u32[]{:S(2)}, u32[]{:S(2)}) collective-permute-start(bf16[8,288,768]{2,1,0:T(8,128)(2,1)S(1)} %copy-done.100), channel_id=1, source_target_pairs={{0,16},{16,0},{1,17},{17,1},{2,18},{18,2},{3,19},{19,3},{4,20},{20... | collective-permute-start | bytes 10616840 | tf_op jit(solution)/shard_map/ppermute | solution.py:959
  142.7 53.0 %collective-permute-start.76 = (bf16[512,384]{1,0:T(8,128)(2,1)S(1)}, bf16[512,384]{1,0:T(8,128)(2,1)S(1)}, u32[]{:S(2)}, u32[]{:S(2)}) collective-permute-start(bf16[512,384]{1,0:T(8,128)(2,1)S(1)} %copy-done.23), channel_id=1, source_target_pairs={{0,16},{16,0},{1,17},{17,1},{2,18},{18,2},{3,19},{19,3},{4,20},{20... | collective-permute-start | bytes 1179656 | tf_op jit(solution)/shard_map/ppermute | solution.py:959
  191.1 9.9 %collective-permute-start.98 = (bf16[8,96,128]{2,1,0:T(8,128)(2,1)}, bf16[8,96,128]{2,1,0:T(8,128)(2,1)S(1)}, u32[]{:S(2)}, u32[]{:S(2)}) collective-permute-start(bf16[8,96,128]{2,1,0:T(8,128)(2,1)} %get-tuple-element.324), channel_id=1, source_target_pairs={{0,4},{1,5},{2,6},{3,7},{4,0},{5,1},{6,2},{7,3},{8,12},{9,13},{10,... | collective-permute-start | bytes 589832 | tf_op jit(solution)/shard_map/ppermute | solution.py:744
  195.1 327.3 %collective-permute-start.36 = (bf16[512,384]{1,0:T(8,128)(2,1)}, bf16[512,384]{1,0:T(8,128)(2,1)}, u32[]{:S(2)}, u32[]{:S(2)}) collective-permute-start(bf16[512,384]{1,0:T(8,128)(2,1)} %get-tuple-element.239.refs_2_), channel_id=1, source_target_pairs={{0,16},{16,0},{1,17},{17,1},{2,18},{18,2},{3,19},{19,3},{4,20},{20... | collective-permute-start | bytes 1179656 | tf_op jit(solution)/shard_map/ppermute | solution.py:959
  195.1 144.0 %collective-permute-start.62 = (bf16[512,384]{1,0:T(8,128)(2,1)S(1)}, bf16[512,384]{1,0:T(8,128)(2,1)S(1)}, u32[]{:S(2)}, u32[]{:S(2)}) collective-permute-start(bf16[512,384]{1,0:T(8,128)(2,1)S(1)} %copy-done.103), channel_id=1, source_target_pairs={{0,16},{16,0},{1,17},{17,1},{2,18},{18,2},{3,19},{19,3},{4,20},{20... | collective-permute-start | bytes 1179656 | tf_op jit(solution)/shard_map/ppermute | solution.py:959
  195.6 119.7 %collective-permute-start.10 = (bf16[512,768]{1,0:T(8,128)(2,1)}, bf16[512,768]{1,0:T(8,128)(2,1)S(1)}, u32[]{:S(2)}, u32[]{:S(2)}) collective-permute-start(bf16[512,768]{1,0:T(8,128)(2,1)} %get-tuple-element.188), channel_id=1, source_target_pairs={{0,16},{16,0},{1,17},{17,1},{2,18},{18,2},{3,19},{19,3},{4,20},{20... | collective-permute-start | bytes 2359304 | tf_op jit(solution)/shard_map/ppermute | solution.py:959
  195.7 152.2 %collective-permute-start.49 = (bf16[512,1536]{1,0:T(8,128)(2,1)}, bf16[512,1536]{1,0:T(8,128)(2,1)}, u32[]{:S(2)}, u32[]{:S(2)}) collective-permute-start(bf16[512,1536]{1,0:T(8,128)(2,1)} %get-tuple-element.258.refs_2_), channel_id=1, source_target_pairs={{0,16},{16,0},{1,17},{17,1},{2,18},{18,2},{3,19},{19,3},{4,20},{20... | collective-permute-start | bytes 4718600 | tf_op jit(solution)/shard_map/ppermute | solution.py:959
  201.0 7.4 %collective-permute-start.94 = (bf16[8,96,128]{2,1,0:T(8,128)(2,1)S(1)}, bf16[8,96,128]{2,1,0:T(8,128)(2,1)S(1)}, u32[]{:S(2)}, u32[]{:S(2)}) collective-permute-start(bf16[8,96,128]{2,1,0:T(8,128)(2,1)S(1)} %copy-done.107), channel_id=1, source_target_pairs={{0,2},{1,3},{2,0},{3,1},{4,6},{5,7},{6,4},{7,5},{8,10},{9,11},{10,... | collective-permute-start | bytes 589832 | tf_op jit(solution)/shard_map/ppermute | solution.py:744
  208.4 6.5 collective-permute-start.90
  214.9 5.9 collective-permute-start.85
  220.8 5.9 collective-permute-start.81
  226.6 6.9 %collective-permute-start.77 = (bf16[8,96,128]{2,1,0:T(8,128)(2,1)}, bf16[8,96,128]{2,1,0:T(8,128)(2,1)S(1)}, u32[]{:S(2)}, u32[]{:S(2)}) collective-permute-start(bf16[8,96,128]{2,1,0:T(8,128)(2,1)} %get-tuple-element.298), channel_id=1, source_target_pairs={{0,1},{1,0},{2,3},{3,2},{4,5},{5,4},{6,7},{7,6},{8,9},{9,8},{10,11... | collective-permute-start | bytes 589832 | tf_op jit(solution)/shard_map/ppermute | solution.py:744
  317.7 258.3 %collective-permute-start.16 = (bf16[8,288,768]{2,1,0:T(8,128)(2,1)}, bf16[8,288,768]{2,1,0:T(8,128)(2,1)}, u32[]{:S(2)}, u32[]{:S(2)}) collective-permute-start(bf16[8,288,768]{2,1,0:T(8,128)(2,1)} %get-tuple-element.209.gg), channel_id=1, source_target_pairs={{0,16},{16,0},{1,17},{17,1},{2,18},{18,2},{3,19},{19,3},{4,20},{20... | collective-permute-start | bytes 10616840 | tf_op jit(solution)/shard_map/ppermute | solution.py:959
  346.4 13.8 %collective-permute-start.71 = (bf16[8,192,128]{2,1,0:T(8,128)(2,1)}, bf16[8,192,128]{2,1,0:T(8,128)(2,1)S(1)}, u32[]{:S(2)}, u32[]{:S(2)}) collective-permute-start(bf16[8,192,128]{2,1,0:T(8,128)(2,1)} %get-tuple-element.289), channel_id=1, source_target_pairs={{0,4},{1,5},{2,6},{3,7},{4,0},{5,1},{6,2},{7,3},{8,12},{9,13},{10,... | collective-permute-start | bytes 1179656 | tf_op jit(solution)/shard_map/ppermute | solution.py:744
  347.1 72.0 %collective-permute-start.13 = (bf16[512,768]{1,0:T(8,128)(2,1)}, bf16[512,768]{1,0:T(8,128)(2,1)S(1)}, u32[]{:S(2)}, u32[]{:S(2)}) collective-permute-start(bf16[512,768]{1,0:T(8,128)(2,1)} %get-tuple-element.198), channel_id=1, source_target_pairs={{0,16},{16,0},{1,17},{17,1},{2,18},{18,2},{3,19},{19,3},{4,20},{20... | collective-permute-start | bytes 2359304 | tf_op jit(solution)/shard_map/ppermute | solution.py:959
  347.9 14.0 %collective-permute-start.67 = (bf16[8,192,128]{2,1,0:T(8,128)(2,1)}, bf16[8,192,128]{2,1,0:T(8,128)(2,1)S(1)}, u32[]{:S(2)}, u32[]{:S(2)}) collective-permute-start(bf16[8,192,128]{2,1,0:T(8,128)(2,1)} %get-tuple-element.284), channel_id=1, source_target_pairs={{0,2},{1,3},{2,0},{3,1},{4,6},{5,7},{6,4},{7,5},{8,10},{9,11},{10,... | collective-permute-start | bytes 1179656 | tf_op jit(solution)/shard_map/ppermute | solution.py:744
  360.3 11.2 %collective-permute-start.63 = (bf16[8,192,128]{2,1,0:T(8,128)(2,1)S(1)}, bf16[8,192,128]{2,1,0:T(8,128)(2,1)S(1)}, u32[]{:S(2)}, u32[]{:S(2)}) collective-permute-start(bf16[8,192,128]{2,1,0:T(8,128)(2,1)S(1)} %copy-done.105), channel_id=1, source_target_pairs={{0,1},{1,0},{2,3},{3,2},{4,5},{5,4},{6,7},{7,6},{8,9},{9,8},{10,11... | collective-permute-start | bytes 1179656 | tf_op jit(solution)/shard_map/ppermute | solution.py:744
  361.9 82.2 %collective-permute-start.58 = (bf16[8,384,128]{2,1,0:T(8,128)(2,1)}, bf16[8,384,128]{2,1,0:T(8,128)(2,1)S(1)}, u32[]{:S(2)}, u32[]{:S(2)}) collective-permute-start(bf16[8,384,128]{2,1,0:T(8,128)(2,1)} %get-tuple-element.270), channel_id=1, source_target_pairs={{0,4},{1,5},{2,6},{3,7},{4,0},{5,1},{6,2},{7,3},{8,12},{9,13},{10,... | collective-permute-start | bytes 2359304 | tf_op jit(solution)/shard_map/ppermute | solution.py:744
  371.5 6.1 collective-permute-start.72
  377.6 5.7 collective-permute-start.68
  383.2 6.7 collective-permute-start.64
  419.0 27.0 %collective-permute-start.54 = (bf16[8,384,128]{2,1,0:T(8,128)(2,1)}, bf16[8,384,128]{2,1,0:T(8,128)(2,1)S(1)}, u32[]{:S(2)}, u32[]{:S(2)}) collective-permute-start(bf16[8,384,128]{2,1,0:T(8,128)(2,1)} %get-tuple-element.265), channel_id=1, source_target_pairs={{0,2},{1,3},{2,0},{3,1},{4,6},{5,7},{6,4},{7,5},{8,10},{9,11},{10,... | collective-permute-start | bytes 2359304 | tf_op jit(solution)/shard_map/ppermute | solution.py:744
  419.1 29.3 %collective-permute-start.50 = (bf16[8,384,128]{2,1,0:T(8,128)(2,1)}, bf16[8,384,128]{2,1,0:T(8,128)(2,1)}, u32[]{:S(2)}, u32[]{:S(2)}) collective-permute-start(bf16[8,384,128]{2,1,0:T(8,128)(2,1)} %get-tuple-element.260), channel_id=1, source_target_pairs={{0,1},{1,0},{2,3},{3,2},{4,5},{5,4},{6,7},{7,6},{8,9},{9,8},{10,11... | collective-permute-start | bytes 2359304 | tf_op jit(solution)/shard_map/ppermute | solution.py:744
  444.1 55.8 %collective-permute-start.14 = (bf16[512,768]{1,0:T(8,128)(2,1)}, bf16[512,768]{1,0:T(8,128)(2,1)S(1)}, u32[]{:S(2)}, u32[]{:S(2)}) collective-permute-start(bf16[512,768]{1,0:T(8,128)(2,1)} %get-tuple-element.202), channel_id=1, source_target_pairs={{0,16},{16,0},{1,17},{17,1},{2,18},{18,2},{3,19},{19,3},{4,20},{20... | collective-permute-start | bytes 2359304 | tf_op jit(solution)/shard_map/ppermute | solution.py:959
  448.4 12.3 %collective-permute-start.59 = (bf16[4,384,128]{2,1,0:T(8,128)(2,1)}, bf16[4,384,128]{2,1,0:T(8,128)(2,1)}, u32[]{:S(2)}, u32[]{:S(2)}) collective-permute-start(bf16[4,384,128]{2,1,0:T(8,128)(2,1)} %add_convert_fusion.1), channel_id=1, source_target_pairs={{0,1},{1,0},{2,3},{3,2},{4,5},{5,4},{6,7},{7,6},{8,9},{9,8},{10,11... | collective-permute-start | bytes 1179656 | tf_op jit(solution)/shard_map/ppermute | solution.py:744
  451.1 17.0 %collective-permute-start.55 = (bf16[4,384,128]{2,1,0:T(8,128)(2,1)}, bf16[4,384,128]{2,1,0:T(8,128)(2,1)S(1)}, u32[]{:S(2)}, u32[]{:S(2)}) collective-permute-start(bf16[4,384,128]{2,1,0:T(8,128)(2,1)} %add_convert_fusion.2), channel_id=1, source_target_pairs={{0,1},{1,0},{2,3},{3,2},{4,5},{5,4},{6,7},{7,6},{8,9},{9,8},{10,11... | collective-permute-start | bytes 1179656 | tf_op jit(solution)/shard_map/ppermute | solution.py:744
  460.8 9.4 %collective-permute-start.51 = (bf16[4,384,128]{2,1,0:T(8,128)(2,1)}, bf16[4,384,128]{2,1,0:T(8,128)(2,1)S(1)}, u32[]{:S(2)}, u32[]{:S(2)}) collective-permute-start(bf16[4,384,128]{2,1,0:T(8,128)(2,1)} %add_convert_fusion.3), channel_id=1, source_target_pairs={{0,2},{1,3},{2,0},{3,1},{4,6},{5,7},{6,4},{7,5},{8,10},{9,11},{10,... | collective-permute-start | bytes 1179656 | tf_op jit(solution)/shard_map/ppermute | solution.py:744
  468.1 144.8 %collective-permute-start.23 = (bf16[512,1536]{1,0:T(8,128)(2,1)}, bf16[512,1536]{1,0:T(8,128)(2,1)}, u32[]{:S(2)}, u32[]{:S(2)}) collective-permute-start(bf16[512,1536]{1,0:T(8,128)(2,1)} %get-tuple-element.221.refs_2_), channel_id=1, source_target_pairs={{0,16},{16,0},{1,17},{17,1},{2,18},{18,2},{3,19},{19,3},{4,20},{20... | collective-permute-start | bytes 4718600 | tf_op jit(solution)/shard_map/ppermute | solution.py:959
  470.2 5.7 collective-permute-start.60
  475.9 6.8 collective-permute-start.56
  482.6 6.7 collective-permute-start.52
  489.3 9.6 %collective-permute-start.61 = (bf16[1,384,128]{2,1,0:T(8,128)(2,1)S(1)}, bf16[1,384,128]{2,1,0:T(8,128)(2,1)S(1)}, u32[]{:S(2)}, u32[]{:S(2)}) collective-permute-start(bf16[1,384,128]{2,1,0:T(8,128)(2,1)S(1)} %add_convert_fusion.28), channel_id=1, source_target_pairs={{0,8},{1,9},{2,10},{3,11},{4,12},{5,13},{6,14},{7,15},{8,0},{9,1},... | collective-permute-start | bytes 294920 | tf_op jit(solution)/shard_map/ppermute | solution.py:744
  498.9 31.0 %collective-permute-start.57 = (bf16[1,384,128]{2,1,0:T(8,128)(2,1)S(1)}, bf16[1,384,128]{2,1,0:T(8,128)(2,1)S(1)}, u32[]{:S(2)}, u32[]{:S(2)}) collective-permute-start(bf16[1,384,128]{2,1,0:T(8,128)(2,1)S(1)} %add_convert_fusion.29), channel_id=1, source_target_pairs={{0,8},{1,9},{2,10},{3,11},{4,12},{5,13},{6,14},{7,15},{8,0},{9,1},... | collective-permute-start | bytes 294920 | tf_op jit(solution)/shard_map/ppermute | solution.py:744
  499.9 32.5 %collective-permute-start.53 = (bf16[1,384,128]{2,1,0:T(8,128)(2,1)S(1)}, bf16[1,384,128]{2,1,0:T(8,128)(2,1)S(1)}, u32[]{:S(2)}, u32[]{:S(2)}) collective-permute-start(bf16[1,384,128]{2,1,0:T(8,128)(2,1)S(1)} %add_convert_fusion.30), channel_id=1, source_target_pairs={{0,8},{1,9},{2,10},{3,11},{4,12},{5,13},{6,14},{7,15},{8,0},{9,1},... | collective-permute-start | bytes 294920 | tf_op jit(solution)/shard_map/ppermute | solution.py:744
  529.0 8.1 %collective-permute-start.45 = (bf16[8,192,128]{2,1,0:T(8,128)(2,1)}, bf16[8,192,128]{2,1,0:T(8,128)(2,1)S(1)}, u32[]{:S(2)}, u32[]{:S(2)}) collective-permute-start(bf16[8,192,128]{2,1,0:T(8,128)(2,1)} %get-tuple-element.252), channel_id=1, source_target_pairs={{0,4},{1,5},{2,6},{3,7},{4,0},{5,1},{6,2},{7,3},{8,12},{9,13},{10,... | collective-permute-start | bytes 1179656 | tf_op jit(solution)/shard_map/ppermute | solution.py:744
  530.8 8.1 %collective-permute-start.41 = (bf16[8,192,128]{2,1,0:T(8,128)(2,1)}, bf16[8,192,128]{2,1,0:T(8,128)(2,1)S(1)}, u32[]{:S(2)}, u32[]{:S(2)}) collective-permute-start(bf16[8,192,128]{2,1,0:T(8,128)(2,1)} %get-tuple-element.247), channel_id=1, source_target_pairs={{0,2},{1,3},{2,0},{3,1},{4,6},{5,7},{6,4},{7,5},{8,10},{9,11},{10,... | collective-permute-start | bytes 1179656 | tf_op jit(solution)/shard_map/ppermute | solution.py:744
  533.4 35.8 %collective-permute-start.15 = (bf16[512,768]{1,0:T(8,128)(2,1)}, bf16[512,768]{1,0:T(8,128)(2,1)S(1)}, u32[]{:S(2)}, u32[]{:S(2)}) collective-permute-start(bf16[512,768]{1,0:T(8,128)(2,1)} %get-tuple-element.206), channel_id=1, source_target_pairs={{0,16},{16,0},{1,17},{17,1},{2,18},{18,2},{3,19},{19,3},{4,20},{20... | collective-permute-start | bytes 2359304 | tf_op jit(solution)/shard_map/ppermute | solution.py:959
  537.1 12.2 %collective-permute-start.37 = (bf16[8,192,128]{2,1,0:T(8,128)(2,1)}, bf16[8,192,128]{2,1,0:T(8,128)(2,1)S(1)}, u32[]{:S(2)}, u32[]{:S(2)}) collective-permute-start(bf16[8,192,128]{2,1,0:T(8,128)(2,1)} %get-tuple-element.242), channel_id=1, source_target_pairs={{0,1},{1,0},{2,3},{3,2},{4,5},{5,4},{6,7},{7,6},{8,9},{9,8},{10,11... | collective-permute-start | bytes 1179656 | tf_op jit(solution)/shard_map/ppermute | solution.py:744
  538.9 12.9 %collective-permute-start.46 = (bf16[4,192,128]{2,1,0:T(8,128)(2,1)S(1)}, bf16[4,192,128]{2,1,0:T(8,128)(2,1)S(1)}, u32[]{:S(2)}, u32[]{:S(2)}) collective-permute-start(bf16[4,192,128]{2,1,0:T(8,128)(2,1)S(1)} %add_convert_fusion.13), channel_id=1, source_target_pairs={{0,1},{1,0},{2,3},{3,2},{4,5},{5,4},{6,7},{7,6},{8,9},{9,8},{10,11... | collective-permute-start | bytes 589832 | tf_op jit(solution)/shard_map/ppermute | solution.py:744
  549.3 5.7 collective-permute-start.42
  551.8 5.7 collective-permute-start.38
  562.1 5.5 collective-permute-start.48
  564.3 44.1 %collective-permute-start.44 = (bf16[1,192,128]{2,1,0:T(8,128)(2,1)S(1)}, bf16[1,192,128]{2,1,0:T(8,128)(2,1)S(1)}, u32[]{:S(2)}, u32[]{:S(2)}) collective-permute-start(bf16[1,192,128]{2,1,0:T(8,128)(2,1)S(1)} %add_convert_fusion.47), channel_id=1, source_target_pairs={{0,8},{1,9},{2,10},{3,11},{4,12},{5,13},{6,14},{7,15},{8,0},{9,1},... | collective-permute-start | bytes 147464 | tf_op jit(solution)/shard_map/ppermute | solution.py:744
  567.6 59.6 %collective-permute-start.40 = (bf16[1,192,128]{2,1,0:T(8,128)(2,1)}, bf16[1,192,128]{2,1,0:T(8,128)(2,1)}, u32[]{:S(2)}, u32[]{:S(2)}) collective-permute-start(bf16[1,192,128]{2,1,0:T(8,128)(2,1)} %add_convert_fusion.48), channel_id=1, source_target_pairs={{0,8},{1,9},{2,10},{3,11},{4,12},{5,13},{6,14},{7,15},{8,0},{9,1},... | collective-permute-start | bytes 147464 | tf_op jit(solution)/shard_map/ppermute | solution.py:744
  611.9 13.1 %collective-permute-start.20 = (f32[4,624]{1,0:T(4,128)}, f32[4,624]{1,0:T(4,128)S(1)}, u32[]{:S(2)}, u32[]{:S(2)}) collective-permute-start(f32[4,624]{1,0:T(4,128)} %slice_add_fusion), channel_id=1, source_target_pairs={{0,2},{1,3},{2,0},{3,1},{4,6},{5,7},{6,4},{7,5},{8,10},{9,11},{10,... | collective-permute-start | bytes 29960 | tf_op jit(solution)/shard_map/ppermute | solution.py:744
  623.8 25.2 %collective-permute-start.32 = (bf16[8,384,128]{2,1,0:T(8,128)(2,1)}, bf16[8,384,128]{2,1,0:T(8,128)(2,1)}, u32[]{:S(2)}, u32[]{:S(2)}) collective-permute-start(bf16[8,384,128]{2,1,0:T(8,128)(2,1)} %get-tuple-element.233), channel_id=1, source_target_pairs={{0,4},{1,5},{2,6},{3,7},{4,0},{5,1},{6,2},{7,3},{8,12},{9,13},{10,... | collective-permute-start | bytes 2359304 | tf_op jit(solution)/shard_map/ppermute | solution.py:744
  625.7 16.6 %collective-permute-start.21 = (f32[2,624]{1,0:T(2,128)S(1)}, f32[2,624]{1,0:T(2,128)S(1)}, u32[]{:S(2)}, u32[]{:S(2)}) collective-permute-start(f32[2,624]{1,0:T(2,128)S(1)} %slice_add_fusion.1), channel_id=1, source_target_pairs={{0,4},{1,5},{2,6},{3,7},{4,0},{5,1},{6,2},{7,3},{8,12},{9,13},{10,... | collective-permute-start | bytes 14984 | tf_op jit(solution)/shard_map/ppermute | solution.py:744
  628.2 22.8 %collective-permute-start.28 = (bf16[8,384,128]{2,1,0:T(8,128)(2,1)}, bf16[8,384,128]{2,1,0:T(8,128)(2,1)S(1)}, u32[]{:S(2)}, u32[]{:S(2)}) collective-permute-start(bf16[8,384,128]{2,1,0:T(8,128)(2,1)} %get-tuple-element.228), channel_id=1, source_target_pairs={{0,2},{1,3},{2,0},{3,1},{4,6},{5,7},{6,4},{7,5},{8,10},{9,11},{10,... | collective-permute-start | bytes 2359304 | tf_op jit(solution)/shard_map/ppermute | solution.py:744
  629.3 23.1 %collective-permute-start.24 = (bf16[8,384,128]{2,1,0:T(8,128)(2,1)}, bf16[8,384,128]{2,1,0:T(8,128)(2,1)S(1)}, u32[]{:S(2)}, u32[]{:S(2)}) collective-permute-start(bf16[8,384,128]{2,1,0:T(8,128)(2,1)} %get-tuple-element.223), channel_id=1, source_target_pairs={{0,1},{1,0},{2,3},{3,2},{4,5},{5,4},{6,7},{7,6},{8,9},{9,8},{10,11... | collective-permute-start | bytes 2359304 | tf_op jit(solution)/shard_map/ppermute | solution.py:744
  650.1 12.1 %collective-permute-start.33 = (bf16[4,384,128]{2,1,0:T(8,128)(2,1)S(1)}, bf16[4,384,128]{2,1,0:T(8,128)(2,1)S(1)}, u32[]{:S(2)}, u32[]{:S(2)}) collective-permute-start(bf16[4,384,128]{2,1,0:T(8,128)(2,1)S(1)} %add_convert_fusion.4), channel_id=1, source_target_pairs={{0,1},{1,0},{2,3},{3,2},{4,5},{5,4},{6,7},{7,6},{8,9},{9,8},{10,11... | collective-permute-start | bytes 1179656 | tf_op jit(solution)/shard_map/ppermute | solution.py:744
  651.1 15.3 %collective-permute-start.29 = (bf16[4,384,128]{2,1,0:T(8,128)(2,1)S(1)}, bf16[4,384,128]{2,1,0:T(8,128)(2,1)S(1)}, u32[]{:S(2)}, u32[]{:S(2)}) collective-permute-start(bf16[4,384,128]{2,1,0:T(8,128)(2,1)S(1)} %add_convert_fusion.5), channel_id=1, source_target_pairs={{0,1},{1,0},{2,3},{3,2},{4,5},{5,4},{6,7},{7,6},{8,9},{9,8},{10,11... | collective-permute-start | bytes 1179656 | tf_op jit(solution)/shard_map/ppermute | solution.py:744
  652.5 14.5 %collective-permute-start.25 = (bf16[4,384,128]{2,1,0:T(8,128)(2,1)S(1)}, bf16[4,384,128]{2,1,0:T(8,128)(2,1)S(1)}, u32[]{:S(2)}, u32[]{:S(2)}) collective-permute-start(bf16[4,384,128]{2,1,0:T(8,128)(2,1)S(1)} %add_convert_fusion.6), channel_id=1, source_target_pairs={{0,2},{1,3},{2,0},{3,1},{4,6},{5,7},{6,4},{7,5},{8,10},{9,11},{10,... | collective-permute-start | bytes 1179656 | tf_op jit(solution)/shard_map/ppermute | solution.py:744
  663.2 5.7 collective-permute-start.34
  666.5 7.0 %collective-permute-start.30 = (bf16[2,384,128]{2,1,0:T(8,128)(2,1)S(1)}, bf16[2,384,128]{2,1,0:T(8,128)(2,1)S(1)}, u32[]{:S(2)}, u32[]{:S(2)}) collective-permute-start(bf16[2,384,128]{2,1,0:T(8,128)(2,1)S(1)} %add_convert_fusion.17), channel_id=1, source_target_pairs={{0,4},{1,5},{2,6},{3,7},{4,0},{5,1},{6,2},{7,3},{8,12},{9,13},{10,... | collective-permute-start | bytes 589832 | tf_op jit(solution)/shard_map/ppermute | solution.py:744
  667.2 10.6 %collective-permute-start.26 = (bf16[2,384,128]{2,1,0:T(8,128)(2,1)S(1)}, bf16[2,384,128]{2,1,0:T(8,128)(2,1)S(1)}, u32[]{:S(2)}, u32[]{:S(2)}) collective-permute-start(bf16[2,384,128]{2,1,0:T(8,128)(2,1)S(1)} %add_convert_fusion.18), channel_id=1, source_target_pairs={{0,4},{1,5},{2,6},{3,7},{4,0},{5,1},{6,2},{7,3},{8,12},{9,13},{10,... | collective-permute-start | bytes 589832 | tf_op jit(solution)/shard_map/ppermute | solution.py:744
  669.9 8.2 %collective-permute-start.35 = (bf16[1,384,128]{2,1,0:T(8,128)(2,1)S(1)}, bf16[1,384,128]{2,1,0:T(8,128)(2,1)S(1)}, u32[]{:S(2)}, u32[]{:S(2)}) collective-permute-start(bf16[1,384,128]{2,1,0:T(8,128)(2,1)S(1)} %add_convert_fusion.34), channel_id=1, source_target_pairs={{0,8},{1,9},{2,10},{3,11},{4,12},{5,13},{6,14},{7,15},{8,0},{9,1},... | collective-permute-start | bytes 294920 | tf_op jit(solution)/shard_map/ppermute | solution.py:744
  673.6 7.0 %collective-permute-start.31 = (bf16[1,384,128]{2,1,0:T(8,128)(2,1)S(1)}, bf16[1,384,128]{2,1,0:T(8,128)(2,1)S(1)}, u32[]{:S(2)}, u32[]{:S(2)}) collective-permute-start(bf16[1,384,128]{2,1,0:T(8,128)(2,1)S(1)} %add_convert_fusion.35), channel_id=1, source_target_pairs={{0,8},{1,9},{2,10},{3,11},{4,12},{5,13},{6,14},{7,15},{8,0},{9,1},... | collective-permute-start | bytes 294920 | tf_op jit(solution)/shard_map/ppermute | solution.py:744
  677.8 5.6 collective-permute-start.27
  (147 other events, 3149.8 us)

commit v2 on v1

--- a/solution.py
+++ b/solution.py
@@ -162,7 +162,7 @@
     def __init__(self, layer, own, got, width):
         self.layer, self.own, self.got, self.width = layer, own, got, width
 
-    def cols(self, per, steps):
+    def cols(self, per):
         layer, width = self.layer, self.width
         d = self.own.shape[0]
 
@@ -170,7 +170,7 @@
             return (0, jnp.where(ids[0] == layer, per(j, ids[0]), 0))
 
         def got_map(j, ids, *_):
-            return (0, jnp.where(ids[0] == layer, 0, j))
+            return (0, jnp.where(ids[0] == layer, 0, per(j, ids[0])))
 
         return [(self.own, (d, width), own_map), (self.got, (d, width), got_map)]
 
@@ -182,7 +182,7 @@
             return (jnp.where(ids[0] == layer, per(j, ids[0]), 0), 0)
 
         def got_map(j, ids, *_):
-            return (jnp.where(ids[0] == layer, 0, j), 0)
+            return (jnp.where(ids[0] == layer, 0, per(j, ids[0])), 0)
 
         return [(self.own, (width, d), own_map), (self.got, (width, d), got_map)]
 
@@ -257,8 +257,7 @@
     if not first:
         outs.append(out_whole((t, d), BF))
     ins = [whole(x) for x in stream] + [whole(gain), whole(bias)]
-    ins += wqkv.cols(lambda j, s: 2 * j + s, 3) + wout.rowblocks(lambda j, s: s)[:1]
-    ins += [whole(wout.got)]
+    ins += wqkv.cols(lambda j, s: 2 * j + s) + wout.rowblocks(lambda j, s: s)
     return call(
         f"self_fwd_{layer}", body, (3,), [ids], ins, outs, flops=2 * t * d * 4 * h2 + 2e8
     )
@@ -306,7 +305,7 @@
 
     per = fh // width
     ins = [whole(x), whole(a_own), whole(a_got), whole(gain), whole(bias)]
-    ins += wup.cols(lambda j, s: s * per + j, per)
+    ins += wup.cols(lambda j, s: s * per + j)
     ins += [(b_up, (1, width), lambda j, *_: (0, j))]
     ins += wdown.rowblocks(lambda j, s: s * per + j)
     ins += [whole(b_down)]
@@ -395,7 +394,7 @@
 
     per = fh // width
     ins = [whole(a) for a in lead] + [whole(gain), whole(bias)]
-    ins += wup.cols(lambda j, s: s * per + j, per)
+    ins += wup.cols(lambda j, s: s * per + j)
     ins += [(b_up, (1, width), lambda j, *_: (0, j))]
     ins += wdown.rowblocks(lambda j, s: s * per + j)
     ins += [whole(b_down)]
@@ -686,8 +685,7 @@
         loop(t // 256, back)
 
     ins = [whole(grad), whole(h_own), whole(h_got), whole(x), whole(gain_x), whole(qkv)]
-    ins += wqkv.cols(lambda j, s: 2 * j + s, 3) + wout.rowblocks(lambda j, s: s)[:1]
-    ins += [whole(wout.got)]
+    ins += wqkv.cols(lambda j, s: 2 * j + s) + wout.rowblocks(lambda j, s: s)
     outs = [
         out_whole((t, d), F32),
         out_whole((t, d), BF),
@@ -702,83 +700,120 @@
     )
 
 
-def text_grad(grad, h_own, h_got, x, gain):
+def text_grad(ids, grad, h_own, h_got, x, gain, dz):
     t, d = x.shape
 
-    def body(gr_ref, p_ref, q_ref, x_ref, g_ref, dx_ref, sums_ref):
+    def body(ids_ref, gr_ref, p_ref, q_ref, x_ref, g_ref, dz_ref, dx_ref, sums_ref):
         sums_ref[...] = jnp.zeros_like(sums_ref)
 
         def chunk(i):
             sl = rows(i, CHUNK)
             dh = p_ref[sl, :] + q_ref[sl, :].astype(F32)
             dv, dhn = norm_grad(x_ref[sl, :].astype(F32), g_ref[...], dh)
-            dx_ref[sl, :] = gr_ref[sl, :] + dv
+            dx_ref[sl, :] = jnp.where(ids_ref[0] == 0, gr_ref[sl, :] + dv, dz_ref[sl, :].astype(F32))
             sums_ref[0] += fold(dhn)
             sums_ref[1] += fold(dh)
 
         loop(t // CHUNK, chunk)
 
-    ins = [whole(a) for a in (grad, h_own, h_got, x, gain)]
+    ins = [whole(a) for a in (grad, h_own, h_got, x, gain, dz)]
     outs = [out_whole((t, d), F32), out_whole((2, 8, d), F32)]
-    return call("text_grad", body, (1,), [], ins, outs)
-
-
-def orders(count):
-    bits = [1 << i for i in range(count.bit_length() - 1)]
-    third = [bits[2], bits[0], bits[1]] + bits[3:]
-    return [bits, [bits[1], bits[0]] + bits[2:], third]
-
-
-def pieces(order, count):
-    result, left = [], list(range(count))
-    rank = lambda r: [0 if r & b else 1 for b in order]
-    for bit in order:
-        result.append(sorted([r for r in left if r & bit], key=rank))
-        left = [r for r in left if not r & bit]
-    return result + [left]
-
-
-def halving(parts, order, sent=BF):
-    count = lax.axis_size("dp")
-    for step, bit in enumerate(order):
-        arrived = lax.ppermute(parts[step].astype(sent), "dp", [(i, i ^ bit) for i in range(count)])
-        at = 0
-        for later in range(step + 1, len(parts)):
-            size = parts[later].shape[0]
-            parts[later] = parts[later].astype(F32) + arrived[at : at + size].astype(F32)
-            at += size
-    return parts[-1][0].astype(F32)
+    return call("text_grad", body, (1,), [ids], ins, outs)
+
+
+def paths(count, turn):
+    bits = list(range(count.bit_length() - 1))
+    near, far = bits[:3], bits[3:]
+    return [near[k % 3 :] + near[: k % 3] + far for k in (turn, turn + 1)]
+
+
+def route(s, me, count, turn):
+    first, second = paths(count, turn)
+    bits = [jnp.where(s == 0, a, b) for a, b in zip(first, second)]
+    return jnp.stack([s, me] + bits).astype(jnp.int32)
+
+
+def tie(value, *after):
+    return lax.optimization_barrier((value, *after))[0]
+
+
+class Sum:
+    def __init__(self, parts, count, turn, own_order=True):
+        self.parts, self.count, self.paths = parts, count, paths(count, turn)
+        if not own_order:
+            self.paths = [self.paths[0]] * 2
+        self.arrived, self.result = [], None
+        self.send(parts[0])
+
+    def send(self, value):
+        self.outgoing = value
+        step, n = len(self.arrived), self.count
+        perm = [(s * n + i, s * n + (i ^ (1 << self.paths[s][step]))) for s in range(2) for i in range(n)]
+        self.flight = lax.ppermute(value, ("section", "dp"), perm)
+
+    def land(self, *after):
+        if self.result is not None:
+            return
+        self.arrived.append(tie(self.flight, *after) if after else self.flight)
+        step = len(self.arrived)
+        low = self.count >> (step + 1)
+        high = max(2 * low, 1)
+        total = self.parts[step].astype(F32)
+        for a in self.arrived:
+            total = total + a[low:high].astype(F32)
+        if step < len(self.parts) - 1:
+            self.send(total.astype(self.parts[0].dtype))
+        else:
+            self.result = self.outgoing = total[0]
+
+
+def finish(sums):
+    while any(x.result is None for x in sums):
+        for x in sums:
+            x.land()
+
+
+def slots(outs, scr):
+    high = scr.shape[0]
+    for out in outs[:-1]:
+        low = high // 2
+
+        def one(i, out=out, low=low):
+            out[i] = scr[low + i].astype(BF)
+
+        loop(high - low, one)
+        high = low
+    outs[-1][0] = scr[0].astype(BF)
+
+
+def putter(ids_ref, scr):
+    def put(dest, first, block):
+        rel, slot = dest ^ ids_ref[1], 0
+        for k in range(scr.shape[0].bit_length() - 1):
+            slot = slot * 2 + ((rel >> ids_ref[2 + k]) & 1)
+        scr[slot, pl.ds(first, block.shape[0]), :] = block.astype(scr.dtype)
+
+    return put
+
+
+def slot_outs(count, row_count, cols):
+    steps = count.bit_length() - 1
+    sizes = [count >> k for k in range(1, steps + 1)] + [1]
+    return [out_whole((n, row_count, cols), BF) for n in sizes]
 
 
 def weight_kernel(name, ids, ins, row_count, count, fill, flops):
     cols = 3 * LANES
-    plan = [pieces(o, count) for o in orders(count)]
-    flat = [(k, piece) for k in range(3) for piece in plan[k]]
 
     def body(ids_ref, *refs):
         scr = refs[-1]
-        me = ids_ref[1]
-
-        def put(dest, first, block):
-            scr[dest ^ me, pl.ds(first, block.shape[0]), :] = block
-
-        fill(ids_ref, refs[: len(ins)], put)
-        for out, (k, piece) in zip(refs[len(ins) : -1], flat):
-            for at, rel in enumerate(piece):
-                out[at] = scr[rel, :, k * LANES : (k + 1) * LANES].astype(BF)
-
-    outs = [out_whole((len(piece), row_count, LANES), BF) for _, piece in flat]
-    got = call(
-        name, body, (1,), [ids], [whole(a) for a in ins], outs,
-        scratch=[pltpu.VMEM((count, row_count, cols), F32)], flops=flops,
-    )
-    step = len(plan[0])
-    return [got[i * step : (i + 1) * step] for i in range(3)]
-
-
-def reduced(parts, count):
-    sums = [halving(list(p), o) for p, o in zip(parts, orders(count))]
-    return jnp.concatenate(sums, -1)
+        fill(ids_ref, refs[: len(ins)], putter(ids_ref, scr))
+        slots(refs[len(ins) : -1], scr)
+
+    return call(
+        name, body, (1,), [ids], [whole(a) for a in ins], slot_outs(count, row_count, cols),
+        scratch=[pltpu.VMEM((count, row_count, cols), BF)], flops=flops,
+    )
 
 
 def up_down_weights(layer, ids, normed, du, act_own, act_got, dm, count):
@@ -845,42 +880,17 @@
     )
 
 
-def cross_weights(ids, h, dcq, att_own, att_got, dc, count):
-    t, d = h.shape
-    h2 = d // 2
-    each = h2 // count
-
-    def fill(ids_ref, refs, put):
-        h_ref, dcq_ref, own_ref, got_ref, dc_ref = refs
-        w = tn(h_ref[...], dcq_ref[...])
-        for half in range(2):
-            for dest in range(count):
-                at = half * h2 + dest * each
-                put(dest, half * each, w[at : at + each])
-        s = ids_ref[0]
-        dc_half = dc_ref[:, lane(s * h2, h2)]
-        for ref, side in ((own_ref, s), (got_ref, 1 - s)):
-            w = tn(ref[...], dc_half)
-            for dest in range(count):
-                put(dest, pl.multiple_of((2 + side) * each, each), w[dest * each : (dest + 1) * each])
-
-    return weight_kernel(
-        "cross_weights", ids, [h, dcq, att_own, att_got, dc], 4 * each, count, fill, 4 * t * d * h2
-    )
-
-
-def key_value_weights(ids, r_own, r_got, g_own, g_got, count):
+def cross_weights(ids, h, dcq, att_own, att_got, dc, r_own, r_got, g_own, g_got, count):
+    t = h.shape[0]
     caps, half, d = r_own.shape
     h2 = d // 2
     each = h2 // count
-    cols = 3 * LANES
-    plan = [pieces(o, count) for o in orders(count)]
-    flat = [(k, piece) for k in range(3) for piece in plan[k]]
-
-    def body(ids_ref, ro, rg, go, gg, *refs):
-        outs, scr, acc = refs[:-2], refs[-2], refs[-1]
+    n_in = 9
+
+    def body(ids_ref, *refs):
+        h_ref, dcq_ref, own_ref, got_ref, dc_ref, ro, rg, go, gg = refs[:n_in]
+        outs, scr, acc = refs[n_in:-2], refs[-2], refs[-1]
         c = pl.program_id(0)
-        me = ids_ref[1]
 
         @pl.when(c == 0)
         def _():
@@ -894,28 +904,63 @@
 
         @pl.when(c == pl.num_programs(0) - 1)
         def _():
+            put = putter(ids_ref, scr)
+            w = tn(h_ref[...], dcq_ref[...])
+            for half_row in range(2):
+                for dest in range(count):
+                    at = half_row * h2 + dest * each
+                    put(dest, half_row * each, w[at : at + each])
+            s = ids_ref[0]
+            dc_half = dc_ref[:, lane(s * h2, h2)]
+            for ref, side in ((own_ref, s), (got_ref, 1 - s)):
+                w = tn(ref[...], dc_half)
+                for dest in range(count):
+                    put(dest, pl.multiple_of((2 + side) * each, each), w[dest * each : (dest + 1) * each])
             for kind in range(2):
                 for part in range(2):
                     for dest in range(count):
                         at = part * h2 + dest * each
-                        first = (2 * kind + part) * each
-                        scr[dest ^ me, first : first + each, :] = acc[
-                            at : at + each, kind * h2 : (kind + 1) * h2
-                        ]
-            for out, (k, piece) in zip(outs, flat):
-                for at, rel in enumerate(piece):
-                    out[at] = scr[rel, :, k * LANES : (k + 1) * LANES].astype(BF)
+                        put(
+                            dest, (4 + 2 * kind + part) * each,
+                            acc[at : at + each, kind * h2 : (kind + 1) * h2],
+                        )
+            slots(outs, scr)
 
     blk = ((1, half, d), lambda c, *_: (c, 0, 0))
-    ins = [(a,) + blk for a in (r_own, r_got, g_own, g_got)]
-    outs = [out_whole((len(piece), 4 * each, LANES), BF) for _, piece in flat]
-    got = call(
-        "key_value_weights", body, (caps,), [ids], ins, outs,
-        scratch=[pltpu.VMEM((count, 4 * each, cols), F32), pltpu.VMEM((d, d), F32)],
+    ins = [whole(a) for a in (h, dcq, att_own, att_got, dc)]
+    ins += [(a,) + blk for a in (r_own, r_got, g_own, g_got)]
+    return call(
+        "cross_weights", body, (caps,), [ids], ins, slot_outs(count, 8 * each, h2),
+        scratch=[pltpu.VMEM((count, 8 * each, h2), F32), pltpu.VMEM((d, d), F32)],
         flops=4 * caps * half * d * d,
     )
-    step = len(plan[0])
-    return [got[i * step : (i + 1) * step] for i in range(3)]
+
+
+def pack_vectors(vectors):
+    width = sum(v.shape[1] for v in vectors)
+
+    def body(*refs):
+        at = 0
+        for ref in refs[:-1]:
+            refs[-1][:, at : at + ref.shape[1]] = ref[...]
+            at += ref.shape[1]
+
+    return call("pack_vectors", body, (1,), [], [whole(v) for v in vectors], [out_whole((1, width), F32)])[0]
+
+
+def choose_vectors(ids, own, got, d, fh):
+    def body(ids_ref, own_ref, got_ref, *outs):
+        s = ids_ref[0]
+        for layer in range(2):
+            pick_one = lambda a, b: jnp.where(s == layer, own_ref[:, a:b], got_ref[:, a:b])
+            for i in range(5):
+                outs[6 * layer + i][...] = pick_one(i * d, (i + 1) * d)
+            low, high = pick_one(5 * d, 5 * d + fh), pick_one(5 * d + fh, 5 * d + 2 * fh)
+            outs[6 * layer + 5][...] = jnp.where(s == 0, low, high)
+
+    outs = [out_whole((1, n), F32) for _ in range(2) for n in [d] * 5 + [fh]]
+    got = call("choose_vectors", body, (1,), [ids], [whole(own), whole(got)], outs)
+    return got[:6], got[6:]
 
 
 def plain_sums(s, count, mlp2, cross, attn2, mlp1, image, attn1):
@@ -976,26 +1021,14 @@
     fh = ff // 2
     other = 1 - s
 
+    fast = d // count == 48
     w_qkv, w_out, w_up, w_down = qkv_weight[0], attn_out_weight[0], up_weight[0], down_weight[0]
-    vec_own = jnp.concatenate(
-        [attn_norm_gain, attn_norm_bias, mlp_norm_gain, mlp_norm_bias, down_bias, up_bias], 1
+    vec_own = pack_vectors(
+        [attn_norm_gain, attn_norm_bias, mlp_norm_gain, mlp_norm_bias, down_bias, up_bias]
     )
     vec_got = swap(vec_own)
-    got_qkv = swap(
-        jnp.concatenate(
-            [lax.dynamic_slice(w_qkv, (0, (2 * j + other) * h2), (d, h2)) for j in range(3)], 1
-        )
-    )
-    got_out = swap(lax.dynamic_slice(w_out, (other * h2, 0), (h2, d)))
-    got_up = swap(lax.dynamic_slice(w_up, (0, other * fh), (d, fh)))
-    got_down = swap(lax.dynamic_slice(w_down, (other * fh, 0), (fh, d)))
-
-    vectors = []
-    for layer in range(2):
-        v = jnp.where(s == layer, vec_own, vec_got)
-        parts = [v[:, i * d : (i + 1) * d] for i in range(5)]
-        parts.append(lax.dynamic_slice(v, (0, 5 * d + s * fh), (1, fh)))
-        vectors.append(parts)
+    got_qkv, got_out, got_up, got_down = swap(w_qkv), swap(w_out), swap(w_up), swap(w_down)
+    vectors = choose_vectors(ids, vec_own, vec_got, d, fh)
     halves = []
     for layer in range(2):
         halves.append(
@@ -1030,31 +1063,63 @@
     y = z3 + mpart + swap(msend).astype(F32)
     layer_out = jnp.where(s == 0, z, y.astype(BF))
 
+    turned = [route(s, me, count, turn) for turn in range(3)] if fast else None
+    live = []
+
+    def begin(parts, turn):
+        live.append(Sum(parts, count, turn))
+        return live[-1]
+
+    def step(*after):
+        for x in live:
+            x.land(*after)
+
+    def after_live(value, *more):
+        return tie(value, *[x.outgoing for x in live], *more) if fast else value
+
+    if fast:
+        m2 = begin(up_down_weights(1, turned[0], n2, du2, act2, swap(act2), cotangent, count), 0)
     (dz3, dc, dcq, dkv_own, dkv_send, cpart, csend, sums_n2) = cross_grad(
-        ids, image_counts, cotangent, dpart, swap(dsend), z3, mg2, cq, cross_query, cross_out, kv_own, kv_got
-    )
+        ids, image_counts, cotangent, dpart, after_live(swap(dsend)), z3, mg2, cq, cross_query, cross_out,
+        kv_own, kv_got,
+    )
+    dkv_mine = swap(dkv_send)
+    if fast:
+        parts = cross_weights(
+            turned[2], ch, dcq, catt, swap(catt), dc, r_own, r_got, dkv_own, dkv_send, count
+        )
+        step(parts[-1])
+        ckv = begin(parts, 2)
     dz2, da2, dqkv2, hpart, hsend, sums_c = self_grad(
-        1, ids, dz3, cpart, swap(csend), z2, gain_t, qkv2, qw2, ow2
-    )
+        1, ids, dz3, cpart, after_live(swap(csend)), z2, gain_t, qkv2, qw2, ow2
+    )
+    if fast:
+        step(sums_c)
+        parts = self_weights(1, turned[1], h2n, dqkv2, att2, swap(att2), da2, count)
+        a2 = begin(parts, 1)
     act1, du1, npart, nsend, sums_a2, bup1, dz = mlp_grad(
-        0, ids, [dz2, hpart, swap(hsend), z, ag2, n1], mg1, mb1, uw1, bu1, dw1, bd1
-    )
+        0, ids, [dz2, hpart, after_live(swap(hsend)), z, ag2, n1], mg1, mb1, uw1, bu1, dw1, bd1
+    )
+    if fast:
+        step(sums_a2)
+        parts = up_down_weights(0, turned[0], n1, du1, act1, after_live(swap(act1)), dz, count)
+        m1 = begin(parts, 0)
     dx1, da1, dqkv1, hpart, hsend, sums_n1 = self_grad(
-        0, ids, dz, npart, swap(nsend), x1, mg1, qkv1, qw1, ow1
-    )
-    dtext, sums_a1 = text_grad(dx1, hpart, swap(hsend), text, ag1)
-
-    dkv_mine = swap(dkv_send)
-    image_grad, sums_i = key_value_grad(ids, image, gain_i, dkv_own, dkv_mine, cross_key_value)
-    input_grad = jnp.where(s == 0, dtext, dz.astype(F32))
-
-    if d // count == 48:
-        m2 = reduced(up_down_weights(1, ids, n2, du2, act2, swap(act2), cotangent, count), count)
-        c2 = reduced(cross_weights(ids, ch, dcq, catt, swap(catt), dc, count), count)
-        a2 = reduced(self_weights(1, ids, h2n, dqkv2, att2, swap(att2), da2, count), count)
-        m1 = reduced(up_down_weights(0, ids, n1, du1, act1, swap(act1), dz, count), count)
-        kv = reduced(key_value_weights(ids, r_own, r_got, dkv_own, dkv_send, count), count)
-        a1 = reduced(self_weights(0, ids, h1, dqkv1, att1, swap(att1), da1, count), count)
+        0, ids, dz, npart, after_live(swap(nsend)), x1, mg1, qkv1, qw1, ow1
+    )
+    if fast:
+        step(sums_n1)
+        parts = self_weights(0, turned[2], h1, dqkv1, att1, after_live(swap(att1)), da1, count)
+        a1 = begin(parts, 2)
+    input_grad, sums_a1 = text_grad(ids, dx1, hpart, after_live(swap(hsend)), text, ag1, dz)
+    image_grad, sums_i = key_value_grad(
+        ids, image, gain_i, dkv_own, after_live(dkv_mine, sums_a1), cross_key_value
+    )
+    if fast:
+        step(sums_i)
+        finish(live)
+        m2, ckv, a2, m1, a1 = [x.result for x in live]
+        c2, kv = ckv[: 2 * d // count], ckv[2 * d // count :]
     else:
         m2, c2, a2, m1, kv, a1 = plain_sums(
             s, count, (n2, du2, act2, cotangent), (ch, dcq, catt, dc), (h2n, dqkv2, att2, da2),
@@ -1110,9 +1175,18 @@
         split(sums_i[0]), split(sums_c[0]), split(sums_i[1]), split(sums_c[1]),
     ]
     widths = [v.shape[1] for v in packed]
-    packed = jnp.take(jnp.concatenate(packed, 1), jnp.arange(count, dtype=jnp.int32) ^ me, axis=0)
-    order = orders(count)[0]
-    vec = halving([packed[jnp.array(p)] for p in pieces(order, count)], order, F32)
+    packed = jnp.concatenate(packed, 1)
+    if fast:
+        packed = packed[:, None]
+        order = paths(count, 0)[0]
+        table = [sum(((r >> (len(order) - 1 - k)) & 1) << b for k, b in enumerate(order)) for r in range(count)]
+        packed = jnp.take(packed, jnp.array(table, jnp.int32) ^ me, axis=0)
+        split_at = [(count >> (k + 1), count >> k) for k in range(len(order))] + [(0, 1)]
+        total = Sum([packed[a:b] for a, b in split_at], count, 0, own_order=False)
+        finish([total])
+        vec = total.result[0]
+    else:
+        vec = lax.psum_scatter(packed, "dp", scatter_dimension=0, tiled=True)[0]
     cut, at = [], 0
     for w in widths:
         cut.append(vec[at : at + w])

time: 700 us -> 456 us (0.65); the launches traced: 689 us -> 455 us
  waiting for transfers between devices: 215 us -> 61.2 us
  starting transfers between devices: 108 us -> 41.7 us
  local copies, waits for them, and re-layouts: 31.9 us -> 19.7 us
    ppermute x76 -> x24, waiting for transfers between devices: 205 us -> 48.1 us  [send(): self.flight = lax.ppermute(value, ('section', 'dp'), perm)]
    ppermute x76 -> x24, starting transfers between devices: 101 us -> 36.2 us  [send(): self.flight = lax.ppermute(value, ('section', 'dp'), perm)]
    dynamic_slice x10 -> x0, local copies, waits for them, and re-layouts: 8.13 us -> none  [the longest x1 3.42 us: on_device(): got_up = swap(lax.dynamic_slice(w_up, (0, other * fh), (d, fh)))]
    unnamed x230 -> x103, local copies, waits for them, and re-layouts: 15.5 us -> 8.32 us
    pallas_call x18 -> x19, Pallas kernels: 285 us -> 288 us  [call(): pl.pallas_call(body, name=name, out_shape=shapes, grid_spec=pltpu.Prefetc...]
    convert_element_type x54 -> x15, other arithmetic: 23.5 us -> 24.1 us  [land(): self.send(total.astype(self.parts[0].dtype))]
  transfers between devices with their start and end apart: 103 -> 51, of which waited for: 66 -> 19; matrix products, arithmetic and copies ran while one was open for 9% -> 11% of each run, Pallas kernels for 41% -> 54%
where the time goes in v2:
time: 456 us; the launch traced here: 455 us
  Pallas kernels  288 us (63%)
  waiting for transfers between devices  61.2 us (13%)
  other arithmetic  42.6 us (9%)
  starting transfers between devices  41.7 us (9%)
  local copies, waits for them, and re-layouts  19.7 us (4%)
    pallas_call x19, Pallas kernels, call(): pl.pallas_call(body, name=name, out_shape=shapes, grid_spec=pltpu.Prefetc...  288 us
    ppermute x24, waiting for transfers between devices, send(): self.flight = lax.ppermute(value, ('section', 'dp'), perm)  48.1 us
    ppermute x24, starting transfers between devices, send(): self.flight = lax.ppermute(value, ('section', 'dp'), perm)  36.2 us
    convert_element_type x15, other arithmetic, land(): self.send(total.astype(self.parts[0].dtype))  24.1 us
    ppermute x27, waiting for transfers between devices, swap(): return lax.ppermute(value, 'section', [(0, 1), (1, 0)])  13 us
  transfers between devices with their start and end apart: 51, of which 19 were waited for; matrix products, arithmetic and copies ran while one was open for 11% of the time, Pallas kernels for 54%

profile of v2, /device:TPU:0, one launch (start us, length us, event | category | flops | bytes accessed | tf_op | source)
XLA Modules:
  0.0 454.8 jit_solution(1995077549533006539)
XLA Ops:
  1.7 1.4 pack_vectors.1.own_ref
  4.2 1.4 fusion.16
  5.6 17.6 %key_value.1 = (bf16[8,288,768]{2,1,0:T(8,128)(2,1)}, bf16[8,288,768]{2,1,0:T(8,128)(2,1)}, bf16[8,288,768]{2,1,0:T(8,128)(2,1)}) custom-call(s32[2]{0:T(128)} %pad_add_fusion.ids_ref, bf16[8,288,768]{2,1,0:T(8,128)(2,1)} %im_ref.3, f32[1,768]{1,0:T(1,128)} %get-tuple-element.313.g_ref, f32[1,768]{1,0:T(1,128)} %get-tuple-element.299.b_ref, ...), custom_call_target="tpu_custom_call" | custom-call | flops 5435817984 | bytes 23599104 | tf_op jit(solution)/shard_map/key_value/pallas_call | solution.py:137
  23.4 2.1 choose_vectors.1
  25.5 1.8 copy-done
  27.2 13.2 %self_fwd_0.1 = (bf16[512,768]{1,0:T(8,128)(2,1)}, bf16[3,512,384]{2,1,0:T(8,128)(2,1)}, bf16[512,384]{1,0:T(8,128)(2,1)}, f32[512,768]{1,0:T(8,128)}, bf16[512,768]{1,0:T(8,128)(2,1)}) custom-call(s32[2]{0:T(128)} %pad_add_fusion.ids_ref, bf16[512,768]{1,0:T(8,128)(2,1)} %x_ref.3, f32[1,768]{1,0:T(1,128)} %get-tuple-element.142.refs_1_.g_ref, ...), custom_call_target="tpu_custom_call" | custom-call | flops 1407959552 | bytes 14948352 | tf_op jit(solution)/shard_map/self_fwd_0/pallas_call | solution.py:137
  40.9 2.1 collective-permute-done.3.q_ref
  43.9 16.3 %mlp_fwd_0.1 = (f32[512,768]{1,0:T(8,128)}, bf16[512,768]{1,0:T(8,128)(2,1)}, f32[512,768]{1,0:T(8,128)}, bf16[512,768]{1,0:T(8,128)(2,1)}) custom-call(s32[2]{0:T(128)} %pad_add_fusion.ids_ref, bf16[512,768]{1,0:T(8,128)(2,1)} %x_ref.3, f32[512,768]{1,0:T(8,128)} %get-tuple-element.144.p_ref, bf16[512,768]{1,0:T(8,128)(2,1)} %copy-done.8, ...), custom_call_target="tpu_custom_call" | custom-call | flops 2415919104 | bytes 26754048 | tf_op jit(solution)/shard_map/mlp_fwd_0/pallas_call | solution.py:137
  60.5 2.1 collective-permute-done.6.refs_2_
  63.5 14.6 %self_fwd_1.1 = (bf16[512,768]{1,0:T(8,128)(2,1)}, bf16[3,512,384]{2,1,0:T(8,128)(2,1)}, bf16[512,384]{1,0:T(8,128)(2,1)}, f32[512,768]{1,0:T(8,128)}, bf16[512,...) custom-call(s32[2]{0:T(128)} %pad_add_fusion.ids_ref, f32[512,768]{1,0:T(8,128)} %get-tuple-element.150.refs_0_.x_ref, ...), custom_call_target="tpu_custom_call" | custom-call | flops 1407959552 | bytes 18880512 | tf_op jit(solution)/shard_map/self_fwd_1/pallas_call | solution.py:137
  78.5 2.1 collective-permute-done.7.q_ref
  81.5 20.0 %cross_fwd.1 = (f32[512,768]{1,0:T(8,128)}, bf16[512,768]{1,0:T(8,128)(2,1)}, bf16[512,384]{1,0:T(8,128)(2,1)}, bf16[512,384]{1,0:T(8,128)(2,1)}, f32[512,768]{1,0:T(8,128)}, /*index=5*/bf16[512,768]{1,0:T(8,128)(2,1)}) custom-call(s32[2]{0:T(128)} %pad_add_fusion.ids_ref, s32[8]{0:T(128)} %cnt_ref.3, bf16[512,768]{1,0:T(8,128)(2,1)} %get-tuple-element.155.z_ref.refs_3_, ...), custom_call_target="tpu_custom_call" | custom-call | flops 2203979776 | bytes 18094080 | tf_op jit(solution)/shard_map/cross_fwd/pallas_call | solution.py:137
  101.8 2.1 collective-permute-done.9.refs_2_
  104.8 23.7 %mlp_grad_1.1 = (bf16[512,1536]{1,0:T(8,128)(2,1)}, bf16[512,1536]{1,0:T(8,128)(2,1)}, f32[512,768]{1,0:T(8,128)}, bf16[512,768]{1,0:T(8,128)(2,1)}, f32[3,8,768...) custom-call(s32[2]{0:T(128)} %pad_add_fusion.ids_ref, ...), custom_call_target="tpu_custom_call" | custom-call | flops 4831838208 | bytes 33954816 | tf_op jit(solution)/shard_map/mlp_grad_1/pallas_call | solution.py:137
  129.7 2.6 collective-permute-done.12.refs_3_
  133.4 11.0 %mlp_weights_1.1 = (bf16[8,384,384]{2,1,0:T(8,128)(2,1)}, bf16[4,384,384]{2,1,0:T(8,128)(2,1)}, bf16[2,384,384]{2,1,0:T(8,128)(2,1)}, bf16[1,384,384]{2,1,0:T(8,128)(2,1)}, bf16[1,384,384]{2,1,0:T(8,128)(2,1)}) custom-call(s32[6]{0:T(128)} %stack.66.ids_ref, bf16[512,768]{1,0:T(8,128)(2,1)} %get-tuple-element.172.refs_0_, ...), custom_call_target="tpu_custom_call" | custom-call | flops 2415919104 | bytes 11010048 | tf_op jit(solution)/shard_map/mlp_weights_1/pallas_call | solution.py:137
  144.5 2.8 collective-permute-start.14
  149.6 27.0 %cross_grad.1 = (f32[512,768]{1,0:T(8,128)}, bf16[512,768]{1,0:T(8,128)(2,1)}, bf16[512,384]{1,0:T(8,128)(2,1)}, bf16[8,288,768]{2,1,0:T(8,128)(2,1)}, bf16[8,28...) custom-call(s32[2]{0:T(128)} %pad_add_fusion.ids_ref, s32[8]{0:T(128)} %cnt_ref.3, ...), custom_call_target="tpu_custom_call" | custom-call | flops 5603979776 | bytes 26790912 | tf_op jit(solution)/shard_map/cross_grad/pallas_call | solution.py:137
  177.4 21.7 %cross_weights.1 = (bf16[8,192,384]{2,1,0:T(8,128)(2,1)}, bf16[4,192,384]{2,1,0:T(8,128)(2,1)}, bf16[2,192,384]{2,1,0:T(8,128)(2,1)}, bf16[1,192,384]{2,1,0:T(8,128)(2,1)}, bf16[1,192,384]{2,1,0:T(8,128)(2,1)}) custom-call(s32[6]{0:T(128)} %stack.67.ids_ref, bf16[512,768]{1,0:T(8,128)(2,1)} %get-tuple-element.182.refs_0_, ...), custom_call_target="tpu_custom_call" | custom-call | flops 5435817984 | bytes 19267584 | tf_op jit(solution)/shard_map/cross_weights/pallas_call | solution.py:137
  199.2 1.6 collective-permute-start.19
  201.1 1.6 collective-permute-start.18
  203.9 19.6 %self_grad_1.1 = (f32[512,768]{1,0:T(8,128)}, bf16[512,768]{1,0:T(8,128)(2,1)}, bf16[3,512,384]{2,1,0:T(8,128)(2,1)}, f32[512,768]{1,0:T(8,128)}, bf16[512,768]{1,0:T(8,128)(2,1)}, /*index=5*/f32[2,8,768]{2,1,0:T(8,128)}) custom-call(s32[2]{0:T(128)} %pad_add_fusion.ids_ref, f32[512,768]{1,0:T(8,128)} %get-tuple-element.178.gr_ref, ...), custom_call_target="tpu_custom_call" | custom-call | flops 1707959552 | bytes 22072320 | tf_op jit(solution)/shard_map/self_grad_1/pallas_call | solution.py:137
  224.3 2.8 collective-permute-done.19
  227.1 6.8 %self_weights_1.1 = (bf16[8,192,384]{2,1,0:T(8,128)(2,1)}, bf16[4,192,384]{2,1,0:T(8,128)(2,1)}, bf16[2,192,384]{2,1,0:T(8,128)(2,1)}, bf16[1,192,384]{2,1,0:T(8,128)(2,1)}, bf16[1,192,384]{2,1,0:T(8,128)(2,1)}) custom-call(s32[6]{0:T(128)} %stack.68.ids_ref, bf16[512,768]{1,0:T(8,128)(2,1)} %get-tuple-element.202.refs_0_, ...), custom_call_target="tpu_custom_call" | custom-call | flops 1207959552 | bytes 5898240 | tf_op jit(solution)/shard_map/self_weights_1/pallas_call | solution.py:137
  233.8 1.8 collective-permute-start.24
  235.6 2.0 add_convert_fusion.6
  237.6 2.1 add_convert_fusion.7
  239.7 21.7 %mlp_grad_0.1 = (bf16[512,1536]{1,0:T(8,128)(2,1)}, bf16[512,1536]{1,0:T(8,128)(2,1)}, f32[512,768]{1,0:T(8,128)}, bf16[512,768]{1,0:T(8,128)(2,1)}, f32[3,8,768...) custom-call(s32[2]{0:T(128)} %pad_add_fusion.ids_ref, f32[512,768]{1,0:T(8,128)} %get-tuple-element.194.refs_0_, ...), custom_call_target="tpu_custom_call" | custom-call | flops 3623878656 | bytes 30812160 | tf_op jit(solution)/shard_map/mlp_grad_0/pallas_call | solution.py:137
  261.9 2.3 collective-permute-start.22
  264.2 13.3 %collective-permute-done.23 = bf16[4,192,384]{2,1,0:T(8,128)(2,1)S(1)} collective-permute-done((bf16[4,192,384]{2,1,0:T(8,128)(2,1)}, bf16[4,192,384]{2,1,0:T(8,128)(2,1)S(1)}, u32[]{:S(2)}, u32[]{:S(2)}) %collective-permute-start.23) | collective-permute-done | bytes 589856 | tf_op jit(solution)/shard_map/ppermute | solution.py:752
  277.5 2.2 add_convert_fusion.5
  279.7 1.8 add_convert_fusion.11
  281.5 1.9 add_convert_fusion.12
  283.5 11.0 %mlp_weights_0.1 = (bf16[8,384,384]{2,1,0:T(8,128)(2,1)}, bf16[4,384,384]{2,1,0:T(8,128)(2,1)}, bf16[2,384,384]{2,1,0:T(8,128)(2,1)}, bf16[1,384,384]{2,1,0:T(8,128)(2,1)}, bf16[1,384,384]{2,1,0:T(8,128)(2,1)}) custom-call(s32[6]{0:T(128)} %stack.66.ids_ref, bf16[512,768]{1,0:T(8,128)(2,1)} %get-tuple-element.208.refs_5_.refs_0_, ...), custom_call_target="tpu_custom_call" | custom-call | flops 2415919104 | bytes 11010048 | tf_op jit(solution)/shard_map/mlp_weights_0/pallas_call | solution.py:137
  296.1 3.3 fusion.1
  301.6 2.1 collective-permute-start.29
  303.7 2.6 collective-permute-start.27
  306.6 19.9 %self_grad_0.1 = (f32[512,768]{1,0:T(8,128)}, bf16[512,768]{1,0:T(8,128)(2,1)}, bf16[3,512,384]{2,1,0:T(8,128)(2,1)}, f32[512,768]{1,0:T(8,128)}, bf16[512,768]{1,0:T(8,128)(2,1)}, /*index=5*/f32[2,8,768]{2,1,0:T(8,128)}) custom-call(s32[2]{0:T(128)} %pad_add_fusion.ids_ref, bf16[512,768]{1,0:T(8,128)(2,1)} %get-tuple-element.209.refs_4_.gr_ref.dz_ref, ...), custom_call_target="tpu_custom_call" | custom-call | flops 1707959552 | bytes 21285888 | tf_op jit(solution)/shard_map/self_grad_0/pallas_call | solution.py:137
  326.5 2.1 collective-permute-start.28
  328.6 1.4 add_bitcast_fusion.1
  330.1 1.9 add_convert_fusion.10
  333.3 2.0 collective-permute-start.46
  335.3 1.7 add_convert_fusion.15
  337.6 1.4 reshape.149
  339.0 1.4 reshape.150
  340.7 2.6 add_convert_fusion
  344.0 6.7 %self_weights_0.1 = (bf16[8,192,384]{2,1,0:T(8,128)(2,1)}, bf16[4,192,384]{2,1,0:T(8,128)(2,1)}, bf16[2,192,384]{2,1,0:T(8,128)(2,1)}, bf16[1,192,384]{2,1,0:T(8,128)(2,1)}, bf16[1,192,384]{2,1,0:T(8,128)(2,1)}) custom-call(s32[6]{0:T(128)} %stack.67.ids_ref, bf16[512,768]{1,0:T(8,128)(2,1)} %get-tuple-element.237.refs_0_, ...), custom_call_target="tpu_custom_call" | custom-call | flops 1207959552 | bytes 5898240 | tf_op jit(solution)/shard_map/self_weights_0/pallas_call | solution.py:137
  351.4 6.8 %text_grad.1 = (f32[512,768]{1,0:T(8,128)}, f32[2,8,768]{2,1,0:T(8,128)}) custom-call(s32[2]{0:T(128)} %pad_add_fusion.ids_ref, f32[512,768]{1,0:T(8,128)} %get-tuple-element.225.gr_ref, f32[512,768]{1,0:T(8,128)} %get-tuple-element.226.p_ref, bf16[512,768]{1,0:T(8,128)(2,1)} %collective-permute-done.26.q_ref, bf16[512,768]{1,0:T(8,128)(2,1)} %x_ref.3, ...), custom_call_target="tpu_custom_call" | custom-call | bytes 7130112 | tf_op jit(solution)/shard_map/text_grad/pallas_call | solution.py:137
  358.2 27.3 %key_value_grad.1 = (f32[8,288,768]{2,1,0:T(8,128)}, f32[2,8,768]{2,1,0:T(8,128)}) custom-call(s32[2]{0:T(128)} %pad_add_fusion.ids_ref, bf16[8,288,768]{2,1,0:T(8,128)(2,1)} %im_ref.3, f32[1,768]{1,0:T(1,128)} %get-tuple-element.313.g_ref, bf16[8,288,768]{2,1,0:T(8,128)(2,1)} %get-tuple-element.187.refs_7_.own_ref, ...), custom_call_target="tpu_custom_call" | custom-call | flops 5435817984 | bytes 27184128 | tf_op jit(solution)/shard_map/key_value_grad/pallas_call | solution.py:137
  385.5 1.7 add_convert_fusion.13
  388.3 2.6 collective-permute-start.47
  395.2 1.3 convert_add_fusion
  396.5 1.8 collective-permute-done.35
  399.1 2.9 collective-permute-done.36
  402.0 1.3 collective-permute-start.37
  403.4 2.3 collective-permute-done.37
  406.2 4.1 collective-permute-done.38
  413.1 1.3 add_convert_fusion.4
  414.4 1.9 collective-permute-start.40
  417.6 8.3 %collective-permute-done.43 = bf16[4,192,384]{2,1,0:T(8,128)(2,1)S(1)} collective-permute-done((bf16[4,192,384]{2,1,0:T(8,128)(2,1)S(1)}, bf16[4,192,384]{2,1,0:T(8,128)(2,1)S(1)}, u32[]{:S(2)}, u32[]{:S(2)}) %collective-permute-start.43) | collective-permute-done | bytes 589856 | tf_op jit(solution)/shard_map/ppermute | solution.py:752
  427.0 1.4 collective-permute-start.44
  429.5 2.3 collective-permute-start.41
  434.8 2.7 collective-permute-start.45
  437.4 10.1 %collective-permute-done.41 = bf16[1,384,384]{2,1,0:T(8,128)(2,1)S(1)} collective-permute-done((bf16[1,384,384]{2,1,0:T(8,128)(2,1)S(1)}, bf16[1,384,384]{2,1,0:T(8,128)(2,1)S(1)}, u32[]{:S(2)}, u32[]{:S(2)}) %collective-permute-start.41) | collective-permute-done | bytes 294944 | tf_op jit(solution)/shard_map/ppermute | solution.py:752
  (246 shorter events, 46.3 us)
Async XLA Ops:
  0.7 42.3 %collective-permute-start.4 = (bf16[768,3072]{1,0:T(8,128)(2,1)}, bf16[768,3072]{1,0:T(8,128)(2,1)}, u32[]{:S(2)}, u32[]{:S(2)}) collective-permute-start(bf16[768,3072]{1,0:T(8,128)(2,1)} %bitcast.75), channel_id=1, source_target_pairs={{0,16},{16,0},{1,17},{17,1},{2,18},{18,2},{3,19},{19,3},{4,20},{20... | collective-permute-start | bytes 14155784 | tf_op jit(solution)/shard_map/ppermute | solution.py:1004
  1.2 41.8 %collective-permute-start.5 = (bf16[3072,768]{1,0:T(8,128)(2,1)}, bf16[3072,768]{1,0:T(8,128)(2,1)}, u32[]{:S(2)}, u32[]{:S(2)}) collective-permute-start(bf16[3072,768]{1,0:T(8,128)(2,1)} %bitcast.79), channel_id=1, source_target_pairs={{0,16},{16,0},{1,17},{17,1},{2,18},{18,2},{3,19},{19,3},{4,20},{20... | collective-permute-start | bytes 14155784 | tf_op jit(solution)/shard_map/ppermute | solution.py:1004
  1.3 24.1 %collective-permute-start.1 = (bf16[768,2304]{1,0:T(8,128)(2,1)}, bf16[768,2304]{1,0:T(8,128)(2,1)S(1)}, u32[]{:S(2)}, u32[]{:S(2)}) collective-permute-start(bf16[768,2304]{1,0:T(8,128)(2,1)} %bitcast.70), channel_id=1, source_target_pairs={{0,16},{16,0},{1,17},{17,1},{2,18},{18,2},{3,19},{19,3},{4,20},{20... | collective-permute-start | bytes 10616840 | tf_op jit(solution)/shard_map/ppermute | solution.py:1004
  3.1 20.1 %collective-permute-start = (f32[1,6912]{1,0:T(1,128)}, f32[1,6912]{1,0:T(1,128)}, u32[]{:S(2)}, u32[]{:S(2)}) collective-permute-start(f32[1,6912]{1,0:T(1,128)} %pack_vectors.1.own_ref), channel_id=1, source_target_pairs={{0,16},{16,0},{1,17},{17,1},{2,18},{18,2},{3,19},{19,3},{4,20},{20... | collective-permute-start | bytes 82952 | tf_op jit(solution)/shard_map/ppermute | solution.py:1004
  3.2 22.2 %collective-permute-start.2 = (bf16[768,768]{1,0:T(8,128)(2,1)}, bf16[768,768]{1,0:T(8,128)(2,1)}, u32[]{:S(2)}, u32[]{:S(2)}) collective-permute-start(bf16[768,768]{1,0:T(8,128)(2,1)} %bitcast.83), channel_id=1, source_target_pairs={{0,16},{16,0},{1,17},{17,1},{2,18},{18,2},{3,19},{19,3},{4,20},{20... | collective-permute-start | bytes 3538952 | tf_op jit(solution)/shard_map/ppermute | solution.py:1004
  23.2 55.2 %collective-permute-start.8 = (bf16[8,288,768]{2,1,0:T(8,128)(2,1)}, bf16[8,288,768]{2,1,0:T(8,128)(2,1)S(1)}, u32[]{:S(2)}, u32[]{:S(2)}) collective-permute-start(bf16[8,288,768]{2,1,0:T(8,128)(2,1)} %get-tuple-element.159), channel_id=1, source_target_pairs={{0,16},{16,0},{1,17},{17,1},{2,18},{18,2},{3,19},{19,3},{4,20},{20... | collective-permute-start | bytes 10616840 | tf_op jit(solution)/shard_map/ppermute | solution.py:1004
  40.4 2.6 collective-permute-start.3
  60.1 2.5 collective-permute-start.6
  78.1 2.5 collective-permute-start.7
  101.4 2.5 collective-permute-start.9
  128.5 3.7 collective-permute-start.12
  129.0 47.6 %collective-permute-start.16 = (bf16[8,288,768]{2,1,0:T(8,128)(2,1)}, bf16[8,288,768]{2,1,0:T(8,128)(2,1)}, u32[]{:S(2)}, u32[]{:S(2)}) collective-permute-start(bf16[8,288,768]{2,1,0:T(8,128)(2,1)} %get-tuple-element.186.refs_5_), channel_id=1, source_target_pairs={{0,16},{16,0},{1,17},{17,1},{2,18},{18,2},{3,19},{19,3},{4,20},{20... | collective-permute-start | bytes 10616840 | tf_op jit(solution)/shard_map/ppermute | solution.py:1004
  144.5 56.3 %collective-permute-start.14 = (bf16[8,384,384]{2,1,0:T(8,128)(2,1)}, bf16[8,384,384]{2,1,0:T(8,128)(2,1)S(1)}, u32[]{:S(2)}, u32[]{:S(2)}) collective-permute-start(bf16[8,384,384]{2,1,0:T(8,128)(2,1)} %get-tuple-element.175), channel_id=1, source_target_pairs={{0,1},{1,0},{2,3},{3,2},{4,5},{5,4},{6,7},{7,6},{8,9},{9,8},{10,11... | collective-permute-start | bytes 7077896 | tf_op jit(solution)/shard_map/ppermute | solution.py:752
  147.2 2.4 collective-permute-start.11
  147.9 28.8 %collective-permute-start.15 = (bf16[512,384]{1,0:T(8,128)(2,1)S(1)}, bf16[512,384]{1,0:T(8,128)(2,1)S(1)}, u32[]{:S(2)}, u32[]{:S(2)}) collective-permute-start(bf16[512,384]{1,0:T(8,128)(2,1)S(1)} %copy-done.45), channel_id=1, source_target_pairs={{0,16},{16,0},{1,17},{17,1},{2,18},{18,2},{3,19},{19,3},{4,20},{20... | collective-permute-start | bytes 1179656 | tf_op jit(solution)/shard_map/ppermute | solution.py:1004
  177.4 23.3 %copy-start.43 = (bf16[512,768]{1,0:T(8,128)(2,1)S(1)}, bf16[512,768]{1,0:T(8,128)(2,1)}, u32[]{:S(2)}) copy-start(bf16[512,768]{1,0:T(8,128)(2,1)} %get-tuple-element.180) | copy-start | bytes 2359300
  177.4 23.4 %copy-start.4 = (bf16[4,384,384]{2,1,0:T(8,128)(2,1)S(1)}, bf16[4,384,384]{2,1,0:T(8,128)(2,1)}, u32[]{:S(2)}) copy-start(bf16[4,384,384]{2,1,0:T(8,128)(2,1)} %get-tuple-element.181) | copy-start | bytes 3538948
  199.2 27.9 %collective-permute-start.19 = (bf16[8,192,384]{2,1,0:T(8,128)(2,1)}, bf16[8,192,384]{2,1,0:T(8,128)(2,1)}, u32[]{:S(2)}, u32[]{:S(2)}) collective-permute-start(bf16[8,192,384]{2,1,0:T(8,128)(2,1)} %get-tuple-element.191), channel_id=1, source_target_pairs={{0,4},{1,5},{2,6},{3,7},{4,0},{5,1},{6,2},{7,3},{8,12},{9,13},{10,... | collective-permute-start | bytes 3538952 | tf_op jit(solution)/shard_map/ppermute | solution.py:752
  200.8 2.3 collective-permute-start.13
  200.8 80.8 %copy-start.3 = (bf16[8,384,384]{2,1,0:T(8,128)(2,1)}, bf16[8,384,384]{2,1,0:T(8,128)(2,1)S(1)}, u32[]{:S(2)}) copy-start(bf16[8,384,384]{2,1,0:T(8,128)(2,1)S(1)} %collective-permute-done.14) | copy-start | bytes 7077892
  201.1 36.5 %collective-permute-start.18 = (bf16[4,384,384]{2,1,0:T(8,128)(2,1)S(1)}, bf16[4,384,384]{2,1,0:T(8,128)(2,1)}, u32[]{:S(2)}, u32[]{:S(2)}) collective-permute-start(bf16[4,384,384]{2,1,0:T(8,128)(2,1)S(1)} %add_convert_fusion.1), channel_id=1, source_target_pairs={{0,2},{1,3},{2,0},{3,1},{4,6},{5,7},{6,4},{7,5},{8,10},{9,11},{10,... | collective-permute-start | bytes 3538952 | tf_op jit(solution)/shard_map/ppermute | solution.py:752
  202.7 24.4 %collective-permute-start.20 = (bf16[512,384]{1,0:T(8,128)(2,1)}, bf16[512,384]{1,0:T(8,128)(2,1)}, u32[]{:S(2)}, u32[]{:S(2)}) collective-permute-start(bf16[512,384]{1,0:T(8,128)(2,1)} %get-tuple-element.204.refs_2_), channel_id=1, source_target_pairs={{0,16},{16,0},{1,17},{17,1},{2,18},{18,2},{3,19},{19,3},{4,20},{20... | collective-permute-start | bytes 1179656 | tf_op jit(solution)/shard_map/ppermute | solution.py:1004
  223.6 16.2 %collective-permute-start.17 = (bf16[512,768]{1,0:T(8,128)(2,1)}, bf16[512,768]{1,0:T(8,128)(2,1)}, u32[]{:S(2)}, u32[]{:S(2)}) collective-permute-start(bf16[512,768]{1,0:T(8,128)(2,1)} %get-tuple-element.196), channel_id=1, source_target_pairs={{0,16},{16,0},{1,17},{17,1},{2,18},{18,2},{3,19},{19,3},{4,20},{20... | collective-permute-start | bytes 2359304 | tf_op jit(solution)/shard_map/ppermute | solution.py:1004
  233.8 43.6 %collective-permute-start.24 = (bf16[8,192,384]{2,1,0:T(8,128)(2,1)}, bf16[8,192,384]{2,1,0:T(8,128)(2,1)}, u32[]{:S(2)}, u32[]{:S(2)}) collective-permute-start(bf16[8,192,384]{2,1,0:T(8,128)(2,1)} %get-tuple-element.206), channel_id=1, source_target_pairs={{0,2},{1,3},{2,0},{3,1},{4,6},{5,7},{6,4},{7,5},{8,10},{9,11},{10,... | collective-permute-start | bytes 3538952 | tf_op jit(solution)/shard_map/ppermute | solution.py:752
  239.7 37.8 %copy-start.11 = (bf16[4,192,384]{2,1,0:T(8,128)(2,1)S(1)}, bf16[4,192,384]{2,1,0:T(8,128)(2,1)}, u32[]{:S(2)}) copy-start(bf16[4,192,384]{2,1,0:T(8,128)(2,1)} %get-tuple-element.217) | copy-start | bytes 1769476
  261.5 22.0 %collective-permute-start.25 = (bf16[512,1536]{1,0:T(8,128)(2,1)}, bf16[512,1536]{1,0:T(8,128)(2,1)}, u32[]{:S(2)}, u32[]{:S(2)}) collective-permute-start(bf16[512,1536]{1,0:T(8,128)(2,1)} %get-tuple-element.220.refs_2_), channel_id=1, source_target_pairs={{0,16},{16,0},{1,17},{17,1},{2,18},{18,2},{3,19},{19,3},{4,20},{20... | collective-permute-start | bytes 4718600 | tf_op jit(solution)/shard_map/ppermute | solution.py:1004
  261.5 15.9 %collective-permute-start.23 = (bf16[4,192,384]{2,1,0:T(8,128)(2,1)}, bf16[4,192,384]{2,1,0:T(8,128)(2,1)S(1)}, u32[]{:S(2)}, u32[]{:S(2)}) collective-permute-start(bf16[4,192,384]{2,1,0:T(8,128)(2,1)} %add_convert_fusion.6), channel_id=1, source_target_pairs={{0,1},{1,0},{2,3},{3,2},{4,5},{5,4},{6,7},{7,6},{8,9},{9,8},{10,11... | collective-permute-start | bytes 1769480 | tf_op jit(solution)/shard_map/ppermute | solution.py:752
  261.9 19.6 %collective-permute-start.22 = (bf16[2,384,384]{2,1,0:T(8,128)(2,1)}, bf16[2,384,384]{2,1,0:T(8,128)(2,1)}, u32[]{:S(2)}, u32[]{:S(2)}) collective-permute-start(bf16[2,384,384]{2,1,0:T(8,128)(2,1)} %add_convert_fusion.7), channel_id=1, source_target_pairs={{0,4},{1,5},{2,6},{3,7},{4,0},{5,1},{6,2},{7,3},{8,12},{9,13},{10,... | collective-permute-start | bytes 1769480 | tf_op jit(solution)/shard_map/ppermute | solution.py:752
  264.2 31.9 %collective-permute-start.10 = (bf16[512,768]{1,0:T(8,128)(2,1)}, bf16[512,768]{1,0:T(8,128)(2,1)}, u32[]{:S(2)}, u32[]{:S(2)}) collective-permute-start(bf16[512,768]{1,0:T(8,128)(2,1)} %get-tuple-element.169), channel_id=1, source_target_pairs={{0,16},{16,0},{1,17},{17,1},{2,18},{18,2},{3,19},{19,3},{4,20},{20... | collective-permute-start | bytes 2359304 | tf_op jit(solution)/shard_map/ppermute | solution.py:1004
  277.5 80.7 %collective-permute-start.32 = (bf16[8,288,768]{2,1,0:T(8,128)(2,1)}, bf16[8,288,768]{2,1,0:T(8,128)(2,1)}, u32[]{:S(2)}, u32[]{:S(2)}) collective-permute-start(bf16[8,288,768]{2,1,0:T(8,128)(2,1)} %get-tuple-element.188.refs_8_), channel_id=1, source_target_pairs={{0,16},{16,0},{1,17},{17,1},{2,18},{18,2},{3,19},{19,3},{4,20},{20... | collective-permute-start | bytes 10616840 | tf_op jit(solution)/shard_map/ppermute | solution.py:1004
  294.5 45.9 %collective-permute-start.30 = (bf16[8,384,384]{2,1,0:T(8,128)(2,1)}, bf16[8,384,384]{2,1,0:T(8,128)(2,1)S(1)}, u32[]{:S(2)}, u32[]{:S(2)}) collective-permute-start(bf16[8,384,384]{2,1,0:T(8,128)(2,1)} %get-tuple-element.222), channel_id=1, source_target_pairs={{0,1},{1,0},{2,3},{3,2},{4,5},{5,4},{6,7},{7,6},{8,9},{9,8},{10,11... | collective-permute-start | bytes 7077896 | tf_op jit(solution)/shard_map/ppermute | solution.py:752
  296.0 10.5 %collective-permute-start.21 = (bf16[512,768]{1,0:T(8,128)(2,1)}, bf16[512,768]{1,0:T(8,128)(2,1)}, u32[]{:S(2)}, u32[]{:S(2)}) collective-permute-start(bf16[512,768]{1,0:T(8,128)(2,1)} %get-tuple-element.211), channel_id=1, source_target_pairs={{0,16},{16,0},{1,17},{17,1},{2,18},{18,2},{3,19},{19,3},{4,20},{20... | collective-permute-start | bytes 2359304 | tf_op jit(solution)/shard_map/ppermute | solution.py:1004
  299.5 4.2 collective-permute-start.33
  301.6 28.4 %collective-permute-start.29 = (bf16[4,192,384]{2,1,0:T(8,128)(2,1)}, bf16[4,192,384]{2,1,0:T(8,128)(2,1)S(1)}, u32[]{:S(2)}, u32[]{:S(2)}) collective-permute-start(bf16[4,192,384]{2,1,0:T(8,128)(2,1)} %add_convert_fusion.5), channel_id=1, source_target_pairs={{0,4},{1,5},{2,6},{3,7},{4,0},{5,1},{6,2},{7,3},{8,12},{9,13},{10,... | collective-permute-start | bytes 1769480 | tf_op jit(solution)/shard_map/ppermute | solution.py:752
  303.7 22.8 %collective-permute-start.27 = (bf16[1,384,384]{2,1,0:T(8,128)(2,1)}, bf16[1,384,384]{2,1,0:T(8,128)(2,1)S(1)}, u32[]{:S(2)}, u32[]{:S(2)}) collective-permute-start(bf16[1,384,384]{2,1,0:T(8,128)(2,1)} %add_convert_fusion.12), channel_id=1, source_target_pairs={{0,8},{1,9},{2,10},{3,11},{4,12},{5,13},{6,14},{7,15},{8,0},{9,1},... | collective-permute-start | bytes 884744 | tf_op jit(solution)/shard_map/ppermute | solution.py:752
  306.5 36.8 %collective-permute-start.31 = (bf16[512,384]{1,0:T(8,128)(2,1)}, bf16[512,384]{1,0:T(8,128)(2,1)}, u32[]{:S(2)}, u32[]{:S(2)}) collective-permute-start(bf16[512,384]{1,0:T(8,128)(2,1)} %get-tuple-element.239.refs_2_), channel_id=1, source_target_pairs={{0,16},{16,0},{1,17},{17,1},{2,18},{18,2},{3,19},{19,3},{4,20},{20... | collective-permute-start | bytes 1179656 | tf_op jit(solution)/shard_map/ppermute | solution.py:1004
  306.6 19.9 %copy-start.25 = (bf16[2,192,384]{2,1,0:T(8,128)(2,1)S(1)}, bf16[2,192,384]{2,1,0:T(8,128)(2,1)}, u32[]{:S(2)}) copy-start(bf16[2,192,384]{2,1,0:T(8,128)(2,1)} %add_convert_fusion.11) | copy-start | bytes 884740
  306.6 22.0 %copy-start.19 = (bf16[1,384,384]{2,1,0:T(8,128)(2,1)S(1)}, bf16[1,384,384]{2,1,0:T(8,128)(2,1)}, u32[]{:S(2)}) copy-start(bf16[1,384,384]{2,1,0:T(8,128)(2,1)} %get-tuple-element.228) | copy-start | bytes 884740
  326.5 6.8 %collective-permute-start.28 = (bf16[2,192,384]{2,1,0:T(8,128)(2,1)S(1)}, bf16[2,192,384]{2,1,0:T(8,128)(2,1)S(1)}, u32[]{:S(2)}, u32[]{:S(2)}) collective-permute-start(bf16[2,192,384]{2,1,0:T(8,128)(2,1)S(1)} %copy-done.25), channel_id=1, source_target_pairs={{0,2},{1,3},{2,0},{3,1},{4,6},{5,7},{6,4},{7,5},{8,10},{9,11},{10,... | collective-permute-start | bytes 884744 | tf_op jit(solution)/shard_map/ppermute | solution.py:752
  330.0 55.5 %copy-start.15 = (bf16[4,192,384]{2,1,0:T(8,128)(2,1)}, bf16[4,192,384]{2,1,0:T(8,128)(2,1)S(1)}, u32[]{:S(2)}) copy-start(bf16[4,192,384]{2,1,0:T(8,128)(2,1)S(1)} %collective-permute-done.29) | copy-start | bytes 1769476
  330.1 20.6 %collective-permute-start.26 = (bf16[512,768]{1,0:T(8,128)(2,1)}, bf16[512,768]{1,0:T(8,128)(2,1)}, u32[]{:S(2)}, u32[]{:S(2)}) collective-permute-start(bf16[512,768]{1,0:T(8,128)(2,1)} %get-tuple-element.227), channel_id=1, source_target_pairs={{0,16},{16,0},{1,17},{17,1},{2,18},{18,2},{3,19},{19,3},{4,20},{20... | collective-permute-start | bytes 2359304 | tf_op jit(solution)/shard_map/ppermute | solution.py:1004
  333.3 52.2 %collective-permute-start.46 = (bf16[2,192,384]{2,1,0:T(8,128)(2,1)}, bf16[2,192,384]{2,1,0:T(8,128)(2,1)}, u32[]{:S(2)}, u32[]{:S(2)}) collective-permute-start(bf16[2,192,384]{2,1,0:T(8,128)(2,1)} %add_convert_fusion.10), channel_id=1, source_target_pairs={{0,1},{1,0},{2,3},{3,2},{4,5},{5,4},{6,7},{7,6},{8,9},{9,8},{10,11... | collective-permute-start | bytes 884744 | tf_op jit(solution)/shard_map/ppermute | solution.py:752
  340.3 50.5 %collective-permute-start.49 = (bf16[1,192,384]{2,1,0:T(8,128)(2,1)}, bf16[1,192,384]{2,1,0:T(8,128)(2,1)}, u32[]{:S(2)}, u32[]{:S(2)}) collective-permute-start(bf16[1,192,384]{2,1,0:T(8,128)(2,1)} %add_convert_fusion.15), channel_id=1, source_target_pairs={{0,8},{1,9},{2,10},{3,11},{4,12},{5,13},{6,14},{7,15},{8,0},{9,1},... | collective-permute-start | bytes 442376 | tf_op jit(solution)/shard_map/ppermute | solution.py:752
  343.3 69.8 %collective-permute-start.39 = (bf16[4,384,384]{2,1,0:T(8,128)(2,1)}, bf16[4,384,384]{2,1,0:T(8,128)(2,1)}, u32[]{:S(2)}, u32[]{:S(2)}) collective-permute-start(bf16[4,384,384]{2,1,0:T(8,128)(2,1)} %add_convert_fusion), channel_id=1, source_target_pairs={{0,2},{1,3},{2,0},{3,1},{4,6},{5,7},{6,4},{7,5},{8,10},{9,11},{10,... | collective-permute-start | bytes 3538952 | tf_op jit(solution)/shard_map/ppermute | solution.py:752
  350.6 60.4 %collective-permute-start.42 = (bf16[8,192,384]{2,1,0:T(8,128)(2,1)}, bf16[8,192,384]{2,1,0:T(8,128)(2,1)}, u32[]{:S(2)}, u32[]{:S(2)}) collective-permute-start(bf16[8,192,384]{2,1,0:T(8,128)(2,1)} %get-tuple-element.242), channel_id=1, source_target_pairs={{0,4},{1,5},{2,6},{3,7},{4,0},{5,1},{6,2},{7,3},{8,12},{9,13},{10,... | collective-permute-start | bytes 3538952 | tf_op jit(solution)/shard_map/ppermute | solution.py:752
  358.2 27.4 %copy-start.28 = (bf16[1,192,384]{2,1,0:T(8,128)(2,1)S(1)}, bf16[1,192,384]{2,1,0:T(8,128)(2,1)}, u32[]{:S(2)}) copy-start(bf16[1,192,384]{2,1,0:T(8,128)(2,1)} %get-tuple-element.264) | copy-start | bytes 442372
  358.2 29.1 %copy-start.32 = (f32[3,8,768]{2,1,0:T(8,128)S(1)}, f32[3,8,768]{2,1,0:T(8,128)}, u32[]{:S(2)}) copy-start(f32[3,8,768]{2,1,0:T(8,128)} %get-tuple-element.213) | copy-start | bytes 221188
  358.2 29.1 %copy-start.38 = (f32[2,8,768]{2,1,0:T(8,128)S(1)}, f32[2,8,768]{2,1,0:T(8,128)}, u32[]{:S(2)}) copy-start(f32[2,8,768]{2,1,0:T(8,128)} %get-tuple-element.245) | copy-start | bytes 147460
  385.5 5.4 %collective-permute-start.34 = (f32[2,8,768]{2,1,0:T(8,128)}, f32[2,8,768]{2,1,0:T(8,128)}, u32[]{:S(2)}, u32[]{:S(2)}) collective-permute-start(f32[2,8,768]{2,1,0:T(8,128)} %get-tuple-element.252), channel_id=1, source_target_pairs={{0,16},{16,0},{1,17},{17,1},{2,18},{18,2},{3,19},{19,3},{4,20},{20... | collective-permute-start | bytes 147464 | tf_op jit(solution)/shard_map/ppermute | solution.py:1004
  388.3 43.6 %collective-permute-start.47 = (bf16[1,192,384]{2,1,0:T(8,128)(2,1)}, bf16[1,192,384]{2,1,0:T(8,128)(2,1)S(1)}, u32[]{:S(2)}, u32[]{:S(2)}) collective-permute-start(bf16[1,192,384]{2,1,0:T(8,128)(2,1)} %add_convert_fusion.13), channel_id=1, source_target_pairs={{0,8},{1,9},{2,10},{3,11},{4,12},{5,13},{6,14},{7,15},{8,0},{9,1},... | collective-permute-start | bytes 442376 | tf_op jit(solution)/shard_map/ppermute | solution.py:752
  393.6 17.4 %copy-start.10 = (bf16[4,192,384]{2,1,0:T(8,128)(2,1)S(1)}, bf16[4,192,384]{2,1,0:T(8,128)(2,1)}, u32[]{:S(2)}) copy-start(bf16[4,192,384]{2,1,0:T(8,128)(2,1)} %get-tuple-element.259) | copy-start | bytes 1769476
  394.5 3.8 collective-permute-start.35
  398.3 3.7 collective-permute-start.36
  402.0 3.7 collective-permute-start.37
  405.7 4.6 %collective-permute-start.38 = (f32[1,1,624]{2,0,1:T(1,128)S(1)}, f32[1,1,624]{2,0,1:T(1,128)S(1)}, u32[]{:S(2)}, u32[]{:S(2)}) collective-permute-start(f32[1,1,624]{2,0,1:T(1,128)S(1)} %slice_add_fusion.3), channel_id=1, source_target_pairs={{0,8},{1,9},{2,10},{3,11},{4,12},{5,13},{6,14},{7,15},{8,0},{9,1},... | collective-permute-start | bytes 7496 | tf_op jit(solution)/shard_map/ppermute | solution.py:752
  406.2 45.0 %collective-permute-start.50 = (f32[4,24,384]{2,1,0:T(8,128)S(1)}, f32[4,24,384]{2,1,0:T(8,128)S(1)}, u32[]{:S(2)}, u32[]{:S(2)}) collective-permute-start(f32[4,24,384]{2,1,0:T(8,128)S(1)} %dynamic-slice_bitcast_fusion), channel_id=1, source_target_pairs={{0,16},{16,0},{1,17},{17,1},{2,18},{18,2},{3,19},{19,3},{4,20},{20... | collective-permute-start | bytes 442376 | tf_op jit(solution)/shard_map/ppermute | solution.py:1004
  412.3 13.6 %collective-permute-start.43 = (bf16[4,192,384]{2,1,0:T(8,128)(2,1)S(1)}, bf16[4,192,384]{2,1,0:T(8,128)(2,1)S(1)}, u32[]{:S(2)}, u32[]{:S(2)}) collective-permute-start(bf16[4,192,384]{2,1,0:T(8,128)(2,1)S(1)} %add_convert_fusion.3), channel_id=1, source_target_pairs={{0,1},{1,0},{2,3},{3,2},{4,5},{5,4},{6,7},{7,6},{8,9},{9,8},{10,11... | collective-permute-start | bytes 1769480 | tf_op jit(solution)/shard_map/ppermute | solution.py:752
  414.4 17.4 %copy-start.27 = (bf16[1,192,384]{2,1,0:T(8,128)(2,1)S(1)}, bf16[1,192,384]{2,1,0:T(8,128)(2,1)}, u32[]{:S(2)}) copy-start(bf16[1,192,384]{2,1,0:T(8,128)(2,1)} %get-tuple-element.262) | copy-start | bytes 442372
  414.4 14.0 %collective-permute-start.40 = (bf16[2,384,384]{2,1,0:T(8,128)(2,1)S(1)}, bf16[2,384,384]{2,1,0:T(8,128)(2,1)S(1)}, u32[]{:S(2)}, u32[]{:S(2)}) collective-permute-start(bf16[2,384,384]{2,1,0:T(8,128)(2,1)S(1)} %add_convert_fusion.4), channel_id=1, source_target_pairs={{0,4},{1,5},{2,6},{3,7},{4,0},{5,1},{6,2},{7,3},{8,12},{9,13},{10,... | collective-permute-start | bytes 1769480 | tf_op jit(solution)/shard_map/ppermute | solution.py:752
  427.0 6.8 %collective-permute-start.44 = (bf16[2,192,384]{2,1,0:T(8,128)(2,1)S(1)}, bf16[2,192,384]{2,1,0:T(8,128)(2,1)S(1)}, u32[]{:S(2)}, u32[]{:S(2)}) collective-permute-start(bf16[2,192,384]{2,1,0:T(8,128)(2,1)S(1)} %add_convert_fusion.8), channel_id=1, source_target_pairs={{0,2},{1,3},{2,0},{3,1},{4,6},{5,7},{6,4},{7,5},{8,10},{9,11},{10,... | collective-permute-start | bytes 884744 | tf_op jit(solution)/shard_map/ppermute | solution.py:752
  428.4 19.1 %copy-start.17 = (bf16[1,384,384]{2,1,0:T(8,128)(2,1)S(1)}, bf16[1,384,384]{2,1,0:T(8,128)(2,1)}, u32[]{:S(2)}) copy-start(bf16[1,384,384]{2,1,0:T(8,128)(2,1)} %get-tuple-element.253) | copy-start | bytes 884740
  429.5 18.0 %collective-permute-start.41 = (bf16[1,384,384]{2,1,0:T(8,128)(2,1)S(1)}, bf16[1,384,384]{2,1,0:T(8,128)(2,1)S(1)}, u32[]{:S(2)}, u32[]{:S(2)}) collective-permute-start(bf16[1,384,384]{2,1,0:T(8,128)(2,1)S(1)} %add_convert_fusion.9), channel_id=1, source_target_pairs={{0,8},{1,9},{2,10},{3,11},{4,12},{5,13},{6,14},{7,15},{8,0},{9,1},... | collective-permute-start | bytes 884744 | tf_op jit(solution)/shard_map/ppermute | solution.py:752
  434.8 14.4 %collective-permute-start.45 = (bf16[1,192,384]{2,1,0:T(8,128)(2,1)S(1)}, bf16[1,192,384]{2,1,0:T(8,128)(2,1)S(1)}, u32[]{:S(2)}, u32[]{:S(2)}) collective-permute-start(bf16[1,192,384]{2,1,0:T(8,128)(2,1)S(1)} %add_convert_fusion.14), channel_id=1, source_target_pairs={{0,8},{1,9},{2,10},{3,11},{4,12},{5,13},{6,14},{7,15},{8,0},{9,1},... | collective-permute-start | bytes 442376 | tf_op jit(solution)/shard_map/ppermute | solution.py:752
  450.3 2.5 collective-permute-start.48
  (34 other events, 235.9 us)
